TPU v7x, 32 devices: a whole 2x2x4 slice. The times are simulated.
32 devices in a mesh: dp: 4 (over y, x), ctx: 2 (over core), tensor: 4 (over z).
Axes of the slice: x: 2, y: 2, z: 4, core: 2. Of those that a mesh axis runs over, the one named last changes fastest.
Arguments:
- hidden_in: float32 [8, 1024, 768], P('dp', ('ctx', 'tensor')), may hold values from -6 to 6
- cotangent: float32 [8, 1024, 768], P('dp', ('ctx', 'tensor')), may hold values from -6 to 6
- segment_ids: int32 [8, 1024], P('dp'), may hold values from -1 to 17, as said below
- attn_gain: float32 [768], replicated, may hold values from 0.5 to 1.5
- attn_shift: float32 [768], replicated, may hold values from -1.75 to 1.75
- query_weight: float32 [768, 768], P('dp', 'tensor'), may hold values from -0.21875 to 0.21875
- key_weight: float32 [768, 768], P('dp', 'tensor'), may hold values from -0.21875 to 0.21875
- value_weight: float32 [768, 768], P('dp', 'tensor'), may hold values from -0.21875 to 0.21875
- query_bias: float32 [768], replicated, may hold values from -1.75 to 1.75
- value_bias: float32 [768], replicated, may hold values from -1.75 to 1.75
- output_weight: float32 [768, 768], P('tensor', 'dp'), may hold values from -3.5 to 3.5
- output_bias: float32 [768], replicated, may hold values from -1.75 to 1.75
- ffn_gain: float32 [768], replicated, may hold values from 0.5 to 1.5
- ffn_shift: float32 [768], replicated, may hold values from -1.75 to 1.75
- inner_weight: float32 [768, 3072], P('dp', 'tensor'), may hold values from -0.21875 to 0.21875
- inner_bias: float32 [3072], replicated, may hold values from -1.75 to 1.75
- outer_weight: float32 [3072, 768], P('tensor', 'dp'), may hold values from -0.15625 to 0.15625
- outer_bias: float32 [768], replicated, may hold values from -1.75 to 1.75
Outputs:
- block_out: float32 [8, 1024, 768], P('dp', ('ctx', 'tensor'))
- grad_input: float32 [8, 1024, 768], P('dp', ('ctx', 'tensor'))
- grad_attn_gain: float32 [768], replicated
- grad_attn_shift: float32 [768], replicated
- grad_query_weight: float32 [768, 768], P('dp', 'tensor')
- grad_key_weight: float32 [768, 768], P('dp', 'tensor')
- grad_value_weight: float32 [768, 768], P('dp', 'tensor')
- grad_query_bias: float32 [768], replicated
- grad_value_bias: float32 [768], replicated
- grad_output_weight: float32 [768, 768], P('tensor', 'dp')
- grad_output_bias: float32 [768], replicated
- grad_ffn_gain: float32 [768], replicated
- grad_ffn_shift: float32 [768], replicated
- grad_inner_weight: float32 [768, 3072], P('dp', 'tensor')
- grad_inner_bias: float32 [3072], replicated
- grad_outer_weight: float32 [3072, 768], P('tensor', 'dp')
- grad_outer_bias: float32 [768], replicated
Inputs may be any that keep to these rules, and one draw needn't show every extreme that they name: `segment_ids`: in each sequence the document numbers are 0, 1, 2, ... in order of position, each document at most 800 tokens and all but the last one cut at least 60; a tail of 1 to 128 tokens at each sequence's end is padding and carries -1.
All inputs are finite; a program needn't handle non-finite values.
Results may differ from a plain program's by a relative error of at most 0.015.
Values may be sent and summed in bfloat16 or wider, within the bound.
A program may use at most 128 MiB of HBM per device.

v0:
```python
import jax
import jax.numpy as jnp
from jax import lax
from jax.sharding import PartitionSpec as P

HDIM = 64


root_half = 0.7071067811865476
inv_root_two_pi = 0.3989422804014327


def smooth_gate(values):
    return values * (0.5 * (1.0 + lax.erf(values * root_half)))


def smooth_slope(values):
    normal_cdf = 0.5 * (1.0 + lax.erf(values * root_half))
    normal_pdf = jnp.exp(-0.5 * values * values) * inv_root_two_pi
    return normal_cdf + values * normal_pdf


def norm_forward(rows, gain, shift):
    centred = rows - jnp.mean(rows, axis=-1, keepdims=True)
    inverse = lax.rsqrt(jnp.mean(centred * centred, axis=-1, keepdims=True) + 1e-05)
    scaled = centred * inverse
    return (scaled * gain + shift, scaled, inverse)


def norm_backward(grad_out, scaled, inverse, gain):
    grad_scaled = grad_out * gain
    plain_mean = jnp.mean(grad_scaled, axis=-1, keepdims=True)
    cross_mean = jnp.mean(grad_scaled * scaled, axis=-1, keepdims=True)
    grad_rows = inverse * (grad_scaled - plain_mean - scaled * cross_mean)
    return (grad_rows, jnp.sum(grad_out * scaled, axis=0), jnp.sum(grad_out, axis=0))


def tensor_rows(block):
    return lax.all_gather(block, "tensor", axis=0, tiled=True)


def tensor_sums(block):
    return lax.psum_scatter(block, "tensor", scatter_dimension=0, tiled=True)


def fetch_weights(shards):
    return (
        lax.all_gather(shards[0], "dp", axis=0, tiled=True),
        lax.all_gather(shards[1], "dp", axis=0, tiled=True),
        lax.all_gather(shards[2], "dp", axis=0, tiled=True),
        lax.all_gather(shards[3], "dp", axis=0, tiled=True),
        lax.all_gather(shards[4], "dp", axis=1, tiled=True),
        lax.all_gather(shards[5], "dp", axis=1, tiled=True),
    )


def place_piece(piece, total, start):
    return lax.dynamic_update_slice(jnp.zeros((total,), jnp.float32), piece, (start,))


def body(
    hidden_in,
    cotangent,
    segment_ids,
    attn_gain,
    attn_shift,
    query_weight,
    key_weight,
    value_weight,
    query_bias,
    value_bias,
    output_weight,
    output_bias,
    ffn_gain,
    ffn_shift,
    inner_weight,
    inner_bias,
    outer_weight,
    outer_bias,
):
    width = hidden_in.shape[2]
    part_width = query_weight.shape[1]
    unit_width = inner_weight.shape[1]
    unit_total = inner_bias.shape[0]
    heads_here = part_width // HDIM
    tensor_at = lax.axis_index("tensor")
    ctx_at = lax.axis_index("ctx")
    half_rows = hidden_in.shape[1] * lax.axis_size("tensor")
    seq_rows = segment_ids.shape[1]
    factor = HDIM ** (-0.5)
    query_piece = lax.dynamic_slice_in_dim(query_bias, tensor_at * part_width, part_width)
    value_piece = lax.dynamic_slice_in_dim(value_bias, tensor_at * part_width, part_width)
    inner_piece = lax.dynamic_slice_in_dim(inner_bias, tensor_at * unit_width, unit_width)
    shards = (
        query_weight.astype(jnp.bfloat16),
        key_weight.astype(jnp.bfloat16),
        value_weight.astype(jnp.bfloat16),
        inner_weight.astype(jnp.bfloat16),
        output_weight.astype(jnp.bfloat16),
        outer_weight.astype(jnp.bfloat16),
    )
    key_index = jnp.arange(seq_rows)
    query_index = ctx_at * half_rows + jnp.arange(half_rows)

    def masked_scores(queries, key_all, allowed):
        scores = (
            jnp.einsum("qhd,khd->hqk", queries, key_all, preferred_element_type=jnp.float32)
            * factor
        )
        return jnp.where(allowed[None, :, :], scores, -1e30)

    def micro(weights_bf, carry, item):
        w_query, w_key, w_value, w_inner, w_output, w_outer = weights_bf
        rows, cot_rows, segment_row = item
        query_seg = lax.dynamic_slice_in_dim(segment_row, ctx_at * half_rows, half_rows)
        allowed = (query_seg[:, None] == segment_row[None, :]) & (
            (segment_row[None, :] >= 0) | (query_index[:, None] == key_index[None, :])
        )
        normed, scaled_a, inverse_a = norm_forward(rows, attn_gain, attn_shift)
        normed_all = tensor_rows(normed.astype(jnp.bfloat16))
        queries = (
            jnp.dot(normed_all, w_query, preferred_element_type=jnp.float32) + query_piece
        ).astype(jnp.bfloat16)
        key_half = jnp.dot(normed_all, w_key, preferred_element_type=jnp.float32).astype(
            jnp.bfloat16
        )
        value_half = (
            jnp.dot(normed_all, w_value, preferred_element_type=jnp.float32) + value_piece
        ).astype(jnp.bfloat16)
        key_all, value_all = (
            lax.all_gather(key_half, "ctx", axis=0, tiled=True),
            lax.all_gather(value_half, "ctx", axis=0, tiled=True),
        )
        queries = queries.reshape(half_rows, heads_here, HDIM)
        key_all = key_all.reshape(seq_rows, heads_here, HDIM)
        value_all = value_all.reshape(seq_rows, heads_here, HDIM)
        masked = masked_scores(queries, key_all, allowed)
        peak = jnp.max(masked, axis=-1, keepdims=True)
        expo = jnp.exp(masked - peak)
        total = jnp.sum(expo, axis=-1, keepdims=True)
        log_total = peak + jnp.log(total)
        probs = (expo / total).astype(jnp.bfloat16)
        mixed = jnp.einsum("hqk,khd->qhd", probs, value_all, preferred_element_type=jnp.float32)
        mixed = mixed.reshape(half_rows, part_width).astype(jnp.bfloat16)
        branch_a = tensor_sums(jnp.dot(mixed, w_output, preferred_element_type=jnp.float32))
        middle = rows + branch_a + output_bias
        normed_f, scaled_f, inverse_f = norm_forward(middle, ffn_gain, ffn_shift)
        normed_f_all = tensor_rows(normed_f.astype(jnp.bfloat16))
        inner = jnp.dot(normed_f_all, w_inner, preferred_element_type=jnp.float32) + inner_piece
        active = smooth_gate(inner).astype(jnp.bfloat16)
        branch_f = tensor_sums(jnp.dot(active, w_outer, preferred_element_type=jnp.float32))
        result_rows = middle + branch_f + outer_bias
        grad_up = tensor_rows(cot_rows.astype(jnp.bfloat16))
        grad_outer_w = jnp.einsum("tf,td->fd", active, grad_up, preferred_element_type=jnp.float32)
        grad_active = jnp.einsum("td,fd->tf", grad_up, w_outer, preferred_element_type=jnp.float32)
        grad_inner = (grad_active * smooth_slope(inner)).astype(jnp.bfloat16)
        grad_inner_w = jnp.einsum(
            "td,tf->df", normed_f_all, grad_inner, preferred_element_type=jnp.float32
        )
        grad_inner_b = jnp.sum(grad_inner.astype(jnp.float32), axis=0)
        grad_normed_f = tensor_sums(
            jnp.einsum("tf,df->td", grad_inner, w_inner, preferred_element_type=jnp.float32)
        )
        grad_rows_f, grad_ffn_g, grad_ffn_s = norm_backward(
            grad_normed_f, scaled_f, inverse_f, ffn_gain
        )
        grad_middle = cot_rows + grad_rows_f
        grad_branch = tensor_rows(grad_middle.astype(jnp.bfloat16))
        grad_output_w = jnp.einsum(
            "tc,td->cd", mixed, grad_branch, preferred_element_type=jnp.float32
        )
        grad_mixed = jnp.einsum(
            "td,cd->tc", grad_branch, w_output, preferred_element_type=jnp.float32
        )
        grad_mixed = grad_mixed.astype(jnp.bfloat16).reshape(half_rows, heads_here, HDIM)
        grad_probs = jnp.einsum(
            "qhd,khd->hqk", grad_mixed, value_all, preferred_element_type=jnp.float32
        )
        grad_value_part = jnp.einsum(
            "hqk,qhd->khd", probs, grad_mixed, preferred_element_type=jnp.float32
        )
        again = jnp.exp(masked_scores(queries, key_all, allowed) - log_total)
        centre = jnp.sum(again * grad_probs, axis=-1, keepdims=True)
        grad_scores = (again * (grad_probs - centre)).astype(jnp.bfloat16)
        grad_queries = (
            jnp.einsum("hqk,khd->qhd", grad_scores, key_all, preferred_element_type=jnp.float32)
            * factor
        )
        grad_queries = grad_queries.reshape(half_rows, part_width).astype(jnp.bfloat16)
        grad_key_part = (
            jnp.einsum("hqk,qhd->khd", grad_scores, queries, preferred_element_type=jnp.float32)
            * factor
        )
        grad_key_sum, grad_value_sum = (
            lax.psum_scatter(
                grad_key_part.reshape(seq_rows, part_width).astype(jnp.bfloat16),
                "ctx",
                scatter_dimension=0,
                tiled=True,
            ).astype(jnp.float32),
            lax.psum_scatter(
                grad_value_part.reshape(seq_rows, part_width).astype(jnp.bfloat16),
                "ctx",
                scatter_dimension=0,
                tiled=True,
            ).astype(jnp.float32),
        )
        grad_keys = grad_key_sum.astype(jnp.bfloat16)
        grad_values = grad_value_sum.astype(jnp.bfloat16)
        grad_query_w = jnp.einsum(
            "td,tc->dc", normed_all, grad_queries, preferred_element_type=jnp.float32
        )
        grad_key_w = jnp.einsum(
            "td,tc->dc", normed_all, grad_keys, preferred_element_type=jnp.float32
        )
        grad_value_w = jnp.einsum(
            "td,tc->dc", normed_all, grad_values, preferred_element_type=jnp.float32
        )
        grad_query_b = jnp.sum(grad_queries.astype(jnp.float32), axis=0)
        grad_value_b = jnp.sum(grad_values.astype(jnp.float32), axis=0)
        grad_normed_part = jnp.einsum(
            "tc,dc->td", grad_queries, w_query, preferred_element_type=jnp.float32
        )
        grad_normed_part = grad_normed_part + jnp.einsum(
            "tc,dc->td", grad_keys, w_key, preferred_element_type=jnp.float32
        )
        grad_normed_part = grad_normed_part + jnp.einsum(
            "tc,dc->td", grad_values, w_value, preferred_element_type=jnp.float32
        )
        grad_normed = tensor_sums(grad_normed_part)
        grad_rows_a, grad_attn_g, grad_attn_s = norm_backward(
            grad_normed, scaled_a, inverse_a, attn_gain
        )
        grad_rows = grad_middle + grad_rows_a
        big_sums, small_sums = carry
        big_sums = (
            big_sums[0] + grad_query_w,
            big_sums[1] + grad_key_w,
            big_sums[2] + grad_value_w,
            big_sums[3] + grad_inner_w,
            big_sums[4] + grad_output_w,
            big_sums[5] + grad_outer_w,
        )
        small_terms = (
            grad_attn_g,
            grad_attn_s,
            place_piece(grad_query_b, width, tensor_at * part_width),
            place_piece(grad_value_b, width, tensor_at * part_width),
            jnp.sum(grad_middle, axis=0),
            grad_ffn_g,
            grad_ffn_s,
            place_piece(grad_inner_b, unit_total, tensor_at * unit_width),
            jnp.sum(cot_rows, axis=0),
        )
        small_sums = tuple((old + new for old, new in zip(small_sums, small_terms)))
        return ((big_sums, small_sums), (result_rows, grad_rows))

    big_init = (
        jnp.zeros((width, part_width), jnp.float32),
        jnp.zeros((width, part_width), jnp.float32),
        jnp.zeros((width, part_width), jnp.float32),
        jnp.zeros((width, unit_width), jnp.float32),
        jnp.zeros((part_width, width), jnp.float32),
        jnp.zeros((unit_width, width), jnp.float32),
    )
    small_init = tuple((jnp.zeros((width,), jnp.float32) for index_small in range(7))) + (
        jnp.zeros((unit_total,), jnp.float32),
        jnp.zeros((width,), jnp.float32),
    )
    small_init = (
        small_init[0],
        small_init[1],
        small_init[2],
        small_init[3],
        small_init[4],
        small_init[5],
        small_init[6],
        small_init[7],
        small_init[8],
    )
    gathered = fetch_weights(shards)

    def scan_step(carry, item):
        return micro(gathered, carry, item)

    (big_sums, small_sums), (block_out, grad_input) = lax.scan(
        scan_step, (big_init, small_init), (hidden_in, cotangent, segment_ids)
    )
    paired = (
        lax.psum(big_sums[0].astype(jnp.bfloat16), "ctx").astype(jnp.float32),
        lax.psum(big_sums[1].astype(jnp.bfloat16), "ctx").astype(jnp.float32),
        lax.psum(big_sums[2].astype(jnp.bfloat16), "ctx").astype(jnp.float32),
        lax.psum(big_sums[3].astype(jnp.bfloat16), "ctx").astype(jnp.float32),
        lax.psum(big_sums[4].astype(jnp.bfloat16), "ctx").astype(jnp.float32),
        lax.psum(big_sums[5].astype(jnp.bfloat16), "ctx").astype(jnp.float32),
    )
    owned = (
        lax.psum_scatter(
            paired[0].astype(jnp.bfloat16), "dp", scatter_dimension=0, tiled=True
        ).astype(jnp.float32),
        lax.psum_scatter(
            paired[1].astype(jnp.bfloat16), "dp", scatter_dimension=0, tiled=True
        ).astype(jnp.float32),
        lax.psum_scatter(
            paired[2].astype(jnp.bfloat16), "dp", scatter_dimension=0, tiled=True
        ).astype(jnp.float32),
        lax.psum_scatter(
            paired[3].astype(jnp.bfloat16), "dp", scatter_dimension=0, tiled=True
        ).astype(jnp.float32),
        lax.psum_scatter(
            paired[4].astype(jnp.bfloat16), "dp", scatter_dimension=1, tiled=True
        ).astype(jnp.float32),
        lax.psum_scatter(
            paired[5].astype(jnp.bfloat16), "dp", scatter_dimension=1, tiled=True
        ).astype(jnp.float32),
    )
    small = lax.psum(
        (
            small_sums[0],
            small_sums[1],
            small_sums[2],
            small_sums[3],
            small_sums[4],
            small_sums[5],
            small_sums[6],
            small_sums[7],
            small_sums[8],
        ),
        ("dp", "ctx", "tensor"),
    )
    return (
        block_out,
        grad_input,
        small[0],
        small[1],
        owned[0],
        owned[1],
        owned[2],
        small[2],
        small[3],
        owned[4],
        small[4],
        small[5],
        small[6],
        owned[3],
        small[7],
        owned[5],
        small[8],
    )


def solution(mesh):
    return jax.shard_map(
        body,
        mesh=mesh,
        in_specs=(
            P("dp", ("ctx", "tensor"), None),
            P("dp", ("ctx", "tensor"), None),
            P("dp", None),
            P(),
            P(),
            P("dp", "tensor"),
            P("dp", "tensor"),
            P("dp", "tensor"),
            P(),
            P(),
            P("tensor", "dp"),
            P(),
            P(),
            P(),
            P("dp", "tensor"),
            P(),
            P("tensor", "dp"),
            P(),
        ),
        out_specs=(
            P("dp", ("ctx", "tensor"), None),
            P("dp", ("ctx", "tensor"), None),
            P(),
            P(),
            P("dp", "tensor"),
            P("dp", "tensor"),
            P("dp", "tensor"),
            P(),
            P(),
            P("tensor", "dp"),
            P(),
            P(),
            P(),
            P("dp", "tensor"),
            P(),
            P("tensor", "dp"),
            P(),
        ),
        check_vma=False,
    )
```

profile of v0, /device:TPU:0, one launch (start us, length us, event | category | flops | bytes accessed | tf_op | source)
XLA Modules:
  0.0 861.7 jit_solution(12696547817139797604)
XLA Ops:
  76.5 555.2 %while.46 = (s32[]{:T(128)}, f32[768,192]{0,1:T(8,128)}, f32[768,192]{0,1:T(8,128)}, f32[768,192]{0,1:T(8,128)}, f32[768,768]{1,0:T(8,128)}, /*index=5*/f32[192,...) while((s32[]{:T(128)}, f32[768,192]{0,1:T(8,128)}, ...), condition=%wide.region_27.28_spmd.clone, body=%wide.region_0.27_spmd.clone.sunk | while | flops 6701124608 | bytes 297685760 | solution.py:286
  78.5 19.6 %all_gather.78 = bf16[512,768]{1,0:T(8,128)(2,1)S(1)} all-gather(bf16[128,768]{1,0:T(8,128)(2,1)S(1)} %add_convert_fusion.4), channel_id=1, replica_groups=mesh['dp'=4,'ctx'=2,'tensor'=4] {'tensor'}, dimensions={0}, use_global_device_ids=true | all-gather | bytes 983040 | tf_op jit(solution)/shard_map/while/body/eval_jaxpr/all_gather | solution.py:39
  118.8 28.5 %all_gather.82 = bf16[512,768]{1,0:T(8,128)(2,1)S(1)} all-gather(bf16[128,768]{1,0:T(8,128)(2,1)S(1)} %bitcast_convert_fusion.2), channel_id=1, replica_groups=mesh['dp'=4,'ctx'=2,'tensor'=4] {'tensor'}, dimensions={0}, use_global_device_ids=true | all-gather | bytes 983040 | tf_op jit(solution)/shard_map/while/body/eval_jaxpr/all_gather | solution.py:39
  147.3 14.8 %reduce-scatter.33.cloned.1.call-done = f32[128,768]{1,0:T(8,128)} async-done(((f32[512,768]{1,0:T(8,128)}), f32[128,768]{1,0:T(8,128)}) %reduce-scatter.33.cloned.1.call-update) | async-done | bytes 393232 | tf_op jit(solution)/shard_map/while/body/eval_jaxpr/reduce_scatter | solution.py:43
  164.4 18.9 %all_gather.81 = bf16[512,768]{1,0:T(8,128)(2,1)S(1)} all-gather(bf16[128,768]{1,0:T(8,128)(2,1)S(1)} %add_convert_fusion.5), channel_id=1, replica_groups=mesh['dp'=4,'ctx'=2,'tensor'=4] {'tensor'}, dimensions={0}, use_global_device_ids=true | all-gather | bytes 983040 | tf_op jit(solution)/shard_map/while/body/eval_jaxpr/all_gather | solution.py:39
  190.0 33.9 %reduce-scatter.35.cloned.1.call-done = f32[128,768]{1,0:T(8,128)} async-done(((f32[512,768]{1,0:T(8,128)}), f32[128,768]{1,0:T(8,128)}) %reduce-scatter.35.cloned.1.call-update) | async-done | bytes 393232 | tf_op jit(solution)/shard_map/while/body/eval_jaxpr/reduce_scatter | solution.py:43
  227.9 18.2 %all_gather.83 = bf16[512,768]{1,0:T(8,128)(2,1)S(1)} all-gather(bf16[128,768]{1,0:T(8,128)(2,1)S(1)} %convert_element_type.329), channel_id=1, replica_groups=mesh['dp'=4,'ctx'=2,'tensor'=4] {'tensor'}, dimensions={0}, use_global_device_ids=true | all-gather | bytes 983040 | tf_op jit(solution)/shard_map/while/body/eval_jaxpr/all_gather | solution.py:39
  288.3 26.1 %reduce-scatter.43.cloned.1.call-done = f32[128,768]{1,0:T(8,128)} async-done(((f32[512,768]{1,0:T(8,128)}), f32[128,768]{1,0:T(8,128)}) %reduce-scatter.43.cloned.1.call-update) | async-done | bytes 393232 | tf_op jit(solution)/shard_map/while/body/eval_jaxpr/reduce_scatter | solution.py:43
  321.2 29.9 %reduce-scatter.41.cloned.1.call-done = f32[128,768]{1,0:T(8,128)} async-done(((f32[512,768]{1,0:T(8,128)}), f32[128,768]{1,0:T(8,128)}) %reduce-scatter.41.cloned.1.call-update) | async-done | bytes 393232 | tf_op jit(solution)/shard_map/while/body/eval_jaxpr/reduce_scatter | solution.py:43
  356.3 18.2 %all_gather.78 = bf16[512,768]{1,0:T(8,128)(2,1)S(1)} all-gather(bf16[128,768]{1,0:T(8,128)(2,1)S(1)} %add_convert_fusion.4), channel_id=1, replica_groups=mesh['dp'=4,'ctx'=2,'tensor'=4] {'tensor'}, dimensions={0}, use_global_device_ids=true | all-gather | bytes 983040 | tf_op jit(solution)/shard_map/while/body/eval_jaxpr/all_gather | solution.py:39
  395.3 27.4 %all_gather.82 = bf16[512,768]{1,0:T(8,128)(2,1)S(1)} all-gather(bf16[128,768]{1,0:T(8,128)(2,1)S(1)} %bitcast_convert_fusion.2), channel_id=1, replica_groups=mesh['dp'=4,'ctx'=2,'tensor'=4] {'tensor'}, dimensions={0}, use_global_device_ids=true | all-gather | bytes 983040 | tf_op jit(solution)/shard_map/while/body/eval_jaxpr/all_gather | solution.py:39
  422.6 15.9 %reduce-scatter.33.cloned.1.call-done = f32[128,768]{1,0:T(8,128)} async-done(((f32[512,768]{1,0:T(8,128)}), f32[128,768]{1,0:T(8,128)}) %reduce-scatter.33.cloned.1.call-update) | async-done | bytes 393232 | tf_op jit(solution)/shard_map/while/body/eval_jaxpr/reduce_scatter | solution.py:43
  440.9 18.9 %all_gather.81 = bf16[512,768]{1,0:T(8,128)(2,1)S(1)} all-gather(bf16[128,768]{1,0:T(8,128)(2,1)S(1)} %add_convert_fusion.5), channel_id=1, replica_groups=mesh['dp'=4,'ctx'=2,'tensor'=4] {'tensor'}, dimensions={0}, use_global_device_ids=true | all-gather | bytes 983040 | tf_op jit(solution)/shard_map/while/body/eval_jaxpr/all_gather | solution.py:39
  466.5 34.7 %reduce-scatter.35.cloned.1.call-done = f32[128,768]{1,0:T(8,128)} async-done(((f32[512,768]{1,0:T(8,128)}), f32[128,768]{1,0:T(8,128)}) %reduce-scatter.35.cloned.1.call-update) | async-done | bytes 393232 | tf_op jit(solution)/shard_map/while/body/eval_jaxpr/reduce_scatter | solution.py:43
  505.2 18.2 %all_gather.83 = bf16[512,768]{1,0:T(8,128)(2,1)S(1)} all-gather(bf16[128,768]{1,0:T(8,128)(2,1)S(1)} %convert_element_type.329), channel_id=1, replica_groups=mesh['dp'=4,'ctx'=2,'tensor'=4] {'tensor'}, dimensions={0}, use_global_device_ids=true | all-gather | bytes 983040 | tf_op jit(solution)/shard_map/while/body/eval_jaxpr/all_gather | solution.py:39
  568.7 22.9 %reduce-scatter.43.cloned.1.call-done = f32[128,768]{1,0:T(8,128)} async-done(((f32[512,768]{1,0:T(8,128)}), f32[128,768]{1,0:T(8,128)}) %reduce-scatter.43.cloned.1.call-update) | async-done | bytes 393232 | tf_op jit(solution)/shard_map/while/body/eval_jaxpr/reduce_scatter | solution.py:43
  599.6 28.6 %reduce-scatter.41.cloned.1.call-done = f32[128,768]{1,0:T(8,128)} async-done(((f32[512,768]{1,0:T(8,128)}), f32[128,768]{1,0:T(8,128)}) %reduce-scatter.41.cloned.1.call-update) | async-done | bytes 393232 | tf_op jit(solution)/shard_map/while/body/eval_jaxpr/reduce_scatter | solution.py:43
  642.2 16.2 %reduce-scatter.31.cloned.1.call-done = bf16[192,192]{1,0:T(8,128)(2,1)} async-done(((bf16[768,192]{1,0:T(8,128)(2,1)}), bf16[192,192]{1,0:T(8,128)(2,1)}) %reduce-scatter.31.cloned.1.call-update) | async-done | bytes 73744
  660.1 26.0 %reduce-scatter.25.cloned.1.call-done = bf16[192,192]{1,0:T(8,128)(2,1)} async-done(((bf16[768,192]{1,0:T(8,128)(2,1)}), bf16[192,192]{1,0:T(8,128)(2,1)}) %reduce-scatter.25.cloned.1.call-update) | async-done | bytes 73744
  687.7 26.0 %reduce-scatter.27.cloned.1.call-done = bf16[192,192]{1,0:T(8,128)(2,1)} async-done(((bf16[768,192]{1,0:T(8,128)(2,1)}), bf16[192,192]{1,0:T(8,128)(2,1)}) %reduce-scatter.27.cloned.1.call-update) | async-done | bytes 73744
  715.4 25.5 %reduce-scatter.29.cloned.1.call-done = bf16[192,192]{1,0:T(8,128)(2,1)} async-done(((bf16[768,192]{1,0:T(8,128)(2,1)}), bf16[192,192]{1,0:T(8,128)(2,1)}) %reduce-scatter.29.cloned.1.call-update) | async-done | bytes 73744
  742.5 29.8 %reduce-scatter.21.cloned.1.call-done = bf16[192,768]{1,0:T(8,128)(2,1)} async-done(((bf16[768,768]{1,0:T(8,128)(2,1)}), bf16[192,768]{1,0:T(8,128)(2,1)}) %reduce-scatter.21.cloned.1.call-update) | async-done | bytes 294928 | tf_op jit(solution)/shard_map/reduce_scatter | solution.py:307
  772.3 31.3 %reduce-scatter.23.cloned.1.call-done = bf16[768,192]{0,1:T(8,128)(2,1)} async-done(((bf16[768,768]{0,1:T(8,128)(2,1)}), bf16[768,192]{0,1:T(8,128)(2,1)}) %reduce-scatter.23.cloned.1.call-update) | async-done | bytes 294928 | tf_op jit(solution)/shard_map/reduce_scatter | solution.py:313
  803.8 40.8 %all-reduce = (f32[768]{0:T(1024)}, f32[768]{0:T(1024)}, f32[768]{0:T(1024)}, f32[768]{0:T(1024)}, f32[768]{0:T(1024)}, /*index=5*/f32[768]{0:T(1024)}, f32[768]{0:T(1024)}, f32[3072]{0:T(1024)}, f32[768]{0:T(1024)}) all-reduce(f32[768]{0:T(1024)S(1)} %copy-done.61, ...), channel_id=1, replica_groups=mesh['dp'=4,'ctx'=2,'tensor'=4] {'dp','ctx','tensor'}, use_global_device_ids=true, to_apply=%region_28.29 | all-reduce | flops 9216 | bytes 73728 | tf_op jit(solution)/shard_map/psum | solution.py:317
  (477 shorter events, 275.0 us)
Async XLA Ops:
  7.2 55.5 %all-gather.3.cloned.1.call-start = ((), (), s32[]{:S(2)}) async-start(), calls=%async_computation.12 | async-start | bytes 1474560 | tf_op jit(solution)/shard_map/all_gather | solution.py:53
  9.2 65.4 %all-gather.5.cloned.1.call-start = ((), (), s32[]{:S(2)}) async-start(), calls=%async_computation.13 | async-start | bytes 1474560 | tf_op jit(solution)/shard_map/all_gather | solution.py:51
  76.5 85.6 %reduce-scatter.33.cloned.1.call-start = ((), (), s32[]{:S(2)}) async-start(), calls=%async_computation.21 | async-start | bytes 1966080 | tf_op jit(solution)/shard_map/while/body/eval_jaxpr/reduce_scatter | solution.py:43
  117.7 106.2 %reduce-scatter.35.cloned.1.call-start = ((), (), s32[]{:S(2)}) async-start(), calls=%async_computation.22 | async-start | bytes 1966080 | tf_op jit(solution)/shard_map/while/body/eval_jaxpr/reduce_scatter | solution.py:43
  190.0 84.3 %reduce-scatter.37.cloned.1.call-start = ((), (), s32[]{:S(2)}) async-start(), calls=%async_computation.23 | async-start | bytes 589824 | tf_op jit(solution)/shard_map/while/body/eval_jaxpr/reduce_scatter | solution.py:195
  257.2 19.8 %reduce-scatter.39.cloned.1.call-start = ((), (), s32[]{:S(2)}) async-start(), calls=%async_computation.24 | async-start | bytes 589824 | tf_op jit(solution)/shard_map/while/body/eval_jaxpr/reduce_scatter | solution.py:201
  260.6 53.8 %reduce-scatter.43.cloned.1.call-start = ((), (), s32[]{:S(2)}) async-start(), calls=%async_computation.26 | async-start | bytes 1966080 | tf_op jit(solution)/shard_map/while/body/eval_jaxpr/reduce_scatter | solution.py:43
  264.2 86.9 %reduce-scatter.41.cloned.1.call-start = ((), (), s32[]{:S(2)}) async-start(), calls=%async_computation.25 | async-start | bytes 1966080 | tf_op jit(solution)/shard_map/while/body/eval_jaxpr/reduce_scatter | solution.py:43
  354.3 84.2 %reduce-scatter.33.cloned.1.call-start = ((), (), s32[]{:S(2)}) async-start(), calls=%async_computation.21 | async-start | bytes 1966080 | tf_op jit(solution)/shard_map/while/body/eval_jaxpr/reduce_scatter | solution.py:43
  394.2 107.0 %reduce-scatter.35.cloned.1.call-start = ((), (), s32[]{:S(2)}) async-start(), calls=%async_computation.22 | async-start | bytes 1966080 | tf_op jit(solution)/shard_map/while/body/eval_jaxpr/reduce_scatter | solution.py:43
  466.4 85.9 %reduce-scatter.37.cloned.1.call-start = ((), (), s32[]{:S(2)}) async-start(), calls=%async_computation.23 | async-start | bytes 589824 | tf_op jit(solution)/shard_map/while/body/eval_jaxpr/reduce_scatter | solution.py:195
  534.5 20.5 %reduce-scatter.39.cloned.1.call-start = ((), (), s32[]{:S(2)}) async-start(), calls=%async_computation.24 | async-start | bytes 589824 | tf_op jit(solution)/shard_map/while/body/eval_jaxpr/reduce_scatter | solution.py:201
  537.9 53.8 %reduce-scatter.43.cloned.1.call-start = ((), (), s32[]{:S(2)}) async-start(), calls=%async_computation.26 | async-start | bytes 1966080 | tf_op jit(solution)/shard_map/while/body/eval_jaxpr/reduce_scatter | solution.py:43
  541.5 86.8 %reduce-scatter.41.cloned.1.call-start = ((), (), s32[]{:S(2)}) async-start(), calls=%async_computation.25 | async-start | bytes 1966080 | tf_op jit(solution)/shard_map/while/body/eval_jaxpr/reduce_scatter | solution.py:43
  631.7 26.8 %reduce-scatter.31.cloned.1.call-start = ((), (), s32[]{:S(2)}) async-start(), calls=%async_computation.19 | async-start | bytes 491520
  633.9 52.3 %reduce-scatter.25.cloned.1.call-start = ((), (), s32[]{:S(2)}) async-start(), calls=%async_computation.16 | async-start | bytes 491520
  634.9 78.9 %reduce-scatter.27.cloned.1.call-start = ((), (), s32[]{:S(2)}) async-start(), calls=%async_computation.17 | async-start | bytes 491520
  637.0 103.9 %reduce-scatter.29.cloned.1.call-start = ((), (), s32[]{:S(2)}) async-start(), calls=%async_computation.18 | async-start | bytes 491520
  638.0 134.3 %reduce-scatter.21.cloned.1.call-start = ((), (), s32[]{:S(2)}) async-start(), calls=%async_computation.14 | async-start | bytes 1474560 | tf_op jit(solution)/shard_map/reduce_scatter | solution.py:307
  639.3 164.4 %reduce-scatter.23.cloned.1.call-start = ((), (), s32[]{:S(2)}) async-start(), calls=%async_computation.15 | async-start | bytes 1474560 | tf_op jit(solution)/shard_map/reduce_scatter | solution.py:313
  642.1 161.6 %copy-start.58 = (f32[768]{0:T(1024)S(1)}, f32[768]{0:T(1024)}, u32[]{:S(2)}) copy-start(f32[768]{0:T(1024)} %get-tuple-element.655) | copy-start | bytes 9220
  642.1 161.6 %copy-start.61 = (f32[768]{0:T(1024)S(1)}, f32[768]{0:T(1024)}, u32[]{:S(2)}) copy-start(f32[768]{0:T(1024)} %get-tuple-element.654) | copy-start | bytes 9220
  642.1 161.6 %copy-start.65 = (f32[768]{0:T(1024)S(1)}, f32[768]{0:T(1024)}, u32[]{:S(2)}) copy-start(f32[768]{0:T(1024)} %get-tuple-element.660) | copy-start | bytes 9220
  642.2 202.4 %all-reduce.4.cloned.1.call-start = ((), (), s32[]{:S(2)}) async-start(), calls=%async_computation.20 | async-start | bytes 1966080 | tf_op jit(solution)/shard_map/psum | solution.py:290
  (120 other events, 2238.5 us)
Sparse Core Ops, SparseCore 0:
  9.9 34.1 all-gather.2
  46.0 28.6 all-gather.4
  117.8 44.2 reduce-scatter.32
  190.1 33.7 reduce-scatter.34
  257.3 7.0 reduce-scatter.36
  266.5 8.9 reduce-scatter.38
  277.8 36.4 reduce-scatter.42
  316.8 34.2 reduce-scatter.40
  394.3 44.2 reduce-scatter.32
  466.5 34.6 reduce-scatter.34
  534.6 7.0 reduce-scatter.36
  543.8 8.9 reduce-scatter.38
  555.2 36.4 reduce-scatter.42
  593.9 34.2 reduce-scatter.40
  635.0 23.3 reduce-scatter.30
  661.7 24.4 reduce-scatter.24
  689.3 24.4 reduce-scatter.26
  716.4 24.3 reduce-scatter.28
  743.8 28.5 reduce-scatter.20
  775.1 28.5 reduce-scatter.22
  807.6 19.6 all-reduce.3
where the time goes:
time: 864 us; the launch traced here: 862 us
  waiting for transfers between devices  372 us (43%)
  blocking collectives  263 us (30%)
  matrix products  101 us (12%)
  other arithmetic  62.3 us (7%)
  local copies, waits for them, and re-layouts  46 us (5%)
  between operations  14.6 us (2%)
    reduce_scatter x8, waiting for transfers between devices, tensor_sums(): return lax.psum_scatter(block, 'tensor', scatter_dimension=0, tiled=True)  207 us
    all_gather x8, blocking collectives, tensor_rows(): return lax.all_gather(block, 'tensor', axis=0, tiled=True)  168 us
    unnamed x13, waiting for transfers between devices  93.9 us
    psum x1, blocking collectives, body(): lax.psum((small_sums[0], small_sums[1], small_sums[2], small_sums[3], sma...  40.8 us
    reduce_scatter x1, waiting for transfers between devices, body(): lax.psum_scatter(paired[5].astype(jnp.bfloat16), 'dp', scatter_dimension=...  31.3 us
    reduce_scatter x1, waiting for transfers between devices, body(): lax.psum_scatter(paired[3].astype(jnp.bfloat16), 'dp', scatter_dimension=...  29.8 us
    unnamed x48, local copies, waits for them, and re-layouts  18.7 us
  transfers between devices with their start and end apart: 21, of which 15 were waited for; matrix products, arithmetic and copies ran while one was open for 12% of the time, Pallas kernels for 0%

commit v1 on v0

--- a/solution.py
+++ b/solution.py
@@ -1,33 +1,582 @@
+import functools
+
 import jax
 import jax.numpy as jnp
 from jax import lax
+from jax.experimental import pallas as pl
+from jax.experimental.pallas import tpu as pltpu
 from jax.sharding import PartitionSpec as P
 
 HDIM = 64
+LANES = 256
+ROOT_HALF = 0.7071067811865476
+INV_ROOT_TWO_PI = 0.3989422804014327
+MESH = pl.DeviceIdType.MESH
+BF = jnp.bfloat16
+F32 = jnp.float32
+HIDE = -1e30
+
+
+def dims(left, right, a, b):
+    return lax.dot_general(left, right, (((a,), (b,)), ((), ())), preferred_element_type=F32)
+
+
+def norm_parts(rows):
+    centred = rows - jnp.mean(rows, axis=-1, keepdims=True)
+    inverse = lax.rsqrt(jnp.mean(centred * centred, axis=-1, keepdims=True) + 1e-05)
+    return centred * inverse, inverse
+
+
+class Place:
+    def __init__(self):
+        self.d = lax.axis_index("dp")
+        self.c = lax.axis_index("ctx")
+        self.t = lax.axis_index("tensor")
+        col, row = self.d % 2, self.d // 2
+        self.dx = row * 2 + (1 - col)
+        self.dy = (1 - row) * 2 + col
+        self.dd = (1 - row) * 2 + (1 - col)
+        self.side = self.t // 2
+        self.mid = self.t + self.side * (3 - 2 * self.t)
+
+    def unmirror(self, place):
+        return place + self.side * (3 - 2 * place)
+
+    def order(self, k):
+        if k == 0:
+            return self.unmirror(1 - self.mid)
+        return self.unmirror(k + 1)
+
+    def order_at(self, k):
+        first = 1 - jnp.minimum(k, 1)
+        near = first * (1 - self.mid) + (1 - first) * (k + 1)
+        own = jnp.minimum(k, 0)
+        return -own * self.t + (1 + own) * self.unmirror(near)
+
+
+def remote(src, dst, send, recv, **where):
+    return pltpu.make_async_remote_copy(
+        src_ref=src, dst_ref=dst, send_sem=send, recv_sem=recv, device_id=where, device_id_type=MESH
+    )
+
+
+def greet(place, line=True, plane=True, core=True):
+    barrier = pltpu.get_barrier_semaphore()
+    count = 0
+    if line:
+        for k in range(1, 4):
+            pl.semaphore_signal(
+                barrier, inc=1, device_id={"tensor": (place.t + k) % 4}, device_id_type=MESH
+            )
+        count += 3
+    if plane:
+        for peer in (place.dx, place.dy, place.dd):
+            pl.semaphore_signal(barrier, inc=1, device_id={"dp": peer}, device_id_type=MESH)
+        count += 3
+    if core:
+        pl.semaphore_signal(barrier, inc=1, device_id={"ctx": 1 - place.c}, device_id_type=MESH)
+        count += 1
+    pl.semaphore_wait(barrier, count)
+
+
+def forward_kernel(
+    hidden, gain, shift, wqkv_s, cargo_s, bias_s, out_bias, gain_f, shift_f, seg_k, seg_q,
+    normed, queries, kv, mixed_in, middle, normed_f, wqkv, wout, weights,
+    cargo, hide, v_turn, mix_turn, mixed,
+    z_send, z_recv, w_send, w_recv, kv_send, kv_recv, m_send, m_recv,
+    cz_send, cp_send, cc_send, c_recv, s_recv, own_sem, out_sem,
+):
+    at = Place()
+    d, c, t = at.d, at.c, at.t
+    greet(at)
+
+    planes = (at.dx, at.dy, at.dd)
+    w_out = [
+        remote(wqkv_s, wqkv.at[d], w_send.at[i], w_recv.at[d], dp=peer)
+        for i, peer in enumerate(planes)
+    ]
+    for copy in w_out:
+        copy.start()
+    own_w = pltpu.make_async_copy(wqkv_s, wqkv.at[d], own_sem.at[0])
+    own_w.start()
+    own_c = pltpu.make_async_copy(cargo_s, cargo.at[c, t, d], own_sem.at[1])
+    own_c.start()
+
+    def z_copy(s, k, dest):
+        return remote(
+            normed.at[s, t], normed.at[s, t], z_send.at[s, k], z_recv.at[s, t], tensor=dest
+        )
+
+    def z_pass(s, shard, dest):
+        return remote(
+            normed.at[s, shard], normed.at[s, shard], z_send.at[s, 3], z_recv.at[s, shard], tensor=dest
+        )
+
+    for s in range(2):
+        scaled, _ = norm_parts(hidden[s])
+        normed[s, t] = (scaled * gain[...] + shift[...]).astype(BF)
+        z_copy(s, 0, at.order(0)).start()
+        z_copy(s, 1, at.order(1)).start()
+
+        @pl.when(at.mid == 1)
+        def _():
+            z_copy(s, 2, at.order(2)).start()
+
+    own_w.wait()
+    own_c.wait()
+
+    def cargo_z(k, dest):
+        return remote(
+            cargo.at[c, t, d], cargo.at[c, t, d], cz_send.at[k], c_recv.at[t, d], tensor=dest
+        )
+
+    def cargo_pass(shard, dest):
+        return remote(
+            cargo.at[c, shard, d], cargo.at[c, shard, d], cz_send.at[3], c_recv.at[shard, d], tensor=dest
+        )
+
+    def cargo_plane(axis, k, shard, owner, dest):
+        return remote(
+            cargo.at[c, shard, owner], cargo.at[c, shard, owner], cp_send.at[axis, k],
+            c_recv.at[shard, owner], dp=dest,
+        )
+
+    def cargo_core(shard, owner):
+        return remote(
+            cargo.at[c, shard, owner], cargo.at[c, shard, owner], cc_send.at[shard, owner],
+            s_recv.at[shard, owner], ctx=1 - c,
+        )
+
+    def cargo_keep(which, shard, owner):
+        return pltpu.make_async_copy(
+            cargo.at[which, shard, owner, pl.ds(0, 192)], weights.at[which, shard, owner],
+            out_sem.at[which, shard, owner],
+        )
+
+    def arrived(shard, owner):
+        remote(
+            cargo.at[c, shard, owner], cargo.at[c, shard, owner], cz_send.at[0],
+            c_recv.at[shard, owner], dp=d,
+        ).wait_recv()
+
+    def spread(k, shard):
+        cargo_plane(0, k, shard, d, at.dx).start()
+        cargo_plane(1, k, shard, d, at.dy).start()
+        cargo_core(shard, d).start()
+        cargo_keep(c, shard, d).start()
+
+    spread(0, t)
+
+    for i, peer in enumerate(planes):
+        remote(wqkv_s, wqkv.at[peer], w_send.at[i], w_recv.at[peer], dp=peer).wait_recv()
+
+    lane_head = lax.broadcasted_iota(jnp.int32, (1, LANES), 1) // HDIM
+
+    def attend(s):
+        keys_seg = seg_k[s]
+        for b in range(2):
+            hide[:, b * 256 : (b + 1) * 256] = jnp.where(
+                keys_seg == seg_q[s, :, b * 256 : (b + 1) * 256], 0.0, HIDE
+            ).astype(F32)
+        all_kv = kv[s].reshape(1024, 2 * LANES)
+        v_turn[...] = all_kv[:, LANES:].T
+        mix_turn[192:, :] = jnp.zeros((64, 512), F32)
+
+        def step(i, carry):
+            h, b = i // 2, i % 2
+            block = pl.ds(pl.multiple_of(b * 256, 256), 256)
+            q_here = queries[s, block, :]
+            q_here = jnp.where(lane_head == h, q_here.astype(F32), 0.0).astype(BF)
+            scores = dims(kv[s].reshape(1024, 2 * LANES)[:, :LANES], q_here, 1, 1) + hide[:, block]
+            peak = jnp.max(scores, axis=0, keepdims=True)
+            expo = jnp.exp(scores - peak)
+            total = jnp.sum(expo, axis=0, keepdims=True)
+            rows = pl.ds(pl.multiple_of(h * HDIM, HDIM), HDIM)
+            turned = jnp.dot(v_turn[rows, :], expo.astype(BF), preferred_element_type=F32)
+            mix_turn[rows, block] = turned / total
+            return carry
+
+        lax.fori_loop(0, 6, step, 0)
+        mixed[s] = mix_turn[...].T.astype(BF).reshape(4, 128, LANES)
+
+    def m_copy(s, k, dest):
+        return remote(
+            mixed.at[s, dest], mixed_in.at[t, s], m_send.at[s, k], m_recv.at[s, t], tensor=dest
+        )
+
+    def kv_copy(s, p):
+        return remote(
+            kv.at[s, c, p], kv.at[s, c, p], kv_send.at[s, p], kv_recv.at[s, p], ctx=1 - c
+        )
+
+    for s in range(2):
+        def project(k, carry):
+            p = at.order_at(k - 1)
+
+            @pl.when(k > 0)
+            def _():
+                remote(
+                    normed.at[s, p], normed.at[s, p], z_send.at[s, 0], z_recv.at[s, p], tensor=p
+                ).wait_recv()
+
+            @pl.when((k == 3) & (at.mid == 1))
+            def _():
+                z_pass(s, p, at.unmirror(0)).start()
+
+            out = jnp.dot(
+                normed[s, p], wqkv[...].reshape(768, 768), preferred_element_type=F32
+            ) + bias_s[...]
+            out = out.astype(BF)
+            queries[s, pl.ds(pl.multiple_of(p * 128, 128), 128), :] = (
+                out[:, :LANES] * jnp.asarray(HDIM**-0.5, BF)
+            )
+            kv[s, c, p] = out[:, LANES:]
+            kv_copy(s, p).start()
+            return carry
+
+        lax.fori_loop(0, 4, project, 0)
+        if s == 0:
+            cargo_z(0, at.order(0)).start()
+            cargo_z(1, at.order(1)).start()
+
+            @pl.when(at.mid == 1)
+            def _():
+                cargo_z(2, at.order(2)).start()
+
+        for p in range(4):
+            remote(
+                kv.at[s, 1 - c, p], kv.at[s, 1 - c, p], kv_send.at[s, p], kv_recv.at[s, p], ctx=1 - c
+            ).wait_recv()
+        attend(s)
+        for k in range(3):
+            m_copy(s, k, (t + k + 1) % 4).start()
+        mixed_in[t, s] = mixed[s, t]
+
+    def diag(k, shard):
+        arrived(shard, at.dx)
+        arrived(shard, at.dy)
+
+        @pl.when(shard < 2)
+        def _():
+            cargo_plane(1, 4 + k, shard, at.dx, at.dy).start()
+
+        @pl.when(shard >= 2)
+        def _():
+            cargo_plane(0, 4 + k, shard, at.dy, at.dx).start()
+
+        cargo_core(shard, at.dx).start()
+        cargo_core(shard, at.dy).start()
+        cargo_keep(c, shard, at.dx).start()
+        cargo_keep(c, shard, at.dy).start()
+
+    for k in range(3):
+        p = at.order(k)
+        arrived(p, d)
+        if k == 2:
+
+            @pl.when(at.mid == 1)
+            def _():
+                cargo_pass(p, at.unmirror(0)).start()
+
+        spread(k + 1, p)
+        diag(k, t if k == 0 else at.order(k - 1))
+    diag(3, at.order(2))
+    for p in range(4):
+        arrived(p, at.dd)
+        cargo_core(p, at.dd).start()
+        cargo_keep(c, p, at.dd).start()
+
+    def from_sibling(i, carry):
+        shard, owner = i // 4, i % 4
+        remote(
+            cargo.at[1 - c, shard, owner], cargo.at[1 - c, shard, owner], cc_send.at[shard, owner],
+            s_recv.at[shard, owner], ctx=1 - c,
+        ).wait_recv()
+        cargo_keep(1 - c, shard, owner).start()
+        for part in range(2):
+            for j in range(3):
+                start = pl.multiple_of(owner * 192 + part * 96 + j * 32, 32)
+                wout[shard, pl.ds(start, 32), :] = cargo[
+                    part, shard, owner, 192:224, j * LANES : (j + 1) * LANES
+                ]
+        return carry
+
+    lax.fori_loop(0, 16, from_sibling, 0)
+
+    for s in range(2):
+        for k in range(3):
+            p = (t + k + 1) % 4
+            remote(
+                mixed.at[s, p], mixed_in.at[p, s], m_send.at[s, k], m_recv.at[s, p], tensor=p
+            ).wait_recv()
+        total = hidden[s] + out_bias[...]
+        for p in range(4):
+            total = total + dims(mixed_in[p, s], wout[p], 1, 1)
+        middle[s] = total
+        scaled, _ = norm_parts(total)
+        normed_f[s] = (scaled * gain_f[...] + shift_f[...]).astype(BF)
+
+    for copy in w_out:
+        copy.wait_send()
+    for s in range(2):
+        z_copy(s, 0, at.order(0)).wait_send()
+        z_copy(s, 1, at.order(1)).wait_send()
+
+        @pl.when(at.mid == 1)
+        def _():
+            z_copy(s, 2, at.order(2)).wait_send()
+            z_pass(s, at.order(2), at.unmirror(0)).wait_send()
+
+        for p in range(4):
+            kv_copy(s, p).wait_send()
+        for k in range(3):
+            m_copy(s, k, (t + k + 1) % 4).wait_send()
+    cargo_z(0, at.order(0)).wait_send()
+    cargo_z(1, at.order(1)).wait_send()
+
+    @pl.when(at.mid == 1)
+    def _():
+        cargo_z(2, at.order(2)).wait_send()
+        cargo_pass(at.order(2), at.unmirror(0)).wait_send()
+
+    for k in range(4):
+        p = t if k == 0 else at.order(k - 1)
+        cargo_plane(0, k, p, d, at.dx).wait_send()
+        cargo_plane(1, k, p, d, at.dy).wait_send()
+
+        @pl.when(p < 2)
+        def _():
+            cargo_plane(1, 4 + k, p, at.dx, at.dy).wait_send()
+
+        @pl.when(p >= 2)
+        def _():
+            cargo_plane(0, 4 + k, p, at.dy, at.dx).wait_send()
+
+    def finish(i, carry):
+        shard, owner = i // 4, i % 4
+        cargo_core(shard, owner).wait_send()
+        cargo_keep(0, shard, owner).wait()
+        cargo_keep(1, shard, owner).wait()
+        return carry
+
+    lax.fori_loop(0, 16, finish, 0)
+
+
+VM = pl.BlockSpec(memory_space=pltpu.VMEM)
+ANY = pl.BlockSpec(memory_space=pl.ANY)
+
+
+def forward_call(*operands):
+    struct = jax.ShapeDtypeStruct
+    dma = pltpu.SemaphoreType.DMA
+    return pl.pallas_call(
+        forward_kernel,
+        out_shape=(
+            struct((2, 4, 128, 768), BF),
+            struct((2, 512, LANES), BF),
+            struct((2, 2, 4, 128, 2 * LANES), BF),
+            struct((4, 2, 128, LANES), BF),
+            struct((2, 128, 768), F32),
+            struct((2, 128, 768), BF),
+            struct((4, 192, 768), BF),
+            struct((4, 768, LANES), BF),
+            struct((2, 4, 4, 192, 768), BF),
+        ),
+        in_specs=[VM] * len(operands),
+        out_specs=(VM,) * 8 + (ANY,),
+        scratch_shapes=[
+            pltpu.VMEM((2, 4, 4, 224, 768), BF),
+            pltpu.VMEM((1024, 512), F32),
+            pltpu.VMEM((LANES, 1024), BF),
+            pltpu.VMEM((LANES, 512), F32),
+            pltpu.VMEM((2, 4, 128, LANES), BF),
+            dma((2, 4)), dma((2, 4)),
+            dma((3,)), dma((4,)),
+            dma((2, 4)), dma((2, 4)),
+            dma((2, 3)), dma((2, 4)),
+            dma((4,)), dma((2, 8)), dma((4, 4)), dma((4, 4)), dma((4, 4)),
+            dma((2,)), dma((2, 4, 4)),
+        ],
+        compiler_params=pltpu.CompilerParams(
+            collective_id=1, has_side_effects=True, vmem_limit_bytes=56 << 20
+        ),
+        name="forward",
+    )(*operands)
+
+
+def pad_heads(block):
+    return jnp.pad(block, [(0, 0)] * (block.ndim - 1) + [(0, LANES - block.shape[-1])])
+
+
+def smooth_slope(values, cdf):
+    return cdf + values * (jnp.exp(-0.5 * values * values) * INV_ROOT_TWO_PI)
+
+
+def norm_backward(grad_out, scaled, inverse, gain):
+    grad_scaled = grad_out * gain
+    plain_mean = jnp.mean(grad_scaled, axis=-1, keepdims=True)
+    cross_mean = jnp.mean(grad_scaled * scaled, axis=-1, keepdims=True)
+    grad_rows = inverse * (grad_scaled - plain_mean - scaled * cross_mean)
+    return (grad_rows, jnp.sum(grad_out * scaled, axis=(0, 1)), jnp.sum(grad_out, axis=(0, 1)))
+
+
+def place_piece(piece, total, start):
+    return lax.dynamic_update_slice(jnp.zeros((total,), F32), piece, (start,))
+
+
+def body(
+    hidden_in, cotangent, segment_ids, attn_gain, attn_shift, query_weight, key_weight,
+    value_weight, query_bias, value_bias, output_weight, output_bias, ffn_gain, ffn_shift,
+    inner_weight, inner_bias, outer_weight, outer_bias,
+):
+    part = query_weight.shape[1]
+    tensor_at = lax.axis_index("tensor")
+    ctx_at = lax.axis_index("ctx")
+    wqkv_s = jnp.concatenate(
+        [pad_heads(query_weight), pad_heads(key_weight), pad_heads(value_weight)], axis=1
+    ).astype(BF)
+    wout_s = pad_heads(output_weight.T.astype(BF))
+    wout_half = lax.dynamic_slice_in_dim(wout_s, ctx_at * 96, 96)
+    wout_half = wout_half.reshape(3, 32, LANES).transpose(1, 0, 2).reshape(32, 768)
+    ff_s = jnp.where(ctx_at == 0, inner_weight, outer_weight.T).astype(BF)
+    cargo_s = jnp.concatenate([ff_s, wout_half], axis=0)
+    q_piece = lax.dynamic_slice_in_dim(query_bias, tensor_at * part, part)
+    v_piece = lax.dynamic_slice_in_dim(value_bias, tensor_at * part, part)
+    bias_s = jnp.concatenate(
+        [pad_heads(q_piece), jnp.zeros((LANES,), F32), pad_heads(v_piece)]
+    )[None, :]
+    places = jnp.arange(segment_ids.shape[1], dtype=jnp.int32)[None, :]
+    seg = jnp.where(segment_ids >= 0, segment_ids, -1 - places)
+    seg_q = lax.dynamic_slice_in_dim(seg, ctx_at * 512, 512, axis=1)
+
+    (normed, queries, kv, mixed_in, middle, normed_f, wqkv, wout, weights) = forward_call(
+        hidden_in, attn_gain[None], attn_shift[None], wqkv_s, cargo_s, bias_s, output_bias[None],
+        ffn_gain[None], ffn_shift[None], seg[:, :, None], seg_q[:, None, :],
+    )
+    w_in = weights[0].reshape(4, 768, 768)
+    w_out = weights[1].reshape(4, 768, 768)
+
+    scaled_a, inverse_a = norm_parts(hidden_in)
+    scaled_f, inverse_f = norm_parts(middle)
+    nf = normed_f.reshape(256, 768)
+    cot = cotangent.reshape(256, 768)
+    up = cot.astype(BF)
+    inner = jnp.einsum("rd,tdu->rtu", nf, w_in, preferred_element_type=F32) + inner_bias.reshape(4, 768)
+    cdf = 0.5 * (1.0 + lax.erf(inner * ROOT_HALF))
+    active = (inner * cdf).astype(BF)
+    block_out = middle + jnp.einsum(
+        "rtu,tdu->rd", active, w_out, preferred_element_type=F32
+    ).reshape(2, 128, 768) + outer_bias
+    grad_active = jnp.einsum("rd,tdu->rtu", up, w_out, preferred_element_type=F32)
+    grad_inner = (grad_active * smooth_slope(inner, cdf)).astype(BF)
+    grad_nf = jnp.einsum("rtu,tdu->rd", grad_inner, w_in, preferred_element_type=F32)
+    grad_w_in = jnp.einsum("rd,rtu->tdu", nf, grad_inner, preferred_element_type=F32)
+    grad_w_out = jnp.einsum("rd,rtu->tdu", up, active, preferred_element_type=F32)
+    grad_rows_f, grad_ffn_g, grad_ffn_s = norm_backward(
+        grad_nf.reshape(2, 128, 768), scaled_f, inverse_f, ffn_gain
+    )
+    grad_middle = cotangent + grad_rows_f
+    grad_branch = grad_middle.astype(BF)
+    gb = grad_branch.reshape(256, 768)
+    grad_wout = jnp.einsum(
+        "trc,rd->tdc", mixed_in.reshape(4, 256, LANES), gb, preferred_element_type=F32
+    )
+    grad_mix = jnp.einsum("rd,tdc->trc", gb, wout, preferred_element_type=F32).astype(BF)
+    grad_mix = lax.all_to_all(grad_mix.reshape(4, 2, 128, LANES), "tensor", 0, 0, tiled=True)
+    grad_mixed = grad_mix.transpose(1, 0, 2, 3).reshape(2, 512, LANES)[..., :part]
+    heads = part // HDIM
+    q3 = queries[..., :part].reshape(2, 512, heads, HDIM)
+    k3 = kv[..., :part].reshape(2, 1024, heads, HDIM)
+    v3 = kv[..., LANES : LANES + part].reshape(2, 1024, heads, HDIM)
+    g3 = grad_mixed.reshape(2, 512, heads, HDIM)
+    scores = jnp.einsum("sqhd,skhd->shqk", q3, k3, preferred_element_type=F32)
+    scores = jnp.where((seg_q[:, :, None] == seg[:, None, :])[:, None], scores, HIDE)
+    probs = jax.nn.softmax(scores, axis=-1)
+    grad_probs = jnp.einsum("sqhd,skhd->shqk", g3, v3, preferred_element_type=F32)
+    centre = jnp.sum(probs * grad_probs, axis=-1, keepdims=True)
+    grad_scores = (probs * (grad_probs - centre)).astype(BF)
+    grad_v = jnp.einsum("shqk,sqhd->skhd", probs.astype(BF), g3, preferred_element_type=F32)
+    grad_k = jnp.einsum("shqk,sqhd->skhd", grad_scores, q3, preferred_element_type=F32)
+    grad_q = jnp.einsum("shqk,skhd->sqhd", grad_scores, k3, preferred_element_type=F32) * HDIM**-0.5
+    grad_q = grad_q.reshape(2, 512, part).astype(BF)
+    grad_k = lax.psum_scatter(
+        grad_k.reshape(2, 1024, part).astype(BF), "ctx", scatter_dimension=1, tiled=True
+    )
+    grad_v = lax.psum_scatter(
+        grad_v.reshape(2, 1024, part).astype(BF), "ctx", scatter_dimension=1, tiled=True
+    )
+    grad_qkv = jnp.concatenate([pad_heads(grad_q), pad_heads(grad_k), pad_heads(grad_v)], axis=-1)
+    grad_qkv = grad_qkv.reshape(1024, 768)
+    grad_wqkv = jnp.einsum(
+        "rd,rc->dc", normed.reshape(1024, 768), grad_qkv, preferred_element_type=F32
+    )
+    grad_na = jnp.einsum("rc,dc->rd", grad_qkv, wqkv.reshape(768, 768), preferred_element_type=F32)
+    grad_na = lax.psum_scatter(
+        grad_na.astype(BF).reshape(2, 512, 768), "tensor", scatter_dimension=1, tiled=True
+    ).astype(F32)
+    grad_rows_a, grad_attn_g, grad_attn_s = norm_backward(grad_na, scaled_a, inverse_a, attn_gain)
+    grad_input = grad_middle + grad_rows_a
+
+    g_in = lax.psum_scatter(
+        grad_w_in.astype(BF).reshape(4, 4, 192, 768), "tensor", scatter_dimension=0, tiled=True
+    )
+    g_in = lax.psum_scatter(g_in, "dp", scatter_dimension=1, tiled=True).reshape(192, 768)
+    g_out = lax.psum_scatter(
+        grad_w_out.astype(BF).reshape(4, 4, 192, 768), "tensor", scatter_dimension=0, tiled=True
+    )
+    g_out = lax.psum_scatter(g_out, "dp", scatter_dimension=1, tiled=True).reshape(192, 768)
+    g_wo = lax.psum_scatter(
+        grad_wout.astype(BF).reshape(4, 4, 192, LANES), "tensor", scatter_dimension=0, tiled=True
+    )
+    g_wo = lax.psum_scatter(g_wo, "dp", scatter_dimension=1, tiled=True).reshape(192, LANES)
+    g_qkv = lax.psum_scatter(
+        grad_wqkv.astype(BF).reshape(4, 192, 768), "dp", scatter_dimension=0, tiled=True
+    ).reshape(192, 768)
+    g_in, g_out, g_wo, g_qkv = lax.psum((g_in, g_out, g_wo, g_qkv), "ctx")
+    g_in, g_out, g_wo, g_qkv = (g.astype(F32) for g in (g_in, g_out, g_wo, g_qkv))
+    sums = jnp.sum(grad_qkv.astype(F32), axis=0)
+    small = lax.psum(
+        jnp.concatenate([
+            grad_attn_g, grad_attn_s,
+            place_piece(sums[:part], 768, tensor_at * part),
+            place_piece(sums[2 * LANES : 2 * LANES + part], 768, tensor_at * part),
+            jnp.sum(grad_middle, axis=(0, 1)), grad_ffn_g, grad_ffn_s,
+            jnp.sum(cotangent, axis=(0, 1)),
+            jnp.sum(grad_inner.astype(F32), axis=0).reshape(3072),
+        ]),
+        ("dp", "ctx", "tensor"),
+    )
+    row = lambda i: small[768 * i : 768 * (i + 1)]
+    return (
+        block_out, grad_input, row(0), row(1),
+        g_qkv[:, :part], g_qkv[:, LANES : LANES + part], g_qkv[:, 2 * LANES : 2 * LANES + part],
+        row(2), row(3), g_wo[:, :part].T, row(4), row(5), row(6), g_in, small[768 * 8 :],
+        g_out.T, row(7),
+    )
 
 
 root_half = 0.7071067811865476
 inv_root_two_pi = 0.3989422804014327
 
 
-def smooth_gate(values):
+def general_gate(values):
     return values * (0.5 * (1.0 + lax.erf(values * root_half)))
 
 
-def smooth_slope(values):
+def general_slope(values):
     normal_cdf = 0.5 * (1.0 + lax.erf(values * root_half))
     normal_pdf = jnp.exp(-0.5 * values * values) * inv_root_two_pi
     return normal_cdf + values * normal_pdf
 
 
-def norm_forward(rows, gain, shift):
+def general_norm(rows, gain, shift):
     centred = rows - jnp.mean(rows, axis=-1, keepdims=True)
     inverse = lax.rsqrt(jnp.mean(centred * centred, axis=-1, keepdims=True) + 1e-05)
     scaled = centred * inverse
     return (scaled * gain + shift, scaled, inverse)
 
 
-def norm_backward(grad_out, scaled, inverse, gain):
+def general_norm_backward(grad_out, scaled, inverse, gain):
     grad_scaled = grad_out * gain
     plain_mean = jnp.mean(grad_scaled, axis=-1, keepdims=True)
     cross_mean = jnp.mean(grad_scaled * scaled, axis=-1, keepdims=True)
@@ -54,11 +603,11 @@
     )
 
 
-def place_piece(piece, total, start):
+def general_piece(piece, total, start):
     return lax.dynamic_update_slice(jnp.zeros((total,), jnp.float32), piece, (start,))
 
 
-def body(
+def general_body(
     hidden_in,
     cotangent,
     segment_ids,
@@ -116,7 +665,7 @@
         allowed = (query_seg[:, None] == segment_row[None, :]) & (
             (segment_row[None, :] >= 0) | (query_index[:, None] == key_index[None, :])
         )
-        normed, scaled_a, inverse_a = norm_forward(rows, attn_gain, attn_shift)
+        normed, scaled_a, inverse_a = general_norm(rows, attn_gain, attn_shift)
         normed_all = tensor_rows(normed.astype(jnp.bfloat16))
         queries = (
             jnp.dot(normed_all, w_query, preferred_element_type=jnp.float32) + query_piece
@@ -144,16 +693,16 @@
         mixed = mixed.reshape(half_rows, part_width).astype(jnp.bfloat16)
         branch_a = tensor_sums(jnp.dot(mixed, w_output, preferred_element_type=jnp.float32))
         middle = rows + branch_a + output_bias
-        normed_f, scaled_f, inverse_f = norm_forward(middle, ffn_gain, ffn_shift)
+        normed_f, scaled_f, inverse_f = general_norm(middle, ffn_gain, ffn_shift)
         normed_f_all = tensor_rows(normed_f.astype(jnp.bfloat16))
         inner = jnp.dot(normed_f_all, w_inner, preferred_element_type=jnp.float32) + inner_piece
-        active = smooth_gate(inner).astype(jnp.bfloat16)
+        active = general_gate(inner).astype(jnp.bfloat16)
         branch_f = tensor_sums(jnp.dot(active, w_outer, preferred_element_type=jnp.float32))
         result_rows = middle + branch_f + outer_bias
         grad_up = tensor_rows(cot_rows.astype(jnp.bfloat16))
         grad_outer_w = jnp.einsum("tf,td->fd", active, grad_up, preferred_element_type=jnp.float32)
         grad_active = jnp.einsum("td,fd->tf", grad_up, w_outer, preferred_element_type=jnp.float32)
-        grad_inner = (grad_active * smooth_slope(inner)).astype(jnp.bfloat16)
+        grad_inner = (grad_active * general_slope(inner)).astype(jnp.bfloat16)
         grad_inner_w = jnp.einsum(
             "td,tf->df", normed_f_all, grad_inner, preferred_element_type=jnp.float32
         )
@@ -161,7 +710,7 @@
         grad_normed_f = tensor_sums(
             jnp.einsum("tf,df->td", grad_inner, w_inner, preferred_element_type=jnp.float32)
         )
-        grad_rows_f, grad_ffn_g, grad_ffn_s = norm_backward(
+        grad_rows_f, grad_ffn_g, grad_ffn_s = general_norm_backward(
             grad_normed_f, scaled_f, inverse_f, ffn_gain
         )
         grad_middle = cot_rows + grad_rows_f
@@ -228,7 +777,7 @@
             "tc,dc->td", grad_values, w_value, preferred_element_type=jnp.float32
         )
         grad_normed = tensor_sums(grad_normed_part)
-        grad_rows_a, grad_attn_g, grad_attn_s = norm_backward(
+        grad_rows_a, grad_attn_g, grad_attn_s = general_norm_backward(
             grad_normed, scaled_a, inverse_a, attn_gain
         )
         grad_rows = grad_middle + grad_rows_a
@@ -244,12 +793,12 @@
         small_terms = (
             grad_attn_g,
             grad_attn_s,
-            place_piece(grad_query_b, width, tensor_at * part_width),
-            place_piece(grad_value_b, width, tensor_at * part_width),
+            general_piece(grad_query_b, width, tensor_at * part_width),
+            general_piece(grad_value_b, width, tensor_at * part_width),
             jnp.sum(grad_middle, axis=0),
             grad_ffn_g,
             grad_ffn_s,
-            place_piece(grad_inner_b, unit_total, tensor_at * unit_width),
+            general_piece(grad_inner_b, unit_total, tensor_at * unit_width),
             jnp.sum(cot_rows, axis=0),
         )
         small_sums = tuple((old + new for old, new in zip(small_sums, small_terms)))
@@ -349,48 +898,20 @@
     )
 
 
+SPECS = (
+    P("dp", ("ctx", "tensor"), None), P("dp", ("ctx", "tensor"), None), P("dp", None), P(), P(),
+    P("dp", "tensor"), P("dp", "tensor"), P("dp", "tensor"), P(), P(), P("tensor", "dp"), P(), P(),
+    P(), P("dp", "tensor"), P(), P("tensor", "dp"), P(),
+)
+OUT_SPECS = (
+    P("dp", ("ctx", "tensor"), None), P("dp", ("ctx", "tensor"), None), P(), P(),
+    P("dp", "tensor"), P("dp", "tensor"), P("dp", "tensor"), P(), P(), P("tensor", "dp"), P(), P(),
+    P(), P("dp", "tensor"), P(), P("tensor", "dp"), P(),
+)
+
+
 def solution(mesh):
+    lined_up = mesh.shape["dp"] == 4 and mesh.shape["tensor"] == 4 and mesh.shape["ctx"] == 2
     return jax.shard_map(
-        body,
-        mesh=mesh,
-        in_specs=(
-            P("dp", ("ctx", "tensor"), None),
-            P("dp", ("ctx", "tensor"), None),
-            P("dp", None),
-            P(),
-            P(),
-            P("dp", "tensor"),
-            P("dp", "tensor"),
-            P("dp", "tensor"),
-            P(),
-            P(),
-            P("tensor", "dp"),
-            P(),
-            P(),
-            P(),
-            P("dp", "tensor"),
-            P(),
-            P("tensor", "dp"),
-            P(),
-        ),
-        out_specs=(
-            P("dp", ("ctx", "tensor"), None),
-            P("dp", ("ctx", "tensor"), None),
-            P(),
-            P(),
-            P("dp", "tensor"),
-            P("dp", "tensor"),
-            P("dp", "tensor"),
-            P(),
-            P(),
-            P("tensor", "dp"),
-            P(),
-            P(),
-            P(),
-            P("dp", "tensor"),
-            P(),
-            P("tensor", "dp"),
-            P(),
-        ),
-        check_vma=False,
-    )
+        body if lined_up else general_body, mesh=mesh, in_specs=SPECS, out_specs=OUT_SPECS, check_vma=False
+    )

time: 864 us -> 646 us (0.75)
  blocking collectives: 263 us -> 39.7 us
  Pallas kernels: 0 us -> 109 us
  matrix products: 101 us -> 59.4 us
  waiting for transfers between devices: 372 us -> 337 us
  other arithmetic: 62.3 us -> 28.6 us
    all_gather x16 -> x0, blocking collectives: 222 us -> none  [the longest x8 168 us: tensor_rows(): return lax.all_gather(block, 'tensor', axis=0, tiled=True)]
    reduce_scatter x14 -> x5, waiting for transfers between devices: 268 us -> 76.2 us  [the longest x1 43.3 us: body(): lax.psum_scatter(grad_w_out.astype(BF).reshape(4, 4, 192, 768), 'tensor',...]
    unnamed x13 -> x16, waiting for transfers between devices: 93.9 us -> 261 us
    pallas_call x0 -> x1, Pallas kernels: none -> 109 us  [forward_call(): pl.pallas_call(forward_kernel, out_shape=(struct((2, 4, 128, 768), BF), s...]
    dot_general x48 -> x14, matrix products: 101 us -> 51 us  [the longest x1 6.8 us: body(): jnp.einsum('rd,tdu->rtu', nf, w_in, preferred_element_type=F32)]
    while x213 -> x0, local copies, waits for them, and re-layouts: 17.7 us -> none
    slice x0 -> x9, local copies, waits for them, and re-layouts: none -> 17.3 us  [the longest x1 6.79 us: body(): w_out = weights[1].reshape(4, 768, 768)]
    convert_element_type x23 -> x4, other arithmetic: 22.6 us -> 8.05 us  [the longest x1 6.14 us: body(): grad_scores = (probs * (grad_probs - centre)).astype(BF)]
  transfers between devices with their start and end apart: 21 -> 12, of which waited for: 15 -> 7; matrix products, arithmetic and copies ran while one was open for 12% -> 11% of each run, Pallas kernels for 0% -> 0%
where the time goes in v1:
time: 646 us; the launch traced here: 644 us
  waiting for transfers between devices  337 us (52%)
  Pallas kernels  109 us (17%)
  matrix products  59.4 us (9%)
  local copies, waits for them, and re-layouts  48.5 us (8%)
  blocking collectives  39.7 us (6%)
  other arithmetic  28.6 us (4%)
  between operations  16.2 us (3%)
    unnamed x16, waiting for transfers between devices  261 us
    pallas_call x1, Pallas kernels, forward_call(): pl.pallas_call(forward_kernel, out_shape=(struct((2, 4, 128, 768), BF), s...  109 us
    reduce_scatter x1, waiting for transfers between devices, body(): lax.psum_scatter(grad_w_out.astype(BF).reshape(4, 4, 192, 768), 'tensor',...  43.3 us
    psum x1, blocking collectives, body(): lax.psum(jnp.concatenate([grad_attn_g, grad_attn_s, place_piece(sums[:par...  39.7 us
    reduce_scatter x1, waiting for transfers between devices, body(): lax.psum_scatter(grad_na.astype(BF).reshape(2, 512, 768), 'tensor', scatt...  32.8 us
  transfers between devices with their start and end apart: 12, of which 7 were waited for; matrix products, arithmetic and copies ran while one was open for 11% of the time, Pallas kernels for 0%

profile of v1, /device:TPU:0, one launch (start us, length us, event | category | flops | bytes accessed | tf_op | source)
XLA Modules:
  0.0 644.0 jit_solution(7429712722114953056)
XLA Ops:
  27.8 109.5 %forward.1 = (bf16[2,4,128,768]{3,2,1,0:T(8,128)(2,1)}, bf16[2,512,256]{2,1,0:T(8,128)(2,1)}, bf16[2,2,4,128,512]{4,3,2,1,0:T(8,128)(2,1)}, bf16[4,2,128,256]{3,...) custom-call(f32[2,128,768]{2,1,0:T(8,128)} %hidden.1, ...), custom_call_target="tpu_custom_call" | custom-call | tf_op jit(solution)/shard_map/forward/pallas_call | solution.py:372
  139.9 6.8 %fusion.47 = (bf16[1,4,4,192,768]{4,3,2,1,0:T(8,128)(2,1)S(1)}, bf16[1,4,4,192,768]{4,3,2,1,0:T(8,128)(2,1)}) fusion(bf16[2,4,4,192,768]{4,3,2,1,0:T(8,128)(2,1)} %get-tuple-element.28), kind=kLoop, calls=%fused_computation.113 | loop fusion | bytes 18874368 | tf_op jit(solution)/shard_map/slice | solution.py:457
  146.7 6.8 %multiply_convert_fusion.1 = (bf16[256,4,768]{2,0,1:T(8,128)(2,1)}, f32[256,4,768]{2,0,1:T(8,128)S(1)}) fusion(f32[4,768]{1,0:T(4,128)S(1)} %add.115, bf16[256,768,1]{1,0,2:T(8,128)(2,1)S(1)} %bitcast.173, bf16[4,768,768]{2,1,0:T(8,128)(2,1)} %bitcast.153), kind=kOutput, calls=%fused_computation.25 | convolution fusion | flops 1212678144 | bytes 9842688 | tf_op jit(solution)/shard_map/rd,tdu->rtu/dot_general | solution.py:464
  153.5 2.8 convert_reduce_fusion
  160.8 4.4 all-to-all-start
  167.0 2.7 fusion.48
  177.4 8.5 %fusion.52 = (f32[2,3,512]{2,1,0:T(4,128)S(1)}, f32[2,3,512,1024]{3,2,1,0:T(8,128)}) fusion(pred[2,512,1024]{2,1,0:T(8,128)(4,1)} %broadcast_compare_fusion, bf16[2,512,3,64]{1,3,2,0:T(8,128)(2,1)S(1)} %bitcast.159, bf16[2,1024,3,64]{1,3,2,0:T(8,128)(2,1)S(1)} %reshape.175), kind=kOutput, calls=%fused_computation.118 | convolution fusion | flops 412091392 | bytes 14823424 | tf_op jit(solution)/shard_map/sub | solution.py:494
  187.8 6.0 fusion.22
  195.3 6.2 multiply_reduce_fusion
  201.5 6.1 multiply_convert_fusion
  214.3 3.7 convolution_convert_fusion.1
  219.8 3.6 convolution_convert_fusion
  224.5 4.8 fusion.27
  231.6 2.7 convolution_convert_fusion.2
  234.9 140.6 %all-reduce.18.cloned.1.call-done = bf16[4,4,192,256]{3,2,0,1:T(8,128)(2,1)} async-done(((bf16[4,4,192,256]{3,2,0,1:T(8,128)(2,1)}), bf16[4,4,192,256]{3,2,0,1:T(8,128)(2,1)}) %all-reduce.18.cloned.1.call-update) | async-done | bytes 1572880
  378.0 4.4 convolution_convert_fusion.3
  383.4 43.3 %reduce-scatter.35.cloned.1.call-done = bf16[1,4,192,768]{3,2,1,0:T(8,128)(2,1)} async-done(((bf16[4,4,192,768]{3,2,1,0:T(8,128)(2,1)}), bf16[1,4,192,768]{3,2,1,0:T(8,128)(2,1)}) %reduce-scatter.35.cloned.1.call-update) | async-done | bytes 1179664 | tf_op jit(solution)/shard_map/reduce_scatter | solution.py:524
  427.0 5.1 fusion.26
  432.3 32.8 %reduce-scatter.31.cloned.1.call-done = bf16[2,128,768]{2,1,0:T(8,128)(2,1)} async-done(((bf16[2,512,768]{2,1,0:T(8,128)(2,1)}), bf16[2,128,768]{2,1,0:T(8,128)(2,1)}) %reduce-scatter.31.cloned.1.call-update) | async-done | bytes 393232 | tf_op jit(solution)/shard_map/reduce_scatter | solution.py:514
  466.7 25.2 %reduce-scatter.39.cloned.1.call-done = bf16[1,1,192,256]{3,2,0,1:T(8,128)(2,1)} async-done(((bf16[1,4,192,256]{3,2,0,1:T(8,128)(2,1)}), bf16[1,1,192,256]{3,2,0,1:T(8,128)(2,1)}) %reduce-scatter.39.cloned.1.call-update) | async-done | bytes 98320
  491.8 31.5 %reduce-scatter.37.cloned.1.call-done = bf16[1,192,768]{2,1,0:T(8,128)(2,1)} async-done(((bf16[4,192,768]{2,1,0:T(8,128)(2,1)}), bf16[1,192,768]{2,1,0:T(8,128)(2,1)}) %reduce-scatter.37.cloned.1.call-update) | async-done | bytes 294928
  523.3 31.5 %reduce-scatter.41.cloned.1.call-done = bf16[1,1,192,768]{3,2,1,0:T(8,128)(2,1)} async-done(((bf16[1,4,192,768]{3,2,1,0:T(8,128)(2,1)}), bf16[1,1,192,768]{3,2,1,0:T(8,128)(2,1)}) %reduce-scatter.41.cloned.1.call-update) | async-done | bytes 294928
  554.8 31.5 %reduce-scatter.43.cloned.1.call-done = bf16[1,1,192,768]{3,2,1,0:T(8,128)(2,1)} async-done(((bf16[1,4,192,768]{3,2,1,0:T(8,128)(2,1)}), bf16[1,1,192,768]{3,2,1,0:T(8,128)(2,1)}) %reduce-scatter.43.cloned.1.call-update) | async-done | bytes 294928
  586.3 39.7 %psum.35 = f32[9216]{0:T(1024)S(1)} all-reduce(f32[9216]{0:T(1024)S(1)} %constant_dynamic-update-slice_fusion), channel_id=1, replica_groups=mesh['dp'=4,'ctx'=2,'tensor'=4] {'dp','ctx','tensor'}, use_global_device_ids=true, to_apply=%region_22.23 | all-reduce | flops 9216 | bytes 73728 | tf_op jit(solution)/shard_map/psum | solution.py:538
  (167 shorter events, 67.8 us)
Async XLA Ops:
  8.0 18.2 %copy-start.16 = (f32[768,192]{0,1:T(8,128)S(1)}, f32[768,192]{0,1:T(8,128)}, u32[]{:S(2)}) copy-start(f32[768,192]{0,1:T(8,128)} %param.34) | copy-start | bytes 1769476
  8.0 18.2 %copy-start.15 = (f32[192,768]{1,0:T(8,128)S(1)}, f32[192,768]{1,0:T(8,128)}, u32[]{:S(2)}) copy-start(f32[192,768]{1,0:T(8,128)} %param.32) | copy-start | bytes 1769476
  24.7 128.7 %copy-start.9 = (bf16[2,128,768]{2,1,0:T(8,128)(2,1)}, bf16[2,128,768]{2,1,0:T(8,128)(2,1)S(1)}, u32[]{:S(2)}) copy-start(bf16[2,128,768]{2,1,0:T(8,128)(2,1)S(1)} %get-tuple-element.90) | copy-start | bytes 1179652
  139.9 6.8 %copy-start.18 = (bf16[2,128,768]{2,1,0:T(8,128)(2,1)S(1)}, bf16[2,128,768]{2,1,0:T(8,128)(2,1)}, u32[]{:S(2)}) copy-start(bf16[2,128,768]{2,1,0:T(8,128)(2,1)} %get-tuple-element.27) | copy-start | bytes 1179652
  146.7 6.8 %copy-start.3 = (bf16[1,4,4,192,768]{4,3,2,1,0:T(8,128)(2,1)}, bf16[1,4,4,192,768]{4,3,2,1,0:T(8,128)(2,1)S(1)}, u32[]{:S(2)}) copy-start(bf16[1,4,4,192,768]{4,3,2,1,0:T(8,128)(2,1)S(1)} %get-tuple-element.85) | copy-start | bytes 14155780
  146.7 9.7 %slice-start = ((s8[4718592]{0:T(1024)(128)(4,1)}), s8[4194304]{0:T(1024)(128)(4,1)S(1)}, s32[]{:S(2)}) async-start(s8[4718592]{0:T(1024)(128)(4,1)} %bitcast.154), calls=%async_computation.21 | async-start | bytes 8388608
  158.4 8.5 %copy-start.17 = (bf16[2,512,256]{2,1,0:T(8,128)(2,1)S(1)}, bf16[2,512,256]{2,1,0:T(8,128)(2,1)}, u32[]{:S(2)}) copy-start(bf16[2,512,256]{2,1,0:T(8,128)(2,1)} %get-tuple-element.30) | copy-start | bytes 1572868
  160.8 25.0 %all-to-all-start = ((bf16[4,2,128,256]{3,2,1,0:T(8,128)(2,1)}), bf16[4,2,128,256]{3,2,1,0:T(8,128)(2,1)}, u32[]{:S(2)}, u32[]{:S(2)}) async-start(bf16[4,2,128,256]{3,2,1,0:T(8,128)(2,1)} %bitcast.24), calls=%async_computation | async-start | bytes 1048576 | tf_op jit(solution)/shard_map/all_to_all | solution.py:485
  165.2 64.4 %reduce-scatter.29.cloned.1.call-start = ((), (), s32[]{:S(2)}) async-start(), calls=%async_computation.11 | async-start | bytes 1572864 | tf_op jit(solution)/shard_map/reduce_scatter | solution.py:505
  177.4 8.5 %copy-start.4 = (bf16[2,1024,3,64]{1,3,2,0:T(8,128)(2,1)}, bf16[2,1024,3,64]{1,3,2,0:T(8,128)(2,1)S(1)}, u32[]{:S(2)}) copy-start(bf16[2,1024,3,64]{1,3,2,0:T(8,128)(2,1)S(1)} %reshape.175) | copy-start | bytes 2359300
  195.2 34.4 %reduce-scatter.27.cloned.1.call-start = ((), (), s32[]{:S(2)}) async-start(), calls=%async_computation.10 | async-start | bytes 1572864 | tf_op jit(solution)/shard_map/reduce_scatter | solution.py:502
  211.6 163.9 %all-reduce.18.cloned.1.call-start = ((), (), s32[]{:S(2)}) async-start(), calls=%async_computation.15 | async-start | bytes 3145728
  213.6 168.9 %reduce-scatter.33.cloned.1.call-start = ((), (), s32[]{:S(2)}) async-start(), calls=%async_computation.13 | async-start | bytes 5898240 | tf_op jit(solution)/shard_map/reduce_scatter | solution.py:520
  218.0 208.7 %reduce-scatter.35.cloned.1.call-start = ((), (), s32[]{:S(2)}) async-start(), calls=%async_computation.14 | async-start | bytes 5898240 | tf_op jit(solution)/shard_map/reduce_scatter | solution.py:524
  223.4 241.8 %reduce-scatter.31.cloned.1.call-start = ((), (), s32[]{:S(2)}) async-start(), calls=%async_computation.12 | async-start | bytes 1966080 | tf_op jit(solution)/shard_map/reduce_scatter | solution.py:514
  234.3 257.6 %reduce-scatter.39.cloned.1.call-start = ((), (), s32[]{:S(2)}) async-start(), calls=%async_computation.17 | async-start | bytes 491520
  377.9 145.4 %reduce-scatter.37.cloned.1.call-start = ((), (), s32[]{:S(2)}) async-start(), calls=%async_computation.16 | async-start | bytes 1474560
  378.0 5.2 copy-start.1
  382.4 44.6 %copy-start.22 = (f32[4,768]{1,0:T(4,128)S(1)}, f32[4,768]{1,0:T(4,128)}, u32[]{:S(2)}) copy-start(f32[4,768]{1,0:T(4,128)} %get-tuple-element.109) | copy-start | bytes 36868
  382.4 44.6 %copy-start.24 = (f32[768]{0:T(1024)S(1)}, f32[768]{0:T(1024)}, u32[]{:S(2)}) copy-start(f32[768]{0:T(1024)} %param.35) | copy-start | bytes 9220
  382.4 172.4 %reduce-scatter.41.cloned.1.call-start = ((), (), s32[]{:S(2)}) async-start(), calls=%async_computation.18 | async-start | bytes 1474560
  383.2 203.1 %reduce-scatter.43.cloned.1.call-start = ((), (), s32[]{:S(2)}) async-start(), calls=%async_computation.19 | async-start | bytes 1474560
  426.7 202.7 %all-reduce.20.cloned.1.call-start = ((), (), s32[]{:S(2)}) async-start(), calls=%async_computation.20 | async-start | bytes 1966080 | tf_op jit(solution)/shard_map/psum | solution.py:535
  427.0 38.2 %copy-start.20 = (f32[768]{0:T(1024)S(1)}, f32[768]{0:T(1024)}, u32[]{:S(2)}) copy-start(f32[768]{0:T(1024)} %param.21) | copy-start | bytes 9220
  (16 other events, 32.9 us)
Sparse Core Ops, SparseCore 0:
  195.3 9.4 reduce-scatter.28
  211.8 9.6 reduce-scatter.26
  223.7 102.0 reduce-scatter.32
  328.0 98.6 reduce-scatter.34
  428.8 36.3 reduce-scatter.30
  468.4 23.3 reduce-scatter.38
  494.7 28.5 reduce-scatter.36
  526.2 28.5 reduce-scatter.40
  557.7 28.5 reduce-scatter.42
  588.7 19.5 all-reduce.19
Sparse Core Ops, SparseCore 1:
  214.5 161.0 all-reduce.17

commit v2 on v1

--- a/solution.py
+++ b/solution.py
@@ -173,7 +173,7 @@
     lane_head = lax.broadcasted_iota(jnp.int32, (1, LANES), 1) // HDIM
 
     def attend(s):
-        keys_seg = seg_k[s]
+        keys_seg = jnp.broadcast_to(seg_k[s], (128, 1024)).T[:, :1]
         for b in range(2):
             hide[:, b * 256 : (b + 1) * 256] = jnp.where(
                 keys_seg == seg_q[s, :, b * 256 : (b + 1) * 256], 0.0, HIDE
@@ -360,6 +360,431 @@
         return carry
 
     lax.fori_loop(0, 16, finish, 0)
+
+
+def erf_parts(values):
+    cdf = 0.5 * (1.0 + lax.erf(values * ROOT_HALF))
+    return cdf, cdf + values * (jnp.exp(-0.5 * values * values) * INV_ROOT_TWO_PI)
+
+
+def backward_kernel(
+    hidden, cot, middle, normed_f, normed, queries, kv, mixed_in, wqkv, wout, weights, seg_k, seg_q,
+    gain_a, gain_f, inner_bias, outer_bias,
+    block_out, grad_input, g_ff, g_wo, g_qkv, small,
+    ff, left, right, left_turn, grad_mid, branch, mixed_sib, g_mix_out, g_mix, part, rx1, rx2, rz,
+    hide, k_turn, q_turn, acc_k, acc_v, kv_out, kv_in, dqkv, gna, rzn, normed_turn, qkv_sib,
+    qkv_in, wide, sums, sums_core, sums_plane, sums_line, gb_turn,
+    ff_sem, l_send, l_recv, r_send, r_recv, b_send, b_recv, x_send, x_recv, m_send, m_recv,
+    p1_send, p1_recv, p2_send, p2_recv, z_send, z_recv, kv_send, kv_recv, n_send, n_recv,
+    qs_send, qs_recv, qp_send, qp_recv, f_send, f_recv, s_send, s_recv,
+):
+    at = Place()
+    d, c, t = at.d, at.c, at.t
+    other = 1 - c
+
+    def load(which, i):
+        return pltpu.make_async_copy(weights.at[which, i], ff.at[i % 2, which], ff_sem.at[which, i])
+
+    for i in range(2):
+        load(0, i).start()
+        load(1, i).start()
+    greet(at)
+
+    left[0, c] = normed_f[...].reshape(256, 768)
+    left[1, c] = cot[...].reshape(256, 768).astype(BF)
+    left_copy = remote(left.at[other, c], left.at[other, c], l_send.at[0], l_recv.at[0], ctx=other)
+    left_copy.start()
+    mixed_copy = remote(mixed_in, mixed_sib, x_send.at[0], x_recv.at[0], ctx=other)
+    mixed_copy.start()
+    sums[...] = jnp.zeros_like(sums)
+
+    def right_copy(i):
+        return remote(
+            right.at[other, i, c], right.at[other, i, c], r_send.at[i], r_recv.at[i], ctx=other
+        )
+
+    def right_wait(i):
+        return remote(right.at[c, i, other], right.at[c, i, other], r_send.at[i], r_recv.at[i], ctx=other)
+
+    wide[...] = jnp.zeros_like(wide)
+
+    def units(i, carry):
+        slot = i % 2
+        load(0, i).wait()
+        load(1, i).wait()
+        total = jnp.zeros((1, 768), F32)
+        for half in range(2):
+            rows = slice(half * 128, half * 128 + 128)
+            inner = (
+                jnp.dot(left[0, c, rows, :], ff[slot, 0], preferred_element_type=F32) + inner_bias[i]
+            )
+            cdf, slope = erf_parts(inner)
+            active = (inner * cdf).astype(BF)
+            right[1, i, c, rows, :] = active
+            wide[rows, :] += dims(active, ff[slot, 1], 1, 1)
+            grad_inner = (
+                jnp.dot(left[1, c, rows, :], ff[slot, 1], preferred_element_type=F32) * slope
+            ).astype(BF)
+            right[0, i, c, rows, :] = grad_inner
+            wide[256 + half * 128 : 384 + half * 128, :] += dims(grad_inner, ff[slot, 0], 1, 1)
+            total = total + jnp.sum(grad_inner.astype(F32), axis=0, keepdims=True)
+        sums[pl.ds(6 + i, 1), :] = total
+        right_copy(i).start()
+
+        @pl.when(i < 2)
+        def _():
+            load(0, i + 2).start()
+            load(1, i + 2).start()
+
+        return carry
+
+    lax.fori_loop(0, 4, units, 0)
+
+    def add_row(i, value):
+        sums[i : i + 1, :] += jnp.sum(value, axis=0, keepdims=True)
+
+    def norm_back(s, rows, source, grad_out, gain):
+        scaled, inverse = norm_parts(source[s, rows, :])
+        grad_scaled = grad_out * gain[...]
+        plain = jnp.mean(grad_scaled, axis=-1, keepdims=True)
+        cross = jnp.mean(grad_scaled * scaled, axis=-1, keepdims=True)
+        return inverse * (grad_scaled - plain - scaled * cross), scaled
+
+    for s in range(2):
+        for half in range(2):
+            rows = slice(half * 64, half * 64 + 64)
+            flat = slice(s * 128 + half * 64, s * 128 + half * 64 + 64)
+            block_out[s, rows, :] = middle[s, rows, :] + wide[flat, :] + outer_bias[...]
+            grad_out = wide[256 + s * 128 + half * 64 : 320 + s * 128 + half * 64, :]
+            grad_rows, scaled = norm_back(s, rows, middle, grad_out, gain_f)
+            grad_rows = grad_rows + cot[s, rows, :]
+            grad_mid[s, rows, :] = grad_rows
+            branch[c, flat, :] = grad_rows.astype(BF)
+            add_row(2, grad_out * scaled)
+            add_row(3, grad_out)
+            add_row(4, grad_rows)
+            add_row(5, cot[s, rows, :])
+    branch_copy = remote(branch.at[c], branch.at[c], b_send.at[0], b_recv.at[0], ctx=other)
+    branch_copy.start()
+
+    def m_copy(s, k, dest):
+        return remote(g_mix_out.at[dest, s], g_mix.at[s, t], m_send.at[s, k], m_recv.at[s, t], tensor=dest)
+
+    for p in range(4):
+        g_mix_out[p] = jnp.dot(branch[c], wout[p], preferred_element_type=F32).astype(BF).reshape(
+            2, 128, LANES
+        )
+    for s in range(2):
+        for k in range(3):
+            m_copy(s, k, (t + k + 1) % 4).start()
+        g_mix[s, t] = g_mix_out[t, s]
+
+    left_copy.wait_send()
+    remote(left.at[c, other], left.at[c, other], l_send.at[0], l_recv.at[0], ctx=other).wait_recv()
+    left_turn[...] = left[c].reshape(512, 768).T
+    remote(branch.at[other], branch.at[other], b_send.at[0], b_recv.at[0], ctx=other).wait_recv()
+    gb_turn[...] = branch[...].reshape(512, 768).T
+    mixed_copy.wait_recv()
+
+    def first(i):
+        near, far = (at.dx, at.dy) if i < 2 else (at.dy, at.dx)
+        return [
+            remote(part.at[i, owner], rx1.at[i, j], p1_send.at[i, j], p1_recv.at[i, j], dp=near)
+            for j, owner in enumerate((near, at.dd))
+        ]
+
+    def second(i):
+        far = at.dy if i < 2 else at.dx
+        return remote(part.at[i, far], rx2.at[i], p2_send.at[i], p2_recv.at[i], dp=far)
+
+    for i in range(4):
+        right_wait(i).wait_recv()
+        both = right[c, i].reshape(512, 768)
+
+        def rows_of(q, carry):
+            start = pl.multiple_of(q * 192, 192)
+            out = jnp.dot(left_turn[pl.ds(start, 192), :], both, preferred_element_type=F32)
+            part[i, q, 0:192, :] = out.astype(BF)
+            start = pl.multiple_of(q * 192 + c * 96, 96)
+            turned = gb_turn[pl.ds(start, 96), :]
+            here, there = turned[:, :256], turned[:, 256:]
+            mine = mixed_in[i].reshape(256, LANES)
+            sib = mixed_sib[i].reshape(256, LANES)
+            low = jnp.where(c == 0, mine.astype(F32), sib.astype(F32)).astype(BF)
+            high = jnp.where(c == 0, sib.astype(F32), mine.astype(F32)).astype(BF)
+            out = jnp.dot(here, low, preferred_element_type=F32) + jnp.dot(
+                there, high, preferred_element_type=F32
+            )
+            for j in range(3):
+                part[i, q, 192:224, j * LANES : (j + 1) * LANES] = out[j * 32 : (j + 1) * 32, :].astype(BF)
+            return carry
+
+        lax.fori_loop(0, 4, rows_of, 0)
+        for copy in first(i):
+            copy.start()
+
+    def add_block(ref, index, *others):
+        def rows(q, carry):
+            block = pl.ds(pl.multiple_of(q * 32, 32), 32)
+            total = ref[index + (block, slice(None))].astype(F32)
+            for o in others:
+                total = total + o[block, :].astype(F32)
+            ref[index + (block, slice(None))] = total.astype(BF)
+            return carry
+
+        lax.fori_loop(0, 7, rows, 0)
+
+    def to_second(i):
+        for copy in first(i):
+            copy.wait_recv()
+        far = at.dy if i < 2 else at.dx
+        add_block(part, (i, far), rx1.at[i, 1])
+        second(i).start()
+        add_block(part, (i, d), rx1.at[i, 0])
+
+    lane_head = lax.broadcasted_iota(jnp.int32, (1, LANES), 1) // HDIM
+
+    def attend(s):
+        keys_seg = jnp.broadcast_to(seg_k[s], (128, 1024)).T[:, :1]
+        for b in range(2):
+            hide[:, b * 256 : (b + 1) * 256] = jnp.where(
+                keys_seg == seg_q[s, :, b * 256 : (b + 1) * 256], 0.0, HIDE
+            ).astype(F32)
+        k_turn[...] = kv[s].reshape(1024, 2 * LANES)[:, :LANES].T
+        q_turn[192:, :] = jnp.zeros((64, 512), F32)
+        acc_k[...] = jnp.zeros_like(acc_k)
+        acc_v[...] = jnp.zeros_like(acc_v)
+
+        def step(i, carry):
+            h, b = i // 2, i % 2
+            block = pl.ds(pl.multiple_of(b * 256, 256), 256)
+            head = lane_head == h
+            q_here = jnp.where(head, queries[s, block, :].astype(F32), 0.0).astype(BF)
+            g_here = g_mix[s, pl.ds(b * 2, 2)].reshape(256, LANES)
+            g_here = jnp.where(head, g_here.astype(F32), 0.0).astype(BF)
+            both = kv[s].reshape(1024, 2 * LANES)
+            scores = dims(both[:, :LANES], q_here, 1, 1) + hide[:, block]
+            peak = jnp.max(scores, axis=0, keepdims=True)
+            expo = jnp.exp(scores - peak)
+            probs = expo * (1.0 / jnp.sum(expo, axis=0, keepdims=True))
+            grad_probs = dims(both[:, LANES:], g_here, 1, 1)
+            centre = jnp.sum(probs * grad_probs, axis=0, keepdims=True)
+            acc_v[...] += jnp.dot(probs.astype(BF), g_here, preferred_element_type=F32)
+            grad_scores = (probs * (grad_probs - centre)).astype(BF)
+            acc_k[...] += jnp.dot(grad_scores, q_here, preferred_element_type=F32)
+            rows = pl.ds(pl.multiple_of(h * HDIM, HDIM), HDIM)
+            q_turn[rows, block] = jnp.dot(k_turn[rows, :], grad_scores, preferred_element_type=F32)
+            return carry
+
+        lax.fori_loop(0, 6, step, 0)
+        dqkv[s, :, :LANES] = (q_turn[...].T * HDIM**-0.5).astype(BF)
+        theirs = pl.ds(pl.multiple_of(other * 512, 512), 512)
+        kv_out[s, :, :LANES] = acc_k[theirs, :].astype(BF)
+        kv_out[s, :, LANES:] = acc_v[theirs, :].astype(BF)
+        kv_copy(s).start()
+        ours = pl.ds(pl.multiple_of(c * 512, 512), 512)
+        dqkv[s, :, LANES : 2 * LANES] = acc_k[ours, :].astype(BF)
+        dqkv[s, :, 2 * LANES :] = acc_v[ours, :].astype(BF)
+
+    def kv_copy(s):
+        return remote(kv_out.at[s], kv_in.at[s], kv_send.at[s], kv_recv.at[s], ctx=other)
+
+    def line_sum(source, landing, send, recv):
+        slot = 2 - at.mid
+        return dict(
+            near=lambda: remote(source(at.order(0)), landing(0), send(0), recv(0), tensor=at.order(0)),
+            next=lambda: remote(source(at.order(1)), landing(slot), send(1), recv(slot), tensor=at.order(1)),
+            far=lambda: remote(source(at.order(2)), landing(3), send(2), recv(3), tensor=at.order(0)),
+            on=lambda: remote(source(at.order(2)), landing(1), send(2), recv(1), tensor=at.order(2)),
+            got=lambda k: remote(landing(k), landing(k), send(0), recv(k), tensor=t),
+        )
+
+    def line_start(line):
+        line["near"]().start()
+        line["next"]().start()
+
+        @pl.when(at.mid == 0)
+        def _():
+            line["far"]().start()
+
+    def line_pass(line, add):
+        @pl.when(at.mid == 1)
+        def _():
+            line["got"](3).wait_recv()
+            add()
+            line["on"]().start()
+
+    def line_got(line):
+        line["got"](0).wait_recv()
+        line["got"](1).wait_recv()
+
+        @pl.when(at.mid == 1)
+        def _():
+            line["got"](2).wait_recv()
+
+    def line_end(line):
+        line["near"]().wait_send()
+        line["next"]().wait_send()
+
+        @pl.when(at.mid == 0)
+        def _():
+            line["far"]().wait_send()
+
+        @pl.when(at.mid == 1)
+        def _():
+            line["on"]().wait_send()
+
+    rows_line = [
+        line_sum(
+            lambda p, s=s: gna.at[s, p], lambda k, s=s: rzn.at[s, k],
+            lambda k, s=s: n_send.at[s, k], lambda k, s=s: n_recv.at[s, k],
+        )
+        for s in range(2)
+    ]
+    cargo_line = line_sum(
+        lambda p: part.at[p, d], lambda k: rz.at[k], lambda k: z_send.at[k], lambda k: z_recv.at[k]
+    )
+
+    for s in range(2):
+        for k in range(3):
+            p = (t + k + 1) % 4
+            remote(g_mix_out.at[p, s], g_mix.at[s, p], m_send.at[s, k], m_recv.at[s, p], tensor=p).wait_recv()
+        attend(s)
+        to_second(2 * s)
+
+    for s in range(2):
+        kv_copy(s).wait_recv()
+        dqkv[s, :, LANES:] = (dqkv[s, :, LANES:].astype(F32) + kv_in[s].astype(F32)).astype(BF)
+        for p in range(4):
+            rows = dqkv[s, p * 128 : (p + 1) * 128, :]
+            gna[s, p] = dims(rows, wqkv[...].reshape(768, 768), 1, 1).astype(BF)
+            sums[pl.ds(12 + t, 1), :] += jnp.sum(rows.astype(F32), axis=0, keepdims=True)
+        line_start(rows_line[s])
+
+    to_second(1)
+    to_second(3)
+
+    normed_turn[...] = normed[...].reshape(1024, 768).T
+
+    def qkv_rows(q, carry):
+        start = pl.multiple_of(q * 96, 96)
+        out = jnp.dot(
+            normed_turn[pl.ds(start, 96), :], dqkv[...].reshape(1024, 768), preferred_element_type=F32
+        )
+        wide[pl.ds(start, 96), :] = out
+        return carry
+
+    lax.fori_loop(0, 8, qkv_rows, 0)
+    for p in range(4):
+        theirs = pl.ds(pl.multiple_of(p * 192 + other * 96, 96), 96)
+        qkv_sib[0, p] = wide[theirs, :].astype(BF)
+    sib_copy = remote(qkv_sib.at[0], qkv_sib.at[1], qs_send.at[0], qs_recv.at[0], ctx=other)
+    sib_copy.start()
+
+    for i in range(4):
+        remote(rx2.at[i], rx2.at[i], p2_send.at[i], p2_recv.at[i], dp=d).wait_recv()
+        add_block(part, (i, d), rx2.at[i])
+    line_start(cargo_line)
+
+    sib_copy.wait_recv()
+    for p in range(4):
+        ours = pl.ds(pl.multiple_of(p * 192 + c * 96, 96), 96)
+        qkv_in[0, p] = (wide[ours, :] + qkv_sib[1, p].astype(F32)).astype(BF)
+    planes = (at.dx, at.dy, at.dd)
+
+    def plane_copy(k):
+        return remote(qkv_in.at[0, planes[k]], qkv_in.at[1, d], qp_send.at[k], qp_recv.at[d], dp=planes[k])
+
+    for k in range(3):
+        plane_copy(k).start()
+    qkv_in[1, d] = qkv_in[0, d]
+
+    for s in range(2):
+        def add_rows(s=s):
+            gna[s, at.order(2)] = (gna[s, at.order(2)].astype(F32) + rzn[s, 3].astype(F32)).astype(BF)
+
+        line_pass(rows_line[s], add_rows)
+    line_pass(cargo_line, lambda: add_block(part, (at.order(2), d), rz.at[3]))
+
+    for k in range(3):
+        remote(qkv_in.at[0, planes[k]], qkv_in.at[1, planes[k]], qp_send.at[k], qp_recv.at[planes[k]], dp=d).wait_recv()
+    total = qkv_in[1, 0].astype(F32)
+    for p in range(1, 4):
+        total = total + qkv_in[1, p].astype(F32)
+    g_qkv[c] = total
+    final = [remote(g_qkv.at[c], g_qkv.at[c], f_send.at[0], f_recv.at[0], ctx=other)]
+    final[0].start()
+
+    for s in range(2):
+        line_got(rows_line[s])
+        for half in range(2):
+            rows = slice(half * 64, half * 64 + 64)
+            grad_out = gna[s, t, rows, :].astype(F32) + rzn[s, 0, rows, :].astype(F32)
+            grad_out = grad_out + rzn[s, 1, rows, :].astype(F32)
+            third = rzn[s, 2, rows, :].astype(F32)
+            grad_out = grad_out + jnp.where(at.mid == 1, third, jnp.zeros_like(third))
+            grad_rows, scaled = norm_back(s, rows, hidden, grad_out, gain_a)
+            grad_input[s, rows, :] = grad_mid[s, rows, :] + grad_rows
+            add_row(0, grad_out * scaled)
+            add_row(1, grad_out)
+
+    core_sum = remote(sums, sums_core, s_send.at[0], s_recv.at[0], ctx=other)
+    core_sum.start()
+
+    line_got(cargo_line)
+    for q in range(7):
+        rows = slice(q * 32, q * 32 + 32)
+        total = part[t, d, rows, :].astype(F32) + rz[0, rows, :].astype(F32) + rz[1, rows, :].astype(F32)
+        third = rz[2, rows, :].astype(F32)
+        total = total + jnp.where(at.mid == 1, third, jnp.zeros_like(third))
+        if q < 6:
+            g_ff[c, rows, :] = total
+        else:
+            g_wo[c] = total
+    final.append(remote(g_ff.at[c], g_ff.at[c], f_send.at[1], f_recv.at[1], ctx=other))
+    final.append(remote(g_wo.at[c], g_wo.at[c], f_send.at[2], f_recv.at[2], ctx=other))
+    final[1].start()
+    final[2].start()
+
+    core_sum.wait()
+    sums_plane[d] = sums[...] + sums_core[...]
+    for k in range(3):
+        remote(sums_plane.at[d], sums_plane.at[d], s_send.at[1 + k], s_recv.at[1 + d], dp=planes[k]).start()
+    for k in range(3):
+        remote(
+            sums_plane.at[planes[k]], sums_plane.at[planes[k]], s_send.at[1 + k], s_recv.at[1 + planes[k]], dp=d
+        ).wait_recv()
+    sums_line[t] = (sums_plane[0] + sums_plane[1]) + (sums_plane[2] + sums_plane[3])
+    for k in range(3):
+        p = (t + k + 1) % 4
+        remote(sums_line.at[t], sums_line.at[t], s_send.at[4 + k], s_recv.at[5 + t], tensor=p).start()
+    for k in range(3):
+        p = (t + k + 1) % 4
+        remote(sums_line.at[p], sums_line.at[p], s_send.at[4 + k], s_recv.at[5 + p], tensor=p).wait_recv()
+    small[...] = (sums_line[0] + sums_line[1]) + (sums_line[2] + sums_line[3])
+
+    for k in range(3):
+        remote(sums_plane.at[d], sums_plane.at[d], s_send.at[1 + k], s_recv.at[1 + d], dp=planes[k]).wait_send()
+        p = (t + k + 1) % 4
+        remote(sums_line.at[t], sums_line.at[t], s_send.at[4 + k], s_recv.at[5 + t], tensor=p).wait_send()
+        plane_copy(k).wait_send()
+    for i, ref in enumerate((g_qkv, g_ff, g_wo)):
+        final[i].wait_send()
+        remote(ref.at[other], ref.at[other], f_send.at[i], f_recv.at[i], ctx=other).wait_recv()
+    sib_copy.wait_send()
+    mixed_copy.wait_send()
+    branch_copy.wait_send()
+    for s in range(2):
+        line_end(rows_line[s])
+        kv_copy(s).wait_send()
+        for k in range(3):
+            m_copy(s, k, (t + k + 1) % 4).wait_send()
+    line_end(cargo_line)
+    for i in range(4):
+        right_copy(i).wait_send()
+        for copy in first(i):
+            copy.wait_send()
+        second(i).wait_send()
 
 
 VM = pl.BlockSpec(memory_space=pltpu.VMEM)
@@ -404,24 +829,70 @@
     )(*operands)
 
 
+def backward_call(*operands):
+    struct = jax.ShapeDtypeStruct
+    dma = pltpu.SemaphoreType.DMA
+    vm = pltpu.VMEM
+    return pl.pallas_call(
+        backward_kernel,
+        out_shape=(
+            struct((2, 128, 768), F32),
+            struct((2, 128, 768), F32),
+            struct((2, 192, 768), F32),
+            struct((2, 32, 768), F32),
+            struct((2, 96, 768), F32),
+            struct((16, 768), F32),
+        ),
+        in_specs=[VM] * 10 + [ANY] + [VM] * (len(operands) - 11),
+        out_specs=(VM,) * 6,
+        scratch_shapes=[
+            vm((2, 2, 768, 768), BF),
+            vm((2, 2, 256, 768), BF),
+            vm((2, 4, 2, 256, 768), BF),
+            vm((768, 512), BF),
+            vm((2, 128, 768), F32),
+            vm((2, 256, 768), BF),
+            vm((4, 2, 128, LANES), BF),
+            vm((4, 2, 128, LANES), BF),
+            vm((2, 4, 128, LANES), BF),
+            vm((4, 4, 224, 768), BF),
+            vm((4, 2, 224, 768), BF),
+            vm((4, 224, 768), BF),
+            vm((4, 224, 768), BF),
+            vm((1024, 512), F32),
+            vm((LANES, 1024), BF),
+            vm((LANES, 512), F32),
+            vm((1024, LANES), F32),
+            vm((1024, LANES), F32),
+            vm((2, 512, 2 * LANES), BF),
+            vm((2, 512, 2 * LANES), BF),
+            vm((2, 512, 768), BF),
+            vm((2, 4, 128, 768), BF),
+            vm((2, 4, 128, 768), BF),
+            vm((768, 1024), BF),
+            vm((2, 4, 96, 768), BF),
+            vm((2, 4, 96, 768), BF),
+            vm((768, 768), F32),
+            vm((16, 768), F32),
+            vm((16, 768), F32),
+            vm((4, 16, 768), F32),
+            vm((4, 16, 768), F32),
+            vm((768, 512), BF),
+            dma((2, 4)), dma((1,)), dma((1,)), dma((4,)), dma((4,)), dma((1,)), dma((1,)),
+            dma((1,)), dma((1,)), dma((2, 3)), dma((2, 4)),
+            dma((4, 2)), dma((4, 2)), dma((4,)), dma((4,)), dma((3,)), dma((4,)),
+            dma((2,)), dma((2,)), dma((2, 3)), dma((2, 4)),
+            dma((1,)), dma((1,)), dma((3,)), dma((4,)), dma((3,)), dma((3,)), dma((7,)), dma((9,)),
+        ],
+        compiler_params=pltpu.CompilerParams(
+            collective_id=2, has_side_effects=True, vmem_limit_bytes=63 << 20
+        ),
+        name="backward",
+    )(*operands)
+
+
 def pad_heads(block):
     return jnp.pad(block, [(0, 0)] * (block.ndim - 1) + [(0, LANES - block.shape[-1])])
-
-
-def smooth_slope(values, cdf):
-    return cdf + values * (jnp.exp(-0.5 * values * values) * INV_ROOT_TWO_PI)
-
-
-def norm_backward(grad_out, scaled, inverse, gain):
-    grad_scaled = grad_out * gain
-    plain_mean = jnp.mean(grad_scaled, axis=-1, keepdims=True)
-    cross_mean = jnp.mean(grad_scaled * scaled, axis=-1, keepdims=True)
-    grad_rows = inverse * (grad_scaled - plain_mean - scaled * cross_mean)
-    return (grad_rows, jnp.sum(grad_out * scaled, axis=(0, 1)), jnp.sum(grad_out, axis=(0, 1)))
-
-
-def place_piece(piece, total, start):
-    return lax.dynamic_update_slice(jnp.zeros((total,), F32), piece, (start,))
 
 
 def body(
@@ -446,112 +917,27 @@
         [pad_heads(q_piece), jnp.zeros((LANES,), F32), pad_heads(v_piece)]
     )[None, :]
     places = jnp.arange(segment_ids.shape[1], dtype=jnp.int32)[None, :]
-    seg = jnp.where(segment_ids >= 0, segment_ids, -1 - places)
+    seg = jnp.where(segment_ids >= 0, segment_ids, -1 - places).astype(F32)
     seg_q = lax.dynamic_slice_in_dim(seg, ctx_at * 512, 512, axis=1)
 
     (normed, queries, kv, mixed_in, middle, normed_f, wqkv, wout, weights) = forward_call(
         hidden_in, attn_gain[None], attn_shift[None], wqkv_s, cargo_s, bias_s, output_bias[None],
-        ffn_gain[None], ffn_shift[None], seg[:, :, None], seg_q[:, None, :],
-    )
-    w_in = weights[0].reshape(4, 768, 768)
-    w_out = weights[1].reshape(4, 768, 768)
-
-    scaled_a, inverse_a = norm_parts(hidden_in)
-    scaled_f, inverse_f = norm_parts(middle)
-    nf = normed_f.reshape(256, 768)
-    cot = cotangent.reshape(256, 768)
-    up = cot.astype(BF)
-    inner = jnp.einsum("rd,tdu->rtu", nf, w_in, preferred_element_type=F32) + inner_bias.reshape(4, 768)
-    cdf = 0.5 * (1.0 + lax.erf(inner * ROOT_HALF))
-    active = (inner * cdf).astype(BF)
-    block_out = middle + jnp.einsum(
-        "rtu,tdu->rd", active, w_out, preferred_element_type=F32
-    ).reshape(2, 128, 768) + outer_bias
-    grad_active = jnp.einsum("rd,tdu->rtu", up, w_out, preferred_element_type=F32)
-    grad_inner = (grad_active * smooth_slope(inner, cdf)).astype(BF)
-    grad_nf = jnp.einsum("rtu,tdu->rd", grad_inner, w_in, preferred_element_type=F32)
-    grad_w_in = jnp.einsum("rd,rtu->tdu", nf, grad_inner, preferred_element_type=F32)
-    grad_w_out = jnp.einsum("rd,rtu->tdu", up, active, preferred_element_type=F32)
-    grad_rows_f, grad_ffn_g, grad_ffn_s = norm_backward(
-        grad_nf.reshape(2, 128, 768), scaled_f, inverse_f, ffn_gain
-    )
-    grad_middle = cotangent + grad_rows_f
-    grad_branch = grad_middle.astype(BF)
-    gb = grad_branch.reshape(256, 768)
-    grad_wout = jnp.einsum(
-        "trc,rd->tdc", mixed_in.reshape(4, 256, LANES), gb, preferred_element_type=F32
-    )
-    grad_mix = jnp.einsum("rd,tdc->trc", gb, wout, preferred_element_type=F32).astype(BF)
-    grad_mix = lax.all_to_all(grad_mix.reshape(4, 2, 128, LANES), "tensor", 0, 0, tiled=True)
-    grad_mixed = grad_mix.transpose(1, 0, 2, 3).reshape(2, 512, LANES)[..., :part]
-    heads = part // HDIM
-    q3 = queries[..., :part].reshape(2, 512, heads, HDIM)
-    k3 = kv[..., :part].reshape(2, 1024, heads, HDIM)
-    v3 = kv[..., LANES : LANES + part].reshape(2, 1024, heads, HDIM)
-    g3 = grad_mixed.reshape(2, 512, heads, HDIM)
-    scores = jnp.einsum("sqhd,skhd->shqk", q3, k3, preferred_element_type=F32)
-    scores = jnp.where((seg_q[:, :, None] == seg[:, None, :])[:, None], scores, HIDE)
-    probs = jax.nn.softmax(scores, axis=-1)
-    grad_probs = jnp.einsum("sqhd,skhd->shqk", g3, v3, preferred_element_type=F32)
-    centre = jnp.sum(probs * grad_probs, axis=-1, keepdims=True)
-    grad_scores = (probs * (grad_probs - centre)).astype(BF)
-    grad_v = jnp.einsum("shqk,sqhd->skhd", probs.astype(BF), g3, preferred_element_type=F32)
-    grad_k = jnp.einsum("shqk,sqhd->skhd", grad_scores, q3, preferred_element_type=F32)
-    grad_q = jnp.einsum("shqk,skhd->sqhd", grad_scores, k3, preferred_element_type=F32) * HDIM**-0.5
-    grad_q = grad_q.reshape(2, 512, part).astype(BF)
-    grad_k = lax.psum_scatter(
-        grad_k.reshape(2, 1024, part).astype(BF), "ctx", scatter_dimension=1, tiled=True
-    )
-    grad_v = lax.psum_scatter(
-        grad_v.reshape(2, 1024, part).astype(BF), "ctx", scatter_dimension=1, tiled=True
-    )
-    grad_qkv = jnp.concatenate([pad_heads(grad_q), pad_heads(grad_k), pad_heads(grad_v)], axis=-1)
-    grad_qkv = grad_qkv.reshape(1024, 768)
-    grad_wqkv = jnp.einsum(
-        "rd,rc->dc", normed.reshape(1024, 768), grad_qkv, preferred_element_type=F32
-    )
-    grad_na = jnp.einsum("rc,dc->rd", grad_qkv, wqkv.reshape(768, 768), preferred_element_type=F32)
-    grad_na = lax.psum_scatter(
-        grad_na.astype(BF).reshape(2, 512, 768), "tensor", scatter_dimension=1, tiled=True
-    ).astype(F32)
-    grad_rows_a, grad_attn_g, grad_attn_s = norm_backward(grad_na, scaled_a, inverse_a, attn_gain)
-    grad_input = grad_middle + grad_rows_a
-
-    g_in = lax.psum_scatter(
-        grad_w_in.astype(BF).reshape(4, 4, 192, 768), "tensor", scatter_dimension=0, tiled=True
-    )
-    g_in = lax.psum_scatter(g_in, "dp", scatter_dimension=1, tiled=True).reshape(192, 768)
-    g_out = lax.psum_scatter(
-        grad_w_out.astype(BF).reshape(4, 4, 192, 768), "tensor", scatter_dimension=0, tiled=True
-    )
-    g_out = lax.psum_scatter(g_out, "dp", scatter_dimension=1, tiled=True).reshape(192, 768)
-    g_wo = lax.psum_scatter(
-        grad_wout.astype(BF).reshape(4, 4, 192, LANES), "tensor", scatter_dimension=0, tiled=True
-    )
-    g_wo = lax.psum_scatter(g_wo, "dp", scatter_dimension=1, tiled=True).reshape(192, LANES)
-    g_qkv = lax.psum_scatter(
-        grad_wqkv.astype(BF).reshape(4, 192, 768), "dp", scatter_dimension=0, tiled=True
-    ).reshape(192, 768)
-    g_in, g_out, g_wo, g_qkv = lax.psum((g_in, g_out, g_wo, g_qkv), "ctx")
-    g_in, g_out, g_wo, g_qkv = (g.astype(F32) for g in (g_in, g_out, g_wo, g_qkv))
-    sums = jnp.sum(grad_qkv.astype(F32), axis=0)
-    small = lax.psum(
-        jnp.concatenate([
-            grad_attn_g, grad_attn_s,
-            place_piece(sums[:part], 768, tensor_at * part),
-            place_piece(sums[2 * LANES : 2 * LANES + part], 768, tensor_at * part),
-            jnp.sum(grad_middle, axis=(0, 1)), grad_ffn_g, grad_ffn_s,
-            jnp.sum(cotangent, axis=(0, 1)),
-            jnp.sum(grad_inner.astype(F32), axis=0).reshape(3072),
-        ]),
-        ("dp", "ctx", "tensor"),
-    )
-    row = lambda i: small[768 * i : 768 * (i + 1)]
+        ffn_gain[None], ffn_shift[None], seg[:, None, :], seg_q[:, None, :],
+    )
+    (block_out, grad_input, g_ff, g_wo, g_qkv, small) = backward_call(
+        hidden_in, cotangent, middle, normed_f, normed, queries, kv, mixed_in, wqkv, wout,
+        weights.reshape(2, 4, 768, 768), seg[:, None, :], seg_q[:, None, :], attn_gain[None],
+        ffn_gain[None], inner_bias.reshape(4, 1, 768), outer_bias[None],
+    )
+    g_qkv = g_qkv.reshape(192, 768)
+    g_wo = g_wo.reshape(2, 32, 3, LANES).transpose(0, 2, 1, 3).reshape(192, LANES)
+    heads = small[12:, :]
     return (
-        block_out, grad_input, row(0), row(1),
+        block_out, grad_input, small[0], small[1],
         g_qkv[:, :part], g_qkv[:, LANES : LANES + part], g_qkv[:, 2 * LANES : 2 * LANES + part],
-        row(2), row(3), g_wo[:, :part].T, row(4), row(5), row(6), g_in, small[768 * 8 :],
-        g_out.T, row(7),
+        heads[:, :part].reshape(-1), heads[:, 2 * LANES : 2 * LANES + part].reshape(-1),
+        g_wo[:, :part].T, small[4], small[2], small[3], g_ff[0], small[6:10].reshape(-1),
+        g_ff[1].T, small[5],
     )
 
 

time: 646 us -> 255 us (0.39)
  waiting for transfers between devices: 337 us -> 0 us
  Pallas kernels: 109 us -> 226 us
  matrix products: 59.4 us -> 0 us
  blocking collectives: 39.7 us -> 0 us
  local copies, waits for them, and re-layouts: 48.5 us -> 21.9 us
  other arithmetic: 28.6 us -> 5.11 us
  between operations: 16.2 us -> 0.81 us
    unnamed x16 -> x0, waiting for transfers between devices: 261 us -> none
    pallas_call x0 -> x1, Pallas kernels: none -> 117 us  [backward_call(): pl.pallas_call(backward_kernel, out_shape=(struct((2, 128, 768), F32), st...]
    reduce_scatter x5 -> x0, waiting for transfers between devices: 76.2 us -> none  [the longest x1 43.3 us: body(): lax.psum_scatter(grad_w_out.astype(BF).reshape(4, 4, 192, 768), 'tensor',...]
    dot_general x14 -> x0, matrix products: 51 us -> none  [the longest x1 6.8 us: body(): jnp.einsum('rd,tdu->rtu', nf, w_in, preferred_element_type=F32)]
    psum x1 -> x0, blocking collectives: 39.7 us -> none  [body(): lax.psum(jnp.concatenate([grad_attn_g, grad_attn_s, place_piece(sums[:par...]
    slice x8 -> x3, local copies, waits for them, and re-layouts: 15.5 us -> 3.27 us  [the longest x1 1.62 us: body(): small[5]]
    sub x1 -> x0, matrix products: 8.46 us -> none  [body(): probs = jax.nn.softmax(scores, axis=-1)]
    reduce_sum x8 -> x0, other arithmetic: 8.09 us -> none  [the longest x1 1.94 us: body(): sums = jnp.sum(grad_qkv.astype(F32), axis=0)]
  transfers between devices with their start and end apart: 12 -> 0, of which waited for: 7 -> 0; matrix products, arithmetic and copies ran while one was open for 11% -> 0% of each run, Pallas kernels for 0% -> 0%
where the time goes in v2:
time: 255 us; the launch traced here: 254 us
  Pallas kernels  226 us (89%)
  local copies, waits for them, and re-layouts  21.9 us (9%)
  other arithmetic  5.11 us (2%)
    pallas_call x1, Pallas kernels, backward_call(): pl.pallas_call(backward_kernel, out_shape=(struct((2, 128, 768), F32), st...  117 us
    pallas_call x1, Pallas kernels, forward_call(): pl.pallas_call(forward_kernel, out_shape=(struct((2, 4, 128, 768), BF), s...  109 us

profile of v2, /device:TPU:0, one launch (start us, length us, event | category | flops | bytes accessed | tf_op | source)
XLA Modules:
  0.0 253.9 jit_solution(6270186382324752826)
XLA Ops:
  0.7 0.9 dynamic_slice.13
  1.6 0.8 dynamic_slice.14
  3.0 1.3 broadcast_in_dim.43.gain.gain_a
  4.2 1.3 broadcast_in_dim.48.gain_f
  5.5 1.3 broadcast_in_dim.44.shift
  6.8 1.3 broadcast_in_dim.47.out_bias
  8.0 1.3 broadcast_in_dim.49.shift_f
  9.3 1.3 broadcast_in_dim.53.outer_bias
  12.5 0.9 convert.15
  13.4 0.9 convert.16
  14.4 0.9 convert.17
  15.3 0.8 fusion.6.wqkv_s
  16.3 0.8 pad_maximum_fusion.cargo_s
  17.0 109.3 %forward.1 = (bf16[2,4,128,768]{3,2,1,0:T(8,128)(2,1)}, bf16[2,512,256]{2,1,0:T(8,128)(2,1)}, bf16[2,2,4,128,512]{4,3,2,1,0:T(8,128)(2,1)}, bf16[4,2,128,256]{3,...) custom-call(f32[2,128,768]{2,1,0:T(8,128)} %hidden.3, ...), custom_call_target="tpu_custom_call" | custom-call | tf_op jit(solution)/shard_map/forward/pallas_call | solution.py:797
  126.4 116.7 %backward.1 = (f32[2,128,768]{2,1,0:T(8,128)}, f32[2,128,768]{2,1,0:T(8,128)}, f32[2,192,768]{2,1,0:T(8,128)}, f32[2,32,768]{2,1,0:T(8,128)}, f32[2,96,768]{2,1,0:T(8,128)}, /*index=5*/f32[16,768]{1,0:T(8,128)}) custom-call(f32[2,128,768]{2,1,0:T(8,128)} %hidden.3, f32[2,128,768]{2,1,0:T(8,128)} %cot.1, f32[2,128,768]{2,1,0:T(8,128)} %get-tuple-element.32.middle, ...), custom_call_target="tpu_custom_call" | custom-call | tf_op jit(solution)/shard_map/backward/pallas_call | solution.py:836
  243.1 0.8 fusion.9
  245.3 0.8 slice.60
  246.1 1.6 slice_reduce_fusion
  248.3 1.0 reshape.76
  249.4 0.8 copy.39
  250.2 0.8 fusion.8
  251.1 1.1 slice_bitcast_fusion
  252.1 0.9 copy.43
  253.0 0.9 copy.44
  (31 shorter events, 4.7 us)
Async XLA Ops:
  0.7 15.5 %copy-start.4 = (f32[768,192]{0,1:T(8,128)S(1)}, f32[768,192]{0,1:T(8,128)}, u32[]{:S(2)}) copy-start(f32[768,192]{0,1:T(8,128)} %param.34) | copy-start | bytes 1769476
  0.7 15.5 %copy-start.3 = (f32[192,768]{1,0:T(8,128)S(1)}, f32[192,768]{1,0:T(8,128)}, u32[]{:S(2)}) copy-start(f32[192,768]{1,0:T(8,128)} %param.32) | copy-start | bytes 1769476
  0.7 15.4 %copy-start.6 = (f32[192,192]{1,0:T(8,128)S(1)}, f32[192,192]{1,0:T(8,128)}, u32[]{:S(2)}) copy-start(f32[192,192]{1,0:T(8,128)} %param.28) | copy-start | bytes 442372
  243.1 7.1 %copy-start.5 = (f32[2,96,768]{2,1,0:T(8,128)S(1)}, f32[2,96,768]{2,1,0:T(8,128)}, u32[]{:S(2)}) copy-start(f32[2,96,768]{2,1,0:T(8,128)} %get-tuple-element.44) | copy-start | bytes 1769476
  243.1 7.9 %copy-start = (f32[2,192,768]{2,1,0:T(8,128)S(1)}, f32[2,192,768]{2,1,0:T(8,128)}, u32[]{:S(2)}) copy-start(f32[2,192,768]{2,1,0:T(8,128)} %get-tuple-element.46) | copy-start | bytes 3538948
  250.2 1.9 copy-start.2
  251.1 2.0 copy-start.1

commit v3 on v0

--- a/solution.py
+++ b/solution.py
@@ -1,33 +1,979 @@
+import functools
+
 import jax
 import jax.numpy as jnp
 from jax import lax
+from jax.experimental import pallas as pl
+from jax.experimental.pallas import tpu as pltpu
 from jax.sharding import PartitionSpec as P
 
 HDIM = 64
+LANES = 256
+ROOT_HALF = 0.7071067811865476
+INV_ROOT_TWO_PI = 0.3989422804014327
+MESH = pl.DeviceIdType.MESH
+BF = jnp.bfloat16
+F32 = jnp.float32
+HIDE = -1e30
+
+
+def dims(left, right, a, b):
+    return lax.dot_general(left, right, (((a,), (b,)), ((), ())), preferred_element_type=F32)
+
+
+def norm_parts(rows):
+    centred = rows - jnp.mean(rows, axis=-1, keepdims=True)
+    inverse = lax.rsqrt(jnp.mean(centred * centred, axis=-1, keepdims=True) + 1e-05)
+    return centred * inverse, inverse
+
+
+class Place:
+    def __init__(self):
+        self.d = lax.axis_index("dp")
+        self.c = lax.axis_index("ctx")
+        self.t = lax.axis_index("tensor")
+        col, row = self.d % 2, self.d // 2
+        self.dx = row * 2 + (1 - col)
+        self.dy = (1 - row) * 2 + col
+        self.dd = (1 - row) * 2 + (1 - col)
+        self.side = self.t // 2
+        self.mid = self.t + self.side * (3 - 2 * self.t)
+
+    def unmirror(self, place):
+        return place + self.side * (3 - 2 * place)
+
+    def order(self, k):
+        if k == 0:
+            return self.unmirror(1 - self.mid)
+        return self.unmirror(k + 1)
+
+    def order_at(self, k):
+        first = 1 - jnp.minimum(k, 1)
+        near = first * (1 - self.mid) + (1 - first) * (k + 1)
+        own = jnp.minimum(k, 0)
+        return -own * self.t + (1 + own) * self.unmirror(near)
+
+
+def remote(src, dst, send, recv, **where):
+    return pltpu.make_async_remote_copy(
+        src_ref=src, dst_ref=dst, send_sem=send, recv_sem=recv, device_id=where, device_id_type=MESH
+    )
+
+
+def greet(place):
+    barrier = pltpu.get_barrier_semaphore()
+    for k in range(1, 4):
+        pl.semaphore_signal(
+            barrier, inc=1, device_id={"tensor": (place.t + k) % 4}, device_id_type=MESH
+        )
+    for peer in (place.dx, place.dy, place.dd):
+        pl.semaphore_signal(barrier, inc=1, device_id={"dp": peer}, device_id_type=MESH)
+    pl.semaphore_signal(barrier, inc=1, device_id={"ctx": 1 - place.c}, device_id_type=MESH)
+    return lambda: pl.semaphore_wait(barrier, 7)
+
+
+class Several:
+    def __init__(self, *copies):
+        self.copies = copies
+
+    def start(self):
+        for copy in self.copies:
+            copy.start()
+
+    def wait_send(self):
+        for copy in self.copies:
+            copy.wait_send()
+
+    def wait_recv(self):
+        for copy in self.copies:
+            copy.wait_recv()
+
+
+def rows_at(start, size, step):
+    return pl.ds(pl.multiple_of(start, step), size)
+
+
+def erf_parts(values):
+    cdf = 0.5 * (1.0 + lax.erf(values * ROOT_HALF))
+    return cdf, cdf + values * (jnp.exp(-0.5 * values * values) * INV_ROOT_TWO_PI)
+
+
+def layer_kernel(
+    hidden, cot, seg, gain_a, shift_a, wq_s, wk_s, wv_s, bias_q, bias_v, wo_s, bias_o, gain_f, shift_f,
+    win_s, bias_in, wout_s, bias_out,
+    block_out, grad_input, g_gain_a, g_shift_a, g_wq, g_wk, g_wv, g_bias_q, g_bias_v, g_wo, g_bias_o,
+    g_gain_f, g_shift_f, g_win, g_bias_in, g_wout, g_bias_out,
+    normed, normed_turn, queries, kv, mixed_in, mixed_sib, wqkv, wout, ffw, turn, q_turn, mixed, g_mix,
+    keys_seg, left, left_in, left_turn, right, right_in, branch, branch_turn, part_wo, rx1, rx2, rz,
+    rx1w, rx2w, rzw, wide, kv_out, kv_in, dqkv, gna, rzn, qkv_sib, qkv_in, sums, sums_core, sums_plane,
+    sums_line, res_ff, res_wo, res_qkv, bias_row, inner_rows,
+    q_send, q_recv, qc_send, qc_recv, z_send, z_recv, kvf_send, kvf_recv, mf_send, mf_recv,
+    cz_send, cp_send, cc_send, c_recv, s_recv,
+    l_send, l_recv, r_send, r_recv, b_send, b_recv, x_send, x_recv, m_send, m_recv,
+    p1_send, p1_recv, p2_send, p2_recv, w1_send, w1_recv, zz_send, zz_recv, kv_send, kv_recv,
+    n_send, n_recv, qs_send, qs_recv, qp_send, qp_recv, f_send, f_recv, s_send, sum_recv,
+):
+    at = Place()
+    d, c, t = at.d, at.c, at.t
+    other = 1 - c
+    planes = (at.dx, at.dy, at.dd)
+    others = [(t + k + 1) % 4 for k in range(3)]
+    arrive = greet(at)
+
+    for ref, start in ((wq_s, 0), (wk_s, LANES), (wv_s, 2 * LANES)):
+        wqkv[d, :, start + 128 : start + 256] = jnp.zeros((192, 128), BF)
+        wqkv[d, :, start : start + 192] = ref[...].astype(BF)
+    arrive()
+
+    def q_copy(i):
+        half = wqkv.at[d, rows_at(c * 96, 96, 96)]
+        return remote(half, half, q_send.at[i], q_recv.at[d], dp=planes[i])
+
+    for i in range(3):
+        q_copy(i).start()
+
+    scaled, _ = norm_parts(hidden[0])
+    normed[0, t] = (scaled * gain_a[...].reshape(1, 768) + shift_a[...].reshape(1, 768)).astype(BF)
+
+    def z_copy(s, k):
+        return remote(normed.at[s, t], normed.at[s, t], z_send.at[s, k], z_recv.at[s, t], tensor=at.order(k))
+
+    def z_pass(s, shard):
+        block = normed.at[s, shard]
+        return remote(block, block, z_send.at[s, 3], z_recv.at[s, shard], tensor=at.unmirror(0))
+
+    def z_start(s):
+        z_copy(s, 0).start()
+        z_copy(s, 1).start()
+
+        @pl.when(at.mid == 1)
+        def _():
+            z_copy(s, 2).start()
+
+    z_start(0)
+
+    here = rows_at(d * 192, 192, 192)
+
+    @pl.when(c == 0)
+    def _():
+        ffw[0, t, here, :] = win_s[...].astype(BF)
+
+    @pl.when(c == 1)
+    def _():
+        ffw[1, t, here, :] = wout_s[...].astype(BF)
+
+    turned = wo_s[...].T
+    turned = jnp.where(c == 0, turned[:96], turned[96:]).astype(BF)
+    here = rows_at(d * 192 + c * 96, 96, 96)
+    wout[t, here, 128:256] = jnp.zeros((96, 128), BF)
+    wout[t, here, 0:192] = turned
+
+    def ff_block(which, shard, owner):
+        return ffw.at[which, shard, rows_at(owner * 192, 192, 192)]
+
+    def wo_block(which, shard, owner):
+        return wout.at[shard, rows_at(owner * 192 + which * 96, 96, 96)]
+
+    def carry_to(shard, owner, send, **where):
+        f, w = ff_block(c, shard, owner), wo_block(c, shard, owner)
+        return Several(
+            remote(w, w, send.at[1], c_recv.at[shard, owner, 1], **where),
+            remote(f, f, send.at[0], c_recv.at[shard, owner, 0], **where),
+        )
+
+    def cargo_z(k):
+        return carry_to(t, d, cz_send.at[k], tensor=at.order(k))
+
+    def cargo_pass(shard):
+        return carry_to(shard, d, cz_send.at[3], tensor=at.unmirror(0))
+
+    def cargo_plane(axis, k, shard, owner, dest):
+        return carry_to(shard, owner, cp_send.at[axis, k], dp=dest)
+
+    def cargo_core(shard, owner):
+        f, w = ff_block(c, shard, owner), wo_block(c, shard, owner)
+        return Several(
+            remote(w, w, cc_send.at[shard, owner, 1], s_recv.at[shard, owner, 1], ctx=other),
+            remote(f, f, cc_send.at[shard, owner, 0], s_recv.at[shard, owner, 0], ctx=other),
+        )
+
+    def arrived(shard, owner):
+        carry_to(shard, owner, cz_send.at[0], dp=d).wait_recv()
+
+    def from_sibling(shard, owner):
+        f, w = ff_block(other, shard, owner), wo_block(other, shard, owner)
+        Several(
+            remote(w, w, cc_send.at[shard, owner, 1], s_recv.at[shard, owner, 1], ctx=other),
+            remote(f, f, cc_send.at[shard, owner, 0], s_recv.at[shard, owner, 0], ctx=other),
+        ).wait_recv()
+
+    def spread(k, shard):
+        cargo_plane(0, k, shard, d, at.dx).start()
+        cargo_plane(1, k, shard, d, at.dy).start()
+        cargo_core(shard, d).start()
+
+    def diag_of(k, shard, act):
+        @pl.when(shard < 2)
+        def _():
+            act(cargo_plane(1, 4 + k, shard, at.dx, at.dy))
+
+        @pl.when(shard >= 2)
+        def _():
+            act(cargo_plane(0, 4 + k, shard, at.dy, at.dx))
+
+    def diag(k, shard):
+        arrived(shard, at.dx)
+        arrived(shard, at.dy)
+        diag_of(k, shard, lambda copy: copy.start())
+        cargo_core(shard, at.dx).start()
+        cargo_core(shard, at.dy).start()
+
+    spread(0, t)
+    cargo_z(0).start()
+    cargo_z(1).start()
+
+    @pl.when(at.mid == 1)
+    def _():
+        cargo_z(2).start()
+
+    scaled, _ = norm_parts(hidden[1])
+    normed[1, t] = (scaled * gain_a[...].reshape(1, 768) + shift_a[...].reshape(1, 768)).astype(BF)
+    left[1] = cot[...].reshape(256, 768).astype(BF)
+    sums[...] = jnp.zeros_like(sums)
+    wide[...] = jnp.zeros_like(wide)
+    bias_row[...] = jnp.zeros_like(bias_row)
+    for p in range(4):
+
+        @pl.when(t == p)
+        def _(p=p):
+            bias_row[:, 0:192] = bias_q[...].reshape(1, 768)[:, p * 192 : (p + 1) * 192]
+            bias_row[:, 512:704] = bias_v[...].reshape(1, 768)[:, p * 192 : (p + 1) * 192]
+
+        inner_rows[p] = bias_in[...].reshape(1, 3072)[:, p * 768 : (p + 1) * 768]
+
+    def seg_rows(s):
+        row = seg[s : s + 1, :]
+        places = lax.broadcasted_iota(jnp.int32, (1, 1024), 1)
+        return jnp.where(row >= 0, row, -1 - places).astype(F32)
+
+    def seg_query(s):
+        row = seg_rows(s)
+        return jnp.where(c == 0, row[:, :512], row[:, 512:])
+
+    def q_core(i):
+        half = wqkv.at[planes[i], rows_at(c * 96, 96, 96)]
+        return remote(half, half, qc_send.at[i], qc_recv.at[i], ctx=other)
+
+    for i in range(3):
+        half = wqkv.at[planes[i], rows_at(c * 96, 96, 96)]
+        remote(half, half, q_send.at[i], q_recv.at[planes[i]], dp=d).wait_recv()
+        q_core(i).start()
+    for i in range(3):
+        half = wqkv.at[planes[i], rows_at(other * 96, 96, 96)]
+        remote(half, half, qc_send.at[i], qc_recv.at[i], ctx=other).wait_recv()
+
+    def kvf_copy(s, p):
+        return remote(kv.at[s, c, p], kv.at[s, c, p], kvf_send.at[s, p], kvf_recv.at[s, p], ctx=other)
+
+    def project(s):
+        def step(k, carry):
+            p = at.order_at(k - 1)
+
+            @pl.when(k > 0)
+            def _():
+                block = normed.at[s, p]
+                remote(block, block, z_send.at[s, 0], z_recv.at[s, p], tensor=p).wait_recv()
+
+            @pl.when((k == 3) & (at.mid == 1))
+            def _():
+                z_pass(s, p).start()
+
+            out = jnp.dot(normed[s, p], wqkv[...].reshape(768, 768), preferred_element_type=F32)
+            out = (out + bias_row[...]).astype(BF)
+            queries[s, rows_at(p * 128, 128, 128), :] = out[:, :LANES] * jnp.asarray(HDIM**-0.5, BF)
+            kv[s, c, p] = out[:, LANES:]
+            kvf_copy(s, p).start()
+            return carry
+
+        lax.fori_loop(0, 4, step, 0)
+
+    lane_head = lax.broadcasted_iota(jnp.int32, (1, LANES), 1) // HDIM
+
+    def masked_scores(s, b, q_here):
+        seg_here = seg_query(s)
+        seg_here = jnp.where(b == 0, seg_here[:, :256], seg_here[:, 256:])
+        keys = kv[s].reshape(1024, 2 * LANES)[:, :LANES]
+        scores = dims(keys, q_here, 1, 1)
+        column = keys_seg[...]
+        visible = jnp.concatenate([column, column], axis=1) == seg_here
+        return jnp.where(visible, scores, HIDE)
+
+    def one_head(h, block):
+        return jnp.where(lane_head == h, block.astype(F32), 0.0).astype(BF)
+
+    def attend(s):
+        for p in range(4):
+            block = kv.at[s, other, p]
+            remote(block, block, kvf_send.at[s, p], kvf_recv.at[s, p], ctx=other).wait_recv()
+        keys_seg[...] = jnp.broadcast_to(seg_rows(s), (128, 1024)).T
+        turn[...] = kv[s].reshape(1024, 2 * LANES)[:, LANES:].T
+        q_turn[192:, :] = jnp.zeros((64, 512), F32)
+
+        def step(i, carry):
+            h, b = i // 2, i % 2
+            block = rows_at(b * 256, 256, 256)
+            scores = masked_scores(s, b, one_head(h, queries[s, block, :]))
+            peak = jnp.max(scores, axis=0, keepdims=True)
+            expo = jnp.exp(scores - peak)
+            total = jnp.sum(expo, axis=0, keepdims=True)
+            rows = rows_at(h * HDIM, HDIM, HDIM)
+            turned = jnp.dot(turn[rows, :], expo.astype(BF), preferred_element_type=F32)
+            q_turn[rows, block] = turned / total
+            return carry
+
+        lax.fori_loop(0, 6, step, 0)
+        mixed[:, s] = q_turn[...].T.astype(BF).reshape(4, 128, LANES)
+        for k in range(3):
+            mf_copy(s, k).start()
+        mixed_in[t, s] = mixed[t, s]
+
+    def mf_copy(s, k):
+        dest = others[k]
+        return remote(mixed.at[dest, s], mixed_in.at[t, s], mf_send.at[s, k], mf_recv.at[s, t], tensor=dest)
+
+    project(0)
+    z_start(1)
+    arrived(at.order(0), d)
+    spread(1, at.order(0))
+    diag(0, t)
+    attend(0)
+    arrived(at.order(1), d)
+    spread(2, at.order(1))
+    diag(1, at.order(0))
+    arrived(at.order(2), d)
+
+    @pl.when(at.mid == 1)
+    def _():
+        cargo_pass(at.order(2)).start()
+
+    spread(3, at.order(2))
+    diag(2, at.order(1))
+    project(1)
+    attend(1)
+    diag(3, at.order(2))
+    normed_turn[...] = normed[...].reshape(1024, 768).T
+    for k in range(4):
+        p = t if k == 0 else at.order(k - 1)
+        arrived(p, at.dd)
+        cargo_core(p, at.dd).start()
+
+    def all_from_sibling(i, carry):
+        from_sibling(i // 4, i % 4)
+        return carry
+
+    lax.fori_loop(0, 16, all_from_sibling, 0)
+    for s in range(2):
+        for k in range(3):
+            p = others[k]
+            block = mixed_in.at[p, s]
+            remote(block, block, mf_send.at[s, k], mf_recv.at[s, p], tensor=p).wait_recv()
+        total = hidden[s] + bias_o[...].reshape(1, 768)
+        for p in range(4):
+            total = total + dims(mixed_in[p, s], wout[p], 1, 1)
+        block_out[s] = total
+        scaled, _ = norm_parts(total)
+        left[0, s * 128 : (s + 1) * 128, :] = (
+            scaled * gain_f[...].reshape(1, 768) + shift_f[...].reshape(1, 768)
+        ).astype(BF)
+
+    left_copy = remote(left.at[other], left_in, l_send.at[0], l_recv.at[0], ctx=other)
+    left_copy.start()
+    mixed_copy = remote(mixed_in, mixed_sib, x_send.at[0], x_recv.at[0], ctx=other)
+    mixed_copy.start()
+
+    for i in range(3):
+        q_copy(i).wait_send()
+        q_core(i).wait_send()
+    for s in range(2):
+        z_copy(s, 0).wait_send()
+        z_copy(s, 1).wait_send()
+
+        @pl.when(at.mid == 1)
+        def _(s=s):
+            z_copy(s, 2).wait_send()
+            z_pass(s, at.order(2)).wait_send()
+
+        for p in range(4):
+            kvf_copy(s, p).wait_send()
+        for k in range(3):
+            mf_copy(s, k).wait_send()
+    cargo_z(0).wait_send()
+    cargo_z(1).wait_send()
+
+    @pl.when(at.mid == 1)
+    def _():
+        cargo_z(2).wait_send()
+        cargo_pass(at.order(2)).wait_send()
+
+    for k in range(4):
+        p = t if k == 0 else at.order(k - 1)
+        cargo_plane(0, k, p, d, at.dx).wait_send()
+        cargo_plane(1, k, p, d, at.dy).wait_send()
+        diag_of(k, p, lambda copy: copy.wait_send())
+
+    def handed_over(i, carry):
+        cargo_core(i // 4, i % 4).wait_send()
+        return carry
+
+    lax.fori_loop(0, 16, handed_over, 0)
+
+    left_turn[0] = left[c].T
+    left_copy.wait_recv()
+    left_turn[1] = left_in[...].T
+
+    def right_copy(i):
+        return remote(right.at[other, i % 2], right_in.at[i], r_send.at[i], r_recv.at[i], ctx=other)
+
+    def near_far(i):
+        near = at.dx + (i // 2) * (at.dy - at.dx)
+        return near, at.dx + at.dy - near
+
+    def first_ff(i, j):
+        near, _ = near_far(i)
+        owner = near if j == 0 else at.dd
+        return remote(ff_block(0, i, owner), rx1.at[i, j], p1_send.at[i, j], p1_recv.at[i, j], dp=near)
+
+    def first_wo(i, j):
+        near, _ = near_far(i)
+        owner = near if j == 0 else at.dd
+        block = part_wo.at[i, rows_at(owner * 192 + c * 96, 96, 96)]
+        return remote(block, rx1w.at[i, j], w1_send.at[i, j], w1_recv.at[i, j], dp=near)
+
+    def weight_gradient(i):
+        right_copy(i).wait_recv()
+
+        def rows_of(q, carry):
+            rows = rows_at(q * 192, 192, 192)
+            out = jnp.dot(left_turn[0, rows, :], right[c, i % 2], preferred_element_type=F32)
+            out = out + jnp.dot(left_turn[1, rows, :], right_in[i], preferred_element_type=F32)
+            ffw[0, i, rows, :] = out.astype(BF)
+            return carry
+
+        lax.fori_loop(0, 4, rows_of, 0)
+        first_ff(i, 0).start()
+        first_ff(i, 1).start()
+
+    def units(i, carry):
+        @pl.when(i >= 2)
+        def _():
+            right_copy(i - 2).wait_send()
+
+        for j in range(3):
+            cols = slice(j * 256, (j + 1) * 256)
+            w_in, w_out = ffw[0, i, :, cols], ffw[1, i, :, cols]
+            inner = jnp.dot(left[0], w_in, preferred_element_type=F32) + inner_rows[i, :, cols]
+            cdf, slope = erf_parts(inner)
+            active = (inner * cdf).astype(BF)
+            right[1, i % 2, :, cols] = active
+            grad_inner = jnp.dot(left[1], w_out, preferred_element_type=F32) * slope
+            grad_inner = grad_inner.astype(BF)
+            right[0, i % 2, :, cols] = grad_inner
+            sums[pl.ds(6 + i, 1), cols] = jnp.sum(grad_inner.astype(F32), axis=0, keepdims=True)
+            up, down = dims(active, w_out, 1, 1), dims(grad_inner, w_in, 1, 1)
+            for k in range(3):
+                wide[k, 0:256, :] += up[:, k * 256 : (k + 1) * 256]
+                wide[k, 256:512, :] += down[:, k * 256 : (k + 1) * 256]
+        right_copy(i).start()
+
+        @pl.when(i > 0)
+        def _():
+            weight_gradient(i - 1)
+
+        return carry
+
+    lax.fori_loop(0, 4, units, 0)
+
+    def add_row(i, value):
+        sums[i : i + 1, :] += jnp.sum(value, axis=0, keepdims=True)
+
+    def norm_back(source, grad_out, gain):
+        scaled, inverse = norm_parts(source)
+        grad_scaled = grad_out * gain[...].reshape(1, 768)
+        plain = jnp.mean(grad_scaled, axis=-1, keepdims=True)
+        cross = jnp.mean(grad_scaled * scaled, axis=-1, keepdims=True)
+        return inverse * (grad_scaled - plain - scaled * cross), scaled
+
+    def wide_rows(start):
+        return jnp.concatenate([wide[k, start : start + 64, :] for k in range(3)], axis=1)
+
+    for s in range(2):
+        for half in range(2):
+            rows = slice(half * 64, half * 64 + 64)
+            start = s * 128 + half * 64
+            middle = block_out[s, rows, :]
+            cot_here = cot[s, rows, :]
+            grad_out = wide_rows(256 + start)
+            grad_rows, scaled = norm_back(middle, grad_out, gain_f)
+            grad_rows = grad_rows + cot_here
+            grad_input[s, rows, :] = grad_rows
+            branch[0, start : start + 64, :] = grad_rows.astype(BF)
+            block_out[s, rows, :] = middle + wide_rows(start) + bias_out[...].reshape(1, 768)
+            add_row(2, grad_out * scaled)
+            add_row(3, grad_out)
+            add_row(4, grad_rows)
+            add_row(5, cot_here)
+    branch_copy = remote(branch.at[0], branch.at[1], b_send.at[0], b_recv.at[0], ctx=other)
+    branch_copy.start()
+
+    def m_copy(s, k):
+        dest = others[k]
+        return remote(mixed.at[dest, s], g_mix.at[s, t], m_send.at[s, k], m_recv.at[s, t], tensor=dest)
+
+    for p in range(4):
+        mixed[p] = jnp.dot(branch[0], wout[p], preferred_element_type=F32).astype(BF).reshape(2, 128, LANES)
+    for s in range(2):
+        for k in range(3):
+            m_copy(s, k).start()
+        g_mix[s, t] = mixed[t, s]
+    weight_gradient(3)
+
+    branch_turn[0] = branch[0].T
+    branch_copy.wait_recv()
+    branch_turn[1] = branch[1].T
+    mixed_copy.wait_recv()
+
+    def wo_gradient(i, carry):
+        out = jnp.dot(branch_turn[0], mixed_in[i].reshape(256, LANES), preferred_element_type=F32)
+        out = out + jnp.dot(branch_turn[1], mixed_sib[i].reshape(256, LANES), preferred_element_type=F32)
+        part_wo[i] = out.astype(BF)
+        first_wo(i, 0).start()
+        first_wo(i, 1).start()
+        return carry
+
+    lax.fori_loop(0, 4, wo_gradient, 0)
+
+    def add_to(target, *terms):
+        total = target[...].astype(F32)
+        for term in terms:
+            total = total + term[...].astype(F32)
+        target[...] = total.astype(BF)
+
+    def wo_part(i, owner):
+        return part_wo.at[i, rows_at(owner * 192 + c * 96, 96, 96)]
+
+    def second(i):
+        _, far = near_far(i)
+        return Several(
+            remote(ff_block(0, i, far), rx2.at[i], p2_send.at[i, 0], p2_recv.at[i, 0], dp=far),
+            remote(wo_part(i, far), rx2w.at[i], p2_send.at[i, 1], p2_recv.at[i, 1], dp=far),
+        )
+
+    def to_second(i):
+        for j in range(2):
+            first_ff(i, j).wait_recv()
+            first_wo(i, j).wait_recv()
+        _, far = near_far(i)
+        add_to(ff_block(0, i, far), rx1.at[i, 1])
+        add_to(wo_part(i, far), rx1w.at[i, 1])
+        second(i).start()
+        add_to(ff_block(0, i, d), rx1.at[i, 0])
+        add_to(wo_part(i, d), rx1w.at[i, 0])
+
+    acc_k, acc_v = wide.at[0], wide.at[1]
+
+    def attend_back(s):
+        for k in range(3):
+            p = others[k]
+            block = g_mix.at[s, p]
+            remote(block, block, m_send.at[s, k], m_recv.at[s, p], tensor=p).wait_recv()
+        keys_seg[...] = jnp.broadcast_to(seg_rows(s), (128, 1024)).T
+        turn[...] = kv[s].reshape(1024, 2 * LANES)[:, :LANES].T
+        q_turn[192:, :] = jnp.zeros((64, 512), F32)
+        acc_k[...] = jnp.zeros((1024, LANES), F32)
+        acc_v[...] = jnp.zeros((1024, LANES), F32)
+
+        def step(i, carry):
+            h, b = i // 2, i % 2
+            block = rows_at(b * 256, 256, 256)
+            q_here = one_head(h, queries[s, block, :])
+            g_here = one_head(h, g_mix[s, pl.ds(b * 2, 2)].reshape(256, LANES))
+            scores = masked_scores(s, b, q_here)
+            peak = jnp.max(scores, axis=0, keepdims=True)
+            expo = jnp.exp(scores - peak)
+            probs = expo * (1.0 / jnp.sum(expo, axis=0, keepdims=True))
+            grad_probs = dims(kv[s].reshape(1024, 2 * LANES)[:, LANES:], g_here, 1, 1)
+            centre = jnp.sum(probs * grad_probs, axis=0, keepdims=True)
+            acc_v[...] += jnp.dot(probs.astype(BF), g_here, preferred_element_type=F32)
+            grad_scores = (probs * (grad_probs - centre)).astype(BF)
+            acc_k[...] += jnp.dot(grad_scores, q_here, preferred_element_type=F32)
+            rows = rows_at(h * HDIM, HDIM, HDIM)
+            q_turn[rows, block] = jnp.dot(turn[rows, :], grad_scores, preferred_element_type=F32)
+            return carry
+
+        lax.fori_loop(0, 6, step, 0)
+        theirs = rows_at(other * 512, 512, 512)
+        kv_out[s, :, :LANES] = acc_k[theirs, :].astype(BF)
+        kv_out[s, :, LANES:] = acc_v[theirs, :].astype(BF)
+        kv_copy(s).start()
+        dqkv[s, :, :LANES] = (q_turn[...].T * HDIM**-0.5).astype(BF)
+        ours = rows_at(c * 512, 512, 512)
+        dqkv[s, :, LANES : 2 * LANES] = acc_k[ours, :].astype(BF)
+        dqkv[s, :, 2 * LANES :] = acc_v[ours, :].astype(BF)
+
+    def kv_copy(s):
+        return remote(kv_out.at[s], kv_in.at[s], kv_send.at[s], kv_recv.at[s], ctx=other)
+
+    class LineSum:
+        def __init__(self, *parts):
+            self.parts = parts
+
+        def copies(self, owner, slot, k, dest):
+            return Several(*[
+                remote(source(owner), landing.at[slot], send.at[k], recv.at[slot], tensor=dest)
+                for source, landing, send, recv in self.parts
+            ])
+
+        def near(self):
+            return self.copies(at.order(0), 0, 0, at.order(0))
+
+        def next(self):
+            return self.copies(at.order(1), 2 - at.mid, 1, at.order(1))
+
+        def far(self):
+            return self.copies(at.order(2), 3, 2, at.order(0))
+
+        def on(self):
+            return self.copies(at.order(2), 1, 2, at.order(2))
+
+        def got(self, slot):
+            self.copies(t, slot, 0, t).wait_recv()
+
+        def start(self):
+            @pl.when(at.mid == 0)
+            def _():
+                self.far().start()
+
+            self.near().start()
+            self.next().start()
+
+        def pass_on(self):
+            @pl.when(at.mid == 1)
+            def _():
+                self.got(3)
+                for source, landing, _, _ in self.parts:
+                    add_to(source(at.order(2)), landing.at[3])
+                self.on().start()
+
+        def collect(self):
+            self.got(0)
+            self.got(1)
+
+            @pl.when(at.mid == 1)
+            def _():
+                self.got(2)
+
+        def end(self):
+            self.near().wait_send()
+            self.next().wait_send()
+
+            @pl.when(at.mid == 0)
+            def _():
+                self.far().wait_send()
+
+            @pl.when(at.mid == 1)
+            def _():
+                self.on().wait_send()
+
+    rows_line = [
+        LineSum((lambda p, s=s: gna.at[s, p], rzn.at[s], n_send.at[s], n_recv.at[s])) for s in range(2)
+    ]
+    cargo_line = LineSum(
+        (lambda p: ff_block(0, p, d), rz, zz_send.at[0], zz_recv.at[0]),
+        (lambda p: wo_part(p, d), rzw, zz_send.at[1], zz_recv.at[1]),
+    )
+
+    def rows_back(s):
+        kv_copy(s).wait_recv()
+        dqkv[s, :, LANES:] = (dqkv[s, :, LANES:].astype(F32) + kv_in[s].astype(F32)).astype(BF)
+        for p in range(4):
+            rows = dqkv[s, p * 128 : (p + 1) * 128, :]
+            gna[s, p] = dims(rows, wqkv[...].reshape(768, 768), 1, 1).astype(BF)
+            sums[pl.ds(12 + t, 1), :] += jnp.sum(rows.astype(F32), axis=0, keepdims=True)
+        rows_line[s].start()
+
+    attend_back(0)
+    to_second(0)
+    to_second(2)
+    rows_back(0)
+    attend_back(1)
+    to_second(1)
+    to_second(3)
+    rows_back(1)
+    rows_line[0].pass_on()
+
+    def qkv_rows(q, carry):
+        rows = rows_at(q * 192, 192, 192)
+        out = jnp.dot(normed_turn[rows, :], dqkv[...].reshape(1024, 768), preferred_element_type=F32)
+        for k in range(3):
+            wide[k, rows, :] = out[:, k * 256 : (k + 1) * 256]
+        return carry
+
+    lax.fori_loop(0, 4, qkv_rows, 0)
+    for p in range(4):
+        theirs = rows_at(p * 192 + other * 96, 96, 96)
+        for k in range(3):
+            qkv_sib[0, p, :, k * 256 : (k + 1) * 256] = wide[k, theirs, :].astype(BF)
+    sib_copy = remote(qkv_sib.at[0], qkv_sib.at[1], qs_send.at[0], qs_recv.at[0], ctx=other)
+    sib_copy.start()
+
+    for i in range(4):
+        second(i).wait_recv()
+        add_to(ff_block(0, i, d), rx2.at[i])
+        add_to(wo_part(i, d), rx2w.at[i])
+    cargo_line.start()
+
+    sib_copy.wait_recv()
+    for p in range(4):
+        ours = rows_at(p * 192 + c * 96, 96, 96)
+        for k in range(3):
+            cols = slice(k * 256, (k + 1) * 256)
+            qkv_in[0, p, :, cols] = (wide[k, ours, :] + qkv_sib[1, p, :, cols].astype(F32)).astype(BF)
+
+    def plane_copy(k):
+        return remote(qkv_in.at[0, planes[k]], qkv_in.at[1, d], qp_send.at[k], qp_recv.at[d], dp=planes[k])
+
+    for k in range(3):
+        plane_copy(k).start()
+    qkv_in[1, d] = qkv_in[0, d]
+    rows_line[1].pass_on()
+    cargo_line.pass_on()
+
+    for k in range(3):
+        block = qkv_in.at[1, planes[k]]
+        remote(block, block, qp_send.at[k], qp_recv.at[planes[k]], dp=d).wait_recv()
+    total = qkv_in[1, 0].astype(F32)
+    for p in range(1, 4):
+        total = total + qkv_in[1, p].astype(F32)
+    res_qkv[c] = total
+
+    def result_copy(i, ref):
+        return remote(ref.at[c], ref.at[c], f_send.at[i], f_recv.at[i], ctx=other)
+
+    result_copy(0, res_qkv).start()
+
+    for s in range(2):
+        rows_line[s].collect()
+        for half in range(2):
+            rows = slice(half * 64, half * 64 + 64)
+            grad_out = gna[s, t, rows, :].astype(F32) + rzn[s, 0, rows, :].astype(F32)
+            grad_out = grad_out + rzn[s, 1, rows, :].astype(F32)
+            third = rzn[s, 2, rows, :].astype(F32)
+            grad_out = grad_out + jnp.where(at.mid == 1, third, jnp.zeros_like(third))
+            grad_rows, scaled = norm_back(hidden[s, rows, :], grad_out, gain_a)
+            grad_input[s, rows, :] += grad_rows
+            add_row(0, grad_out * scaled)
+            add_row(1, grad_out)
+
+    core_sum = remote(sums, sums_core, s_send.at[0], sum_recv.at[0], ctx=other)
+    core_sum.start()
+
+    cargo_line.collect()
+    total = ffw[0, t, rows_at(d * 192, 192, 192), :].astype(F32) + rz[0].astype(F32) + rz[1].astype(F32)
+    third = rz[2].astype(F32)
+    res_ff[c] = total + jnp.where(at.mid == 1, third, jnp.zeros_like(third))
+    total = part_wo[t, rows_at(d * 192 + c * 96, 96, 96), :].astype(F32) + rzw[0].astype(F32)
+    total = total + rzw[1].astype(F32)
+    third = rzw[2].astype(F32)
+    res_wo[c] = total + jnp.where(at.mid == 1, third, jnp.zeros_like(third))
+    result_copy(1, res_ff).start()
+    result_copy(2, res_wo).start()
+
+    core_sum.wait_recv()
+    sums_plane[d] = sums[...] + sums_core[...]
+
+    def plane_sum(k, owner):
+        block = sums_plane.at[owner]
+        return remote(block, block, s_send.at[1 + k], sum_recv.at[1 + owner], dp=planes[k])
+
+    def line_copy(k, owner):
+        block = sums_line.at[owner]
+        return remote(block, block, s_send.at[4 + k], sum_recv.at[5 + owner], tensor=others[k])
+
+    for k in range(3):
+        plane_sum(k, d).start()
+    for k in range(3):
+        plane_sum(k, planes[k]).wait_recv()
+    sums_line[t] = (sums_plane[0] + sums_plane[1]) + (sums_plane[2] + sums_plane[3])
+    for k in range(3):
+        line_copy(k, t).start()
+
+    for i, ref in enumerate((res_qkv, res_ff, res_wo)):
+        result_copy(i, ref).wait_send()
+        block = ref.at[other]
+        remote(block, block, f_send.at[i], f_recv.at[i], ctx=other).wait_recv()
+    for which in range(2):
+        rows = slice(which * 96, (which + 1) * 96)
+        for ref, start in ((g_wq, 0), (g_wk, LANES), (g_wv, 2 * LANES)):
+            ref[rows, :] = res_qkv[which, :, start : start + 192]
+    g_win[...] = res_ff[0]
+    g_wout[...] = res_ff[1]
+    g_wo[...] = res_wo[...].reshape(192, LANES).T[:192, :]
+
+    for k in range(3):
+        line_copy(k, others[k]).wait_recv()
+    total = (sums_line[0] + sums_line[1]) + (sums_line[2] + sums_line[3])
+    for i, ref in enumerate((g_gain_a, g_shift_a, g_gain_f, g_shift_f, g_bias_o, g_bias_out)):
+        ref[...] = total[i]
+    g_bias_in[...] = jnp.concatenate([total[6 + i : 7 + i, :] for i in range(4)], axis=1).reshape(3072)
+    g_bias_q[...] = jnp.concatenate([total[12 + i : 13 + i, :192] for i in range(4)], axis=1).reshape(768)
+    g_bias_v[...] = jnp.concatenate(
+        [total[12 + i : 13 + i, 2 * LANES : 2 * LANES + 192] for i in range(4)], axis=1
+    ).reshape(768)
+
+    core_sum.wait_send()
+    for k in range(3):
+        plane_sum(k, d).wait_send()
+        line_copy(k, t).wait_send()
+        plane_copy(k).wait_send()
+    sib_copy.wait_send()
+    left_copy.wait_send()
+    mixed_copy.wait_send()
+    branch_copy.wait_send()
+    for s in range(2):
+        rows_line[s].end()
+        kv_copy(s).wait_send()
+        for k in range(3):
+            m_copy(s, k).wait_send()
+    cargo_line.end()
+    for i in range(4):
+        for j in range(2):
+            first_ff(i, j).wait_send()
+            first_wo(i, j).wait_send()
+        second(i).wait_send()
+    right_copy(2).wait_send()
+    right_copy(3).wait_send()
+
+
+def deliver_kernel(*refs):
+    sems = refs[-1]
+    count = (len(refs) - 1) // 2
+    copies = [pltpu.make_async_copy(refs[i], refs[count + i], sems.at[i]) for i in range(count)]
+    for copy in copies:
+        copy.start()
+    for copy in copies:
+        copy.wait()
+
+
+VM = pl.BlockSpec(memory_space=pltpu.VMEM)
+ANY = pl.BlockSpec(memory_space=pl.ANY)
+
+
+def body(*operands):
+    struct = jax.ShapeDtypeStruct
+    dma = pltpu.SemaphoreType.DMA
+    vm = pltpu.VMEM
+    operands = operands[:16] + (operands[16].T, operands[17])
+    hidden, cotangent, _, gain, _, wq, wk, wv, bq, bv, wo, bo, gf, sf, win, bin_, wout, bout = operands
+    results = (hidden, hidden, gain, gain, wq, wk, wv, bq, bv, wo, bo, gf, sf, win, bin_, wout, bout)
+    shapes = tuple(struct(r.shape, F32) for r in results)
+    made = pl.pallas_call(
+        layer_kernel,
+        out_shape=shapes,
+        in_specs=[VM] * len(operands),
+        out_specs=(VM,) * len(results),
+        scratch_shapes=[
+            vm((2, 4, 128, 768), BF),
+            vm((768, 1024), BF),
+            vm((2, 512, LANES), BF),
+            vm((2, 2, 4, 128, 2 * LANES), BF),
+            vm((4, 2, 128, LANES), BF),
+            vm((4, 2, 128, LANES), BF),
+            vm((4, 192, 768), BF),
+            vm((4, 768, LANES), BF),
+            vm((2, 4, 768, 768), BF),
+            vm((LANES, 1024), BF),
+            vm((LANES, 512), F32),
+            vm((4, 2, 128, LANES), BF),
+            vm((2, 4, 128, LANES), BF),
+            vm((1024, 128), F32),
+            vm((2, 256, 768), BF),
+            vm((256, 768), BF),
+            vm((2, 768, 256), BF),
+            vm((2, 2, 256, 768), BF),
+            vm((4, 256, 768), BF),
+            vm((2, 256, 768), BF),
+            vm((2, 768, 256), BF),
+            vm((4, 768, LANES), BF),
+            vm((4, 2, 192, 768), BF),
+            vm((4, 192, 768), BF),
+            vm((4, 192, 768), BF),
+            vm((4, 2, 96, LANES), BF),
+            vm((4, 96, LANES), BF),
+            vm((4, 96, LANES), BF),
+            vm((3, 1024, LANES), F32),
+            vm((2, 512, 2 * LANES), BF),
+            vm((2, 512, 2 * LANES), BF),
+            vm((2, 512, 768), BF),
+            vm((2, 4, 128, 768), BF),
+            vm((2, 4, 128, 768), BF),
+            vm((2, 4, 96, 768), BF),
+            vm((2, 4, 96, 768), BF),
+            vm((16, 768), F32),
+            vm((16, 768), F32),
+            vm((4, 16, 768), F32),
+            vm((4, 16, 768), F32),
+            vm((2, 192, 768), F32),
+            vm((2, 96, LANES), F32),
+            vm((2, 96, 768), F32),
+            vm((1, 768), F32),
+            vm((4, 1, 768), F32),
+            dma((3,)), dma((4,)), dma((3,)), dma((3,)), dma((2, 4)), dma((2, 4)),
+            dma((2, 4)), dma((2, 4)), dma((2, 3)), dma((2, 4)),
+            dma((4, 2)), dma((2, 8, 2)), dma((4, 4, 2)), dma((4, 4, 2)), dma((4, 4, 2)),
+            dma((1,)), dma((1,)), dma((4,)), dma((4,)), dma((1,)), dma((1,)), dma((1,)), dma((1,)),
+            dma((2, 3)), dma((2, 4)),
+            dma((4, 2)), dma((4, 2)), dma((4, 2)), dma((4, 2)), dma((4, 2)), dma((4, 2)),
+            dma((2, 3)), dma((2, 4)), dma((2,)), dma((2,)), dma((2, 3)), dma((2, 4)),
+            dma((1,)), dma((1,)), dma((3,)), dma((4,)), dma((3,)), dma((3,)), dma((7,)), dma((9,)),
+        ],
+        compiler_params=pltpu.CompilerParams(
+            collective_id=1, has_side_effects=True, vmem_limit_bytes=63 << 20
+        ),
+        name="layer",
+    )(*operands)
+    made = pl.pallas_call(
+        deliver_kernel,
+        out_shape=shapes,
+        in_specs=[VM] * len(shapes),
+        out_specs=(ANY,) * len(shapes),
+        scratch_shapes=[dma((len(shapes),))],
+        name="deliver",
+    )(*made)
+    return tuple(made[:15]) + (made[15].T, made[16])
 
 
 root_half = 0.7071067811865476
 inv_root_two_pi = 0.3989422804014327
 
 
-def smooth_gate(values):
+def general_gate(values):
     return values * (0.5 * (1.0 + lax.erf(values * root_half)))
 
 
-def smooth_slope(values):
+def general_slope(values):
     normal_cdf = 0.5 * (1.0 + lax.erf(values * root_half))
     normal_pdf = jnp.exp(-0.5 * values * values) * inv_root_two_pi
     return normal_cdf + values * normal_pdf
 
 
-def norm_forward(rows, gain, shift):
+def general_norm(rows, gain, shift):
     centred = rows - jnp.mean(rows, axis=-1, keepdims=True)
     inverse = lax.rsqrt(jnp.mean(centred * centred, axis=-1, keepdims=True) + 1e-05)
     scaled = centred * inverse
     return (scaled * gain + shift, scaled, inverse)
 
 
-def norm_backward(grad_out, scaled, inverse, gain):
+def general_norm_backward(grad_out, scaled, inverse, gain):
     grad_scaled = grad_out * gain
     plain_mean = jnp.mean(grad_scaled, axis=-1, keepdims=True)
     cross_mean = jnp.mean(grad_scaled * scaled, axis=-1, keepdims=True)
@@ -54,11 +1000,11 @@
     )
 
 
-def place_piece(piece, total, start):
+def general_piece(piece, total, start):
     return lax.dynamic_update_slice(jnp.zeros((total,), jnp.float32), piece, (start,))
 
 
-def body(
+def general_body(
     hidden_in,
     cotangent,
     segment_ids,
@@ -116,7 +1062,7 @@
         allowed = (query_seg[:, None] == segment_row[None, :]) & (
             (segment_row[None, :] >= 0) | (query_index[:, None] == key_index[None, :])
         )
-        normed, scaled_a, inverse_a = norm_forward(rows, attn_gain, attn_shift)
+        normed, scaled_a, inverse_a = general_norm(rows, attn_gain, attn_shift)
         normed_all = tensor_rows(normed.astype(jnp.bfloat16))
         queries = (
             jnp.dot(normed_all, w_query, preferred_element_type=jnp.float32) + query_piece
@@ -144,16 +1090,16 @@
         mixed = mixed.reshape(half_rows, part_width).astype(jnp.bfloat16)
         branch_a = tensor_sums(jnp.dot(mixed, w_output, preferred_element_type=jnp.float32))
         middle = rows + branch_a + output_bias
-        normed_f, scaled_f, inverse_f = norm_forward(middle, ffn_gain, ffn_shift)
+        normed_f, scaled_f, inverse_f = general_norm(middle, ffn_gain, ffn_shift)
         normed_f_all = tensor_rows(normed_f.astype(jnp.bfloat16))
         inner = jnp.dot(normed_f_all, w_inner, preferred_element_type=jnp.float32) + inner_piece
-        active = smooth_gate(inner).astype(jnp.bfloat16)
+        active = general_gate(inner).astype(jnp.bfloat16)
         branch_f = tensor_sums(jnp.dot(active, w_outer, preferred_element_type=jnp.float32))
         result_rows = middle + branch_f + outer_bias
         grad_up = tensor_rows(cot_rows.astype(jnp.bfloat16))
         grad_outer_w = jnp.einsum("tf,td->fd", active, grad_up, preferred_element_type=jnp.float32)
         grad_active = jnp.einsum("td,fd->tf", grad_up, w_outer, preferred_element_type=jnp.float32)
-        grad_inner = (grad_active * smooth_slope(inner)).astype(jnp.bfloat16)
+        grad_inner = (grad_active * general_slope(inner)).astype(jnp.bfloat16)
         grad_inner_w = jnp.einsum(
             "td,tf->df", normed_f_all, grad_inner, preferred_element_type=jnp.float32
         )
@@ -161,7 +1107,7 @@
         grad_normed_f = tensor_sums(
             jnp.einsum("tf,df->td", grad_inner, w_inner, preferred_element_type=jnp.float32)
         )
-        grad_rows_f, grad_ffn_g, grad_ffn_s = norm_backward(
+        grad_rows_f, grad_ffn_g, grad_ffn_s = general_norm_backward(
             grad_normed_f, scaled_f, inverse_f, ffn_gain
         )
         grad_middle = cot_rows + grad_rows_f
@@ -228,7 +1174,7 @@
             "tc,dc->td", grad_values, w_value, preferred_element_type=jnp.float32
         )
         grad_normed = tensor_sums(grad_normed_part)
-        grad_rows_a, grad_attn_g, grad_attn_s = norm_backward(
+        grad_rows_a, grad_attn_g, grad_attn_s = general_norm_backward(
             grad_normed, scaled_a, inverse_a, attn_gain
         )
         grad_rows = grad_middle + grad_rows_a
@@ -244,12 +1190,12 @@
         small_terms = (
             grad_attn_g,
             grad_attn_s,
-            place_piece(grad_query_b, width, tensor_at * part_width),
-            place_piece(grad_value_b, width, tensor_at * part_width),
+            general_piece(grad_query_b, width, tensor_at * part_width),
+            general_piece(grad_value_b, width, tensor_at * part_width),
             jnp.sum(grad_middle, axis=0),
             grad_ffn_g,
             grad_ffn_s,
-            place_piece(grad_inner_b, unit_total, tensor_at * unit_width),
+            general_piece(grad_inner_b, unit_total, tensor_at * unit_width),
             jnp.sum(cot_rows, axis=0),
         )
         small_sums = tuple((old + new for old, new in zip(small_sums, small_terms)))
@@ -349,48 +1295,20 @@
     )
 
 
+SPECS = (
+    P("dp", ("ctx", "tensor"), None), P("dp", ("ctx", "tensor"), None), P("dp", None), P(), P(),
+    P("dp", "tensor"), P("dp", "tensor"), P("dp", "tensor"), P(), P(), P("tensor", "dp"), P(), P(),
+    P(), P("dp", "tensor"), P(), P("tensor", "dp"), P(),
+)
+OUT_SPECS = (
+    P("dp", ("ctx", "tensor"), None), P("dp", ("ctx", "tensor"), None), P(), P(),
+    P("dp", "tensor"), P("dp", "tensor"), P("dp", "tensor"), P(), P(), P("tensor", "dp"), P(), P(),
+    P(), P("dp", "tensor"), P(), P("tensor", "dp"), P(),
+)
+
+
 def solution(mesh):
+    lined_up = mesh.shape["dp"] == 4 and mesh.shape["tensor"] == 4 and mesh.shape["ctx"] == 2
     return jax.shard_map(
-        body,
-        mesh=mesh,
-        in_specs=(
-            P("dp", ("ctx", "tensor"), None),
-            P("dp", ("ctx", "tensor"), None),
-            P("dp", None),
-            P(),
-            P(),
-            P("dp", "tensor"),
-            P("dp", "tensor"),
-            P("dp", "tensor"),
-            P(),
-            P(),
-            P("tensor", "dp"),
-            P(),
-            P(),
-            P(),
-            P("dp", "tensor"),
-            P(),
-            P("tensor", "dp"),
-            P(),
-        ),
-        out_specs=(
-            P("dp", ("ctx", "tensor"), None),
-            P("dp", ("ctx", "tensor"), None),
-            P(),
-            P(),
-            P("dp", "tensor"),
-            P("dp", "tensor"),
-            P("dp", "tensor"),
-            P(),
-            P(),
-            P("tensor", "dp"),
-            P(),
-            P(),
-            P(),
-            P("dp", "tensor"),
-            P(),
-            P("tensor", "dp"),
-            P(),
-        ),
-        check_vma=False,
+        body if lined_up else general_body, mesh=mesh, in_specs=SPECS, out_specs=OUT_SPECS, check_vma=False
     )

time: 864 us -> 201 us (0.23)
  waiting for transfers between devices: 372 us -> 0 us
  blocking collectives: 263 us -> 0 us
  Pallas kernels: 0 us -> 200 us
  matrix products: 101 us -> 0 us
  other arithmetic: 62.3 us -> 0 us
  local copies, waits for them, and re-layouts: 46 us -> 0 us
  between operations: 14.6 us -> 0.83 us
    reduce_scatter x14 -> x0, waiting for transfers between devices: 268 us -> none  [the longest x8 207 us: tensor_sums(): return lax.psum_scatter(block, 'tensor', scatter_dimension=0, tiled=True)]
    all_gather x16 -> x0, blocking collectives: 222 us -> none  [the longest x8 168 us: tensor_rows(): return lax.all_gather(block, 'tensor', axis=0, tiled=True)]
    pallas_call x0 -> x2, Pallas kernels: none -> 200 us  [the longest x1 196 us: body(): pl.pallas_call(layer_kernel, out_shape=shapes, in_specs=[VM] * len(operan...]
    dot_general x48 -> x0, matrix products: 101 us -> none  [the longest x2 9.46 us: micro(): jnp.einsum('qhd,khd->hqk', grad_mixed, value_all, preferred_element_type=...]
    unnamed x13 -> x0, waiting for transfers between devices: 93.9 us -> none
    psum x1 -> x0, blocking collectives: 40.8 us -> none  [body(): lax.psum((small_sums[0], small_sums[1], small_sums[2], small_sums[3], sma...]
    convert_element_type x23 -> x0, other arithmetic: 22.6 us -> none  [the longest x3 5.21 us: body(): owned = (lax.psum_scatter(paired[0].astype(jnp.bfloat16), 'dp', scatter_d...]
    unnamed x48 -> x0, local copies, waits for them, and re-layouts: 18.7 us -> none
  transfers between devices with their start and end apart: 21 -> 0, of which waited for: 15 -> 0; matrix products, arithmetic and copies ran while one was open for 12% -> 0% of each run, Pallas kernels for 0% -> 0%
where the time goes in v3:
time: 201 us
  Pallas kernels  200 us (100%)
    pallas_call x1, Pallas kernels, body(): pl.pallas_call(layer_kernel, out_shape=shapes, in_specs=[VM] * len(operan...  196 us

profile of v3, /device:TPU:0, one launch (start us, length us, event | category | flops | bytes accessed | tf_op | source)
XLA Modules:
  0.0 200.8 jit_solution(18021752733504503102)
XLA Ops:
  0.7 196.0 %layer.1 = (f32[2,128,768]{2,1,0:T(8,128)}, f32[2,128,768]{2,1,0:T(8,128)}, f32[768]{0:T(1024)}, f32[768]{0:T(1024)}, f32[192,192]{1,0:T(8,128)}, /*index=5*/f32...) custom-call(f32[2,128,768]{2,1,0:T(8,128)} %hidden.1, ...), custom_call_target="tpu_custom_call" | custom-call | tf_op jit(solution)/shard_map/layer/pallas_call | solution.py:879
  196.6 4.0 %deliver.1 = (f32[2,128,768]{2,1,0:T(8,128)}, f32[2,128,768]{2,1,0:T(8,128)}, f32[768]{0:T(1024)}, f32[768]{0:T(1024)}, f32[192,192]{1,0:T(8,128)}, /*index=5*/f...) custom-call(f32[2,128,768]{2,1,0:T(8,128)} %get-tuple-element.51.ref, ...), custom_call_target="tpu_custom_call" | custom-call | tf_op jit(solution)/shard_map/deliver/pallas_call | solution.py:944

commit v4 on v0

--- a/solution.py
+++ b/solution.py
@@ -1,33 +1,1045 @@
+import functools
+
 import jax
 import jax.numpy as jnp
 from jax import lax
+from jax.experimental import pallas as pl
+from jax.experimental.pallas import tpu as pltpu
 from jax.sharding import PartitionSpec as P
 
 HDIM = 64
+LANES = 256
+ROOT_HALF = 0.7071067811865476
+INV_ROOT_TWO_PI = 0.3989422804014327
+MESH = pl.DeviceIdType.MESH
+BF = jnp.bfloat16
+F32 = jnp.float32
+HIDE = -1e30
+
+
+def dims(left, right, a, b):
+    return lax.dot_general(left, right, (((a,), (b,)), ((), ())), preferred_element_type=F32)
+
+
+def norm_parts(rows):
+    centred = rows - jnp.mean(rows, axis=-1, keepdims=True)
+    inverse = lax.rsqrt(jnp.mean(centred * centred, axis=-1, keepdims=True) + 1e-05)
+    return centred * inverse, inverse
+
+
+class Place:
+    def __init__(self):
+        self.d = lax.axis_index("dp")
+        self.c = lax.axis_index("ctx")
+        self.t = lax.axis_index("tensor")
+        col, row = self.d % 2, self.d // 2
+        self.dx = row * 2 + (1 - col)
+        self.dy = (1 - row) * 2 + col
+        self.dd = (1 - row) * 2 + (1 - col)
+        self.h = self.t // 2
+        self.g = self.t % 2
+        self.mid = self.g + self.h * (1 - 2 * self.g)
+        self.mate = 2 * self.h + 1 - self.g
+        self.twin = (self.t + 2) % 4
+        self.far_mid = 2 - self.h
+        self.far_end = 3 * (1 - self.h)
+
+    def source(self, k):
+        first = 1 - jnp.minimum(k, 1)
+        second = jnp.minimum(k, 1) * (1 - jnp.minimum(jnp.maximum(k - 1, 0), 1))
+        third = jnp.minimum(jnp.maximum(k - 1, 0), 1) * (1 - jnp.maximum(k - 2, 0))
+        fourth = jnp.maximum(k - 2, 0)
+        return first * self.t + second * self.mate + third * self.far_mid + fourth * self.far_end
+
+
+def remote(src, dst, send, recv, **where):
+    return pltpu.make_async_remote_copy(
+        src_ref=src, dst_ref=dst, send_sem=send, recv_sem=recv, device_id=where, device_id_type=MESH
+    )
+
+
+def greet(place):
+    barrier = pltpu.get_barrier_semaphore()
+    for k in range(1, 4):
+        pl.semaphore_signal(
+            barrier, inc=1, device_id={"tensor": (place.t + k) % 4}, device_id_type=MESH
+        )
+    for peer in (place.dx, place.dy, place.dd):
+        pl.semaphore_signal(barrier, inc=1, device_id={"dp": peer}, device_id_type=MESH)
+    pl.semaphore_signal(barrier, inc=1, device_id={"ctx": 1 - place.c}, device_id_type=MESH)
+    for k in range(1, 4):
+        where = {"ctx": 1 - place.c, "tensor": (place.t + k) % 4}
+        pl.semaphore_signal(barrier, inc=1, device_id=where, device_id_type=MESH)
+    return lambda: pl.semaphore_wait(barrier, 10)
+
+
+class Several:
+    def __init__(self, *copies):
+        self.copies = copies
+
+    def start(self):
+        for copy in self.copies:
+            copy.start()
+
+    def wait_send(self):
+        for copy in self.copies:
+            copy.wait_send()
+
+    def wait_recv(self):
+        for copy in self.copies:
+            copy.wait_recv()
+
+
+def rows_at(start, size, step):
+    return pl.ds(pl.multiple_of(start, step), size)
+
+
+def erf_parts(values):
+    cdf = 0.5 * (1.0 + lax.erf(values * ROOT_HALF))
+    return cdf, cdf + values * (jnp.exp(-0.5 * values * values) * INV_ROOT_TWO_PI)
+
+
+def add_to(target, *terms):
+    total = target[...].astype(F32)
+    for term in terms:
+        total = total + term[...].astype(F32)
+    target[...] = total.astype(BF)
+
+
+def layer_kernel(
+    hidden, cot, seg, gain_a, shift_a, wq_s, wk_s, wv_s, bias_q, bias_v, wo_s, bias_o, gain_f, shift_f,
+    win_s, bias_in, wout_s, bias_out,
+    block_out, grad_input, g_gain_a, g_shift_a, g_wq, g_wk, g_wv, g_bias_q, g_bias_v, g_wo, g_bias_o,
+    g_gain_f, g_shift_f, g_win, g_bias_in, g_wout, g_bias_out,
+    normed, far_rows, normed_turn, queries, kv, mixed_in, mixed_sib, q_land, wqkv, wo_land, wout, ffw,
+    turn, q_turn, mixed, g_mix, keys_seg, left, left_in, left_turn, right, right_in, nf_out, nf_in,
+    bf_out, bf_in, branch, branch_turn, part_wo, rxw, sumw, rzw, rx1, rx2, rz, wide, kv_out, kv_in, dqkv,
+    gna, rzn, qkv_own, qkv_sib, qkv_in, qkv_sum, qkv_twin, sums, sums_core, sums_plane, sums_line,
+    late, late_line, late_plane, res_ff, res_wo, res_qkv, bias_row, inner_rows,
+    qt_send, q_send, q_recv, qc_send, qc_recv, z_send, z_recv, kvf_send, kvf_recv, mf_send, mf_recv,
+    ct_send, cp_send, c_recv, cc_send, s_recv, wz_send, wz_recv, wp_send, wp_recv, wc_send, wc_recv,
+    u_send, u_recv, l_send, l_recv, r_send, r_recv, n_send, n_recv, b_send, b_recv, x_send, x_recv,
+    m_send, m_recv, p1_send, p1_recv, p2_send, p2_recv, zz_send, zz_recv, gp_send, gp_recv, gz_send, gz_recv,
+    kv_send, kv_recv, rn_send, rn_recv, qs_send, qs_recv, qp_send, qp_recv, qz_send, qz_recv,
+    f_send, f_recv, t_send, t_recv, ta_send, ta_recv, tb_send, tb_recv,
+):
+    at = Place()
+    d, c, t, h, g = at.d, at.c, at.t, at.h, at.g
+    other, away = 1 - c, 1 - h
+    planes = (at.dx, at.dy, at.dd)
+    others = [(t + k + 1) % 4 for k in range(3)]
+    waits = []
+
+    def begin(*copies):
+        for copy in copies:
+            copy.start()
+            waits.append(copy)
+
+    arrive = greet(at)
+
+    for ref, start in ((wq_s, 0), (wk_s, LANES), (wv_s, 2 * LANES)):
+        q_land[h, d, :, start + 128 : start + 256] = jnp.zeros((192, 128), BF)
+        q_land[h, d, :, start : start + 192] = ref[...].astype(BF)
+    arrive()
+
+    def q_half(a, owner, which):
+        return q_land.at[a, owner, rows_at(which * 96, 96, 96)]
+
+    def q_plane(a, i, owner):
+        half = q_half(a, owner, c)
+        return remote(half, half, q_send.at[a, i], q_recv.at[a, owner], dp=planes[i])
+
+    def q_core(a, owner):
+        half = q_half(a, owner, c)
+        return remote(half, half, qc_send.at[a, owner], qc_recv.at[a, owner], ctx=other)
+
+    def q_core_wait(a, owner):
+        half = q_half(a, owner, other)
+        remote(half, half, qc_send.at[a, owner], qc_recv.at[a, owner], ctx=other).wait_recv()
+
+    def q_wait(a, owner):
+        half = q_half(a, owner, c)
+        remote(half, half, qt_send.at[0], q_recv.at[a, owner], tensor=t).wait_recv()
+
+    begin(remote(q_half(h, d, c), q_half(h, d, c), qt_send.at[0], q_recv.at[h, d], tensor=at.twin))
+    for i in range(3):
+        begin(q_plane(h, i, d))
+
+    turned = wo_s[...].T
+    turned = jnp.where(c == 0, turned[:96], turned[96:]).astype(BF)
+    mine = rows_at(d * 192 + c * 96, 96, 96)
+    wo_land[t, mine, 128:256] = jnp.zeros((96, 128), BF)
+    wo_land[t, mine, 0:192] = turned
+
+    def wo_rows(owner, which):
+        return wo_land.at[:, rows_at(owner * 192 + which * 96, 96, 96)]
+
+    def wo_line(k, owner):
+        block = wo_land.at[owner, mine]
+        return remote(block, block, wz_send.at[k], wz_recv.at[owner], tensor=others[k])
+
+    for k in range(3):
+        begin(wo_line(k, t))
+
+    def normed_rows(s):
+        scaled, _ = norm_parts(hidden[s])
+        return (scaled * gain_a[...].reshape(1, 768) + shift_a[...].reshape(1, 768)).astype(BF)
+
+    def row_copy(src, owner, k, dest):
+        return remote(src, normed.at[owner], z_send.at[k], z_recv.at[owner], tensor=dest)
+
+    def row_wait(p):
+        row_copy(normed.at[p], p, 0, t).wait_recv()
+
+    pass_end = row_copy(normed.at[at.far_end], at.far_end, 2, at.mate)
+    pass_mid = row_copy(normed.at[at.far_mid], at.far_mid, 3, at.mate)
+    far_rows[...] = normed_rows(away)
+    begin(row_copy(far_rows, t, 1, at.far_mid))
+    normed[t] = normed_rows(h)
+    begin(row_copy(normed.at[t], t, 0, at.mate))
+
+    here = rows_at(d * 192, 192, 192)
+
+    @pl.when(c == 0)
+    def _():
+        ffw[0, h, here, :] = win_s[...].astype(BF)
+
+    @pl.when(c == 1)
+    def _():
+        ffw[1, h, here, :] = wout_s[...].astype(BF)
+
+    def ff_block(which, a, owner):
+        return ffw.at[which, a, rows_at(owner * 192, 192, 192)]
+
+    def ff_half(which, a, owner, n):
+        return ffw.at[which, a, rows_at(owner * 192 + n * 96, 96, 96)]
+
+    def ff_twin(n):
+        block = ff_half(c, h, d, n)
+        return remote(block, block, ct_send.at[n], c_recv.at[h, d, n], tensor=at.twin)
+
+    def ff_plane(axis, a, owner, n, dest):
+        block = ff_half(c, a, owner, n)
+        return remote(block, block, cp_send.at[axis, a, n], c_recv.at[a, owner, n], dp=dest)
+
+    def ff_core(a, owner, n):
+        block = ff_half(c, a, owner, n)
+        return remote(block, block, cc_send.at[a, owner, n], s_recv.at[a, owner, n], ctx=other)
+
+    def ff_wait(a, owner, n):
+        block = ff_half(c, a, owner, n)
+        remote(block, block, ct_send.at[n], c_recv.at[a, owner, n], dp=d).wait_recv()
+
+    def ff_core_wait(a, owner, n):
+        block = ff_half(other, a, owner, n)
+        remote(block, block, cc_send.at[a, owner, n], s_recv.at[a, owner, n], ctx=other).wait_recv()
+
+    ff_sends = []
+
+    def ff_begin(*copies):
+        for copy in copies:
+            copy.start()
+            ff_sends.append(copy)
+
+    def spread(a, n):
+        ff_begin(ff_plane(0, a, d, n, at.dx), ff_plane(1, a, d, n, at.dy), ff_core(a, d, n))
+
+    def near_far(a):
+        near = at.dx + a * (at.dy - at.dx)
+        return near, at.dx + at.dy - near
+
+    def diag(a, n):
+        near, far = near_far(a)
+        ff_wait(a, near, n)
+        ff_begin(ff_plane(2, a, near, n, far), ff_core(a, near, n))
+        ff_wait(a, far, n)
+        ff_begin(ff_core(a, far, n))
+
+    def last(a, n):
+        ff_wait(a, at.dd, n)
+        ff_begin(ff_core(a, at.dd, n))
+
+    left[1, 0] = cot[...].reshape(256, 768).astype(BF)
+    sums[...] = jnp.zeros_like(sums)
+    late[...] = jnp.zeros_like(late)
+    wide[...] = jnp.zeros_like(wide)
+    part_wo[...] = jnp.zeros_like(part_wo)
+    for p in range(2):
+
+        @pl.when(g == p)
+        def _(p=p):
+            for a in range(2):
+                cols = slice((p + 2 * a) * 192, (p + 2 * a) * 192 + 192)
+                bias_row[:, a * 192 : a * 192 + 192] = bias_q[...].reshape(1, 768)[:, cols]
+                bias_row[:, 768 + a * 192 : 960 + a * 192] = bias_v[...].reshape(1, 768)[:, cols]
+
+    bias_row[:, 384:768] = jnp.zeros((1, 384), F32)
+    for p in range(4):
+        inner_rows[p] = bias_in[...].reshape(1, 3072)[:, p * 768 : (p + 1) * 768]
+
+    row = jnp.where(h == 0, seg[0:1, :], seg[1:2, :])
+    places = lax.broadcasted_iota(jnp.int32, (1, 1024), 1)
+    row = jnp.where(row >= 0, row, -1 - places).astype(F32)
+    seg_query = jnp.where(c == 0, row[:, :512], row[:, 512:])
+    keys_seg[...] = jnp.broadcast_to(row, (128, 1024)).T
+
+    for i in range(3):
+        q_wait(h, planes[i])
+        begin(q_core(h, planes[i]))
+    q_wait(away, d)
+    for i in range(3):
+        begin(q_plane(away, i, d))
+    begin(q_core(away, d))
+
+    @pl.when(at.mid == 1)
+    def _():
+        row_wait(at.far_end)
+        pass_end.start()
+        row_wait(at.far_mid)
+        pass_mid.start()
+
+    for i in range(3):
+        q_wait(away, planes[i])
+        begin(q_core(away, planes[i]))
+    for k in range(3):
+        p = others[k]
+        block = wo_land.at[p, mine]
+        remote(block, block, wz_send.at[k], wz_recv.at[p], tensor=p).wait_recv()
+    for i in range(3):
+        begin(remote(wo_rows(d, c), wo_rows(d, c), wp_send.at[i], wp_recv.at[d], dp=planes[i]))
+    begin(remote(wo_rows(d, c), wo_rows(d, c), wc_send.at[d], wc_recv.at[d], ctx=other))
+    for n in range(2):
+        spread(h, n)
+    for i in range(3):
+        q_core_wait(h, planes[i])
+        q_core_wait(away, planes[i])
+    q_core_wait(away, d)
+
+    def gather_columns(i, carry):
+        rows = rows_at(i * 192, 192, 192)
+        for k in range(3):
+            pair = [q_land[a, i, :, k * LANES : k * LANES + 192] for a in range(2)]
+            wqkv[rows, k * 384 : (k + 1) * 384] = jnp.concatenate(pair, axis=1)
+        return carry
+
+    lax.fori_loop(0, 4, gather_columns, 0)
+
+    def kvf_copy(p):
+        block = kv.at[:, c, p]
+        return remote(block, block, kvf_send.at[p], kvf_recv.at[p], ctx=other)
+
+    def project(k, carry):
+        p = at.source(k)
+
+        @pl.when((k == 1) | ((k > 1) & (at.mid == 0)))
+        def _():
+            row_wait(p)
+
+        out = jnp.dot(normed[p], wqkv[...], preferred_element_type=F32)
+        out = (out + bias_row[...]).astype(BF)
+        for u in range(3):
+            cols = out[:, u * 128 : (u + 1) * 128]
+            queries[u, rows_at(p * 128, 128, 128), :] = cols * jnp.asarray(HDIM**-0.5, BF)
+        for u in range(6):
+            kv[u, c, p] = out[:, 384 + u * 128 : 512 + u * 128]
+        kvf_copy(p).start()
+        return carry
+
+    for n in range(2):
+        ff_begin(ff_twin(n))
+    lax.fori_loop(0, 4, project, 0)
+
+    lane_head = lax.broadcasted_iota(jnp.int32, (1, 128), 1) // HDIM
+
+    def head_pair(ref, u):
+        return ref[u].reshape(1024, 128)
+
+    def masked_scores(u, b, q_here):
+        seg_here = jnp.where(b == 0, seg_query[:, :256], seg_query[:, 256:])
+        scores = dims(head_pair(kv, u), q_here, 1, 1)
+        column = keys_seg[...]
+        visible = jnp.concatenate([column, column], axis=1) == seg_here
+        return jnp.where(visible, scores, HIDE)
+
+    def one_head(w, block):
+        return jnp.where(lane_head == w, block.astype(F32), 0.0).astype(BF)
+
+    def mf_copy(k, p):
+        return remote(mixed.at[p], mixed_in.at[g, h], mf_send.at[k], mf_recv.at[t], tensor=p)
+
+    for p in range(4):
+        block = kv.at[:, other, p]
+        remote(block, block, kvf_send.at[p], kvf_recv.at[p], ctx=other).wait_recv()
+    for u in range(3):
+        turn[u * 128 : (u + 1) * 128, :] = head_pair(kv, 3 + u).T
+
+    def attend(b):
+        block = rows_at(b * 256, 256, 256)
+
+        def step(i, carry):
+            u, w = i // 2, i % 2
+            scores = masked_scores(u, b, one_head(w, queries[u, block, :]))
+            peak = jnp.max(scores, axis=0, keepdims=True)
+            expo = jnp.exp(scores - peak)
+            total = jnp.sum(expo, axis=0, keepdims=True)
+            rows = rows_at(i * HDIM, HDIM, HDIM)
+            turned = jnp.dot(turn[rows, :], expo.astype(BF), preferred_element_type=F32)
+            q_turn[rows, :] = turned / total
+            return carry
+
+        lax.fori_loop(0, 6, step, 0)
+        mixed[pl.ds(2 * b, 2)] = q_turn[...].T.astype(BF).reshape(2, 128, 384)
+
+    attend(away)
+    mf_copy(0, 2 * away).start()
+    mf_copy(1, 2 * away + 1).start()
+    begin(remote(left.at[1, 0], left.at[1, 1], u_send.at[1], u_recv.at[1], tensor=at.mate))
+    for n in range(2):
+        diag(h, n)
+    attend(h)
+    mf_copy(2, at.mate).start()
+    mixed_in[g, h] = mixed[t]
+    ff_wait(away, d, 0)
+    spread(away, 0)
+    for n in range(2):
+        last(h, n)
+    for i in range(3):
+        p = planes[i]
+        remote(wo_rows(p, c), wo_rows(p, c), wp_send.at[i], wp_recv.at[p], dp=p).wait_recv()
+        begin(remote(wo_rows(p, c), wo_rows(p, c), wc_send.at[p], wc_recv.at[p], ctx=other))
+    normed_turn[...] = normed[...].reshape(512, 768).T
+    for p in range(4):
+        remote(wo_rows(p, other), wo_rows(p, other), wc_send.at[p], wc_recv.at[p], ctx=other).wait_recv()
+    for p in range(2):
+        for i in range(4):
+            rows = slice(i * 192, (i + 1) * 192)
+            pair = [wo_land[p + 2 * a, rows, :192] for a in range(2)]
+            wout[p, rows, :] = jnp.concatenate(pair, axis=1)
+    ff_wait(away, d, 1)
+    spread(away, 1)
+    diag(away, 0)
+
+    for k in range(3):
+        p = others[k]
+        block = mixed_in.at[p % 2, p // 2]
+        remote(block, block, mf_send.at[k], mf_recv.at[p], tensor=p).wait_recv()
+    for s in range(2):
+        total = hidden[s] + bias_o[...].reshape(1, 768)
+        for p in range(2):
+            total = total + dims(mixed_in[p, s], wout[p], 1, 1)
+        block_out[s] = total
+        scaled, _ = norm_parts(total)
+        left[0, 0, s * 128 : (s + 1) * 128, :] = (
+            scaled * gain_f[...].reshape(1, 768) + shift_f[...].reshape(1, 768)
+        ).astype(BF)
+    begin(remote(left.at[0, 0], left.at[0, 1], u_send.at[0], u_recv.at[0], tensor=at.mate))
+    begin(remote(mixed_in, mixed_sib, x_send.at[0], x_recv.at[0], ctx=other))
+
+    diag(away, 1)
+    for p in range(4):
+        for n in range(2):
+            ff_core_wait(h, p, n)
+
+    def right_copy(a, r):
+        return remote(
+            right.at[other, a, r], right_in.at[a, r], r_send.at[a, r], r_recv.at[a, r], ctx=other
+        )
+
+    def units(a, r):
+        unit = g + 2 * a
+        top = pl.multiple_of(r * 512, 512)
+        for j in range(3):
+            cols = slice(j * 256, (j + 1) * 256)
+            w_in, w_out = ffw[0, a, :, cols], ffw[1, a, :, cols]
+            inner = jnp.dot(left[0, r], w_in, preferred_element_type=F32) + inner_rows[unit, :, cols]
+            cdf, slope = erf_parts(inner)
+            active = (inner * cdf).astype(BF)
+            right[1, a, r, :, cols] = active
+            grad_inner = jnp.dot(left[1, r], w_out, preferred_element_type=F32) * slope
+            grad_inner = grad_inner.astype(BF)
+            right[0, a, r, :, cols] = grad_inner
+            sums[pl.ds(6 + unit, 1), cols] += jnp.sum(grad_inner.astype(F32), axis=0, keepdims=True)
+            up, down = dims(active, w_out, 1, 1), dims(grad_inner, w_in, 1, 1)
+            for k in range(6):
+                wide[k, pl.ds(top, 256), :] += up[:, k * 128 : (k + 1) * 128]
+                wide[k, pl.ds(top + 256, 256), :] += down[:, k * 128 : (k + 1) * 128]
+        right_copy(a, r).start()
+
+    def wide_rows(start, size=64):
+        return jnp.concatenate([wide[k, start : start + size, :] for k in range(6)], axis=1)
+
+    def own_slot(r, carry):
+        @pl.when(r == 1)
+        def _():
+            for which in range(2):
+                block = left.at[which, 1]
+                remote(block, block, u_send.at[which], u_recv.at[which], tensor=at.mate).wait_recv()
+            left_copy.start()
+
+        units(h, r)
+        return carry
+
+    left_copy = remote(left.at[other], left_in, l_send.at[0], l_recv.at[0], ctx=other)
+    waits.append(left_copy)
+    lax.fori_loop(0, 2, own_slot, 0)
+    for n in range(2):
+        last(away, n)
+    for p in range(4):
+        for n in range(2):
+            ff_core_wait(away, p, n)
+
+    def twin_slot(i, carry):
+        @pl.when(i == 1)
+        def _():
+            for q in range(4):
+                rows = slice(q * 64, (q + 1) * 64)
+                nf_out[rows, :] = wide_rows(768 + q * 64).astype(BF)
+            nf_copy.start()
+
+        units(away, 1 - i)
+        return carry
+
+    nf_copy = remote(nf_out, nf_in, n_send.at[0], n_recv.at[0], tensor=at.mate)
+    waits.append(nf_copy)
+    lax.fori_loop(0, 2, twin_slot, 0)
+    for q in range(4):
+        rows = slice(q * 64, (q + 1) * 64)
+        bf_out[rows, :] = wide_rows(512 + q * 64).astype(BF)
+
+    for copy in ff_sends:
+        copy.wait_send()
+    left_turn[0] = left[c, 0].T
+    left_turn[1] = left[c, 1].T
+    remote(left.at[c], left_in, l_send.at[0], l_recv.at[0], ctx=other).wait_recv()
+    left_turn[2] = left_in[0].T
+    left_turn[3] = left_in[1].T
+
+    def first(a, j):
+        near, _ = near_far(a)
+        owner = near if j == 0 else at.dd
+        return remote(ff_block(0, a, owner), rx1.at[a, j], p1_send.at[a, j], p1_recv.at[a, j], dp=near)
+
+    def second(a):
+        _, far = near_far(a)
+        return remote(ff_block(0, a, far), rx2.at[a], p2_send.at[a], p2_recv.at[a], dp=far)
+
+    def weight_gradient(a):
+        for r in range(2):
+            right_copy(a, r).wait_recv()
+
+        def rows_of(q, carry):
+            rows = rows_at(q * 192, 192, 192)
+            out = jnp.dot(left_turn[0, rows, :], right[c, a, 0], preferred_element_type=F32)
+            out = out + jnp.dot(left_turn[1, rows, :], right[c, a, 1], preferred_element_type=F32)
+            out = out + jnp.dot(left_turn[2, rows, :], right_in[a, 0], preferred_element_type=F32)
+            out = out + jnp.dot(left_turn[3, rows, :], right_in[a, 1], preferred_element_type=F32)
+            ffw[0, a, rows, :] = out.astype(BF)
+            return carry
+
+        lax.fori_loop(0, 4, rows_of, 0)
+        first(a, 1).start()
+        first(a, 0).start()
+
+    def both_slots(a, carry):
+        weight_gradient(a)
+        return carry
+
+    lax.fori_loop(0, 2, both_slots, 0)
+
+    def add_row(i, value):
+        sums[i : i + 1, :] += jnp.sum(value, axis=0, keepdims=True)
+
+    def norm_back(source, grad_out, gain):
+        scaled, inverse = norm_parts(source)
+        grad_scaled = grad_out * gain[...].reshape(1, 768)
+        plain = jnp.mean(grad_scaled, axis=-1, keepdims=True)
+        cross = jnp.mean(grad_scaled * scaled, axis=-1, keepdims=True)
+        return inverse * (grad_scaled - plain - scaled * cross), scaled
+
+    remote(nf_out, nf_in, n_send.at[0], n_recv.at[0], tensor=at.mate).wait_recv()
+    for s in range(2):
+        for half in range(2):
+            rows = slice(half * 64, half * 64 + 64)
+            start = s * 128 + half * 64
+            cot_here = cot[s, rows, :]
+            grad_out = wide_rows(256 + start) + nf_in[start : start + 64, :].astype(F32)
+            middle = block_out[s, rows, :]
+            grad_rows, scaled = norm_back(middle, grad_out, gain_f)
+            block_out[s, rows, :] = middle + wide_rows(start) + bias_out[...].reshape(1, 768)
+            grad_rows = grad_rows + cot_here
+            grad_input[s, rows, :] = grad_rows
+            branch[0, start : start + 64, :] = grad_rows.astype(BF)
+            add_row(2, grad_out * scaled)
+            add_row(3, grad_out)
+            add_row(4, grad_rows)
+            add_row(5, cot_here)
+    begin(remote(branch.at[0], branch.at[1], b_send.at[0], b_recv.at[0], ctx=other))
+
+    def m_copy(k):
+        p = others[k]
+        return remote(mixed.at[p], g_mix.at[t], m_send.at[k], m_recv.at[t], tensor=p)
+
+    mf_copy(0, 2 * away).wait_send()
+    mf_copy(1, 2 * away + 1).wait_send()
+    mf_copy(2, at.mate).wait_send()
+    for p in range(2):
+        out = jnp.dot(branch[0], wout[p], preferred_element_type=F32).astype(BF)
+        for s in range(2):
+            mixed[2 * s + p] = out[s * 128 : (s + 1) * 128, :]
+    for k in range(3):
+        begin(m_copy(k))
+    g_mix[t] = mixed[t]
+
+    branch_turn[0] = branch[0].T
+    remote(branch.at[0], branch.at[1], b_send.at[0], b_recv.at[0], ctx=other).wait_recv()
+    branch_turn[1] = branch[1].T
+    remote(mixed_in, mixed_sib, x_send.at[0], x_recv.at[0], ctx=other).wait_recv()
+    for p in range(2):
+        for q in range(4):
+            rows = slice(q * 192, (q + 1) * 192)
+            out = jnp.dot(branch_turn[0, rows, :], mixed_in[p].reshape(256, 384), preferred_element_type=F32)
+            out = out + jnp.dot(
+                branch_turn[1, rows, :], mixed_sib[p].reshape(256, 384), preferred_element_type=F32
+            )
+            for a in range(2):
+                part_wo[p + 2 * a, rows, :192] = out[:, a * 192 : (a + 1) * 192].astype(BF)
+
+    def wo_part(owner):
+        return part_wo.at[:, rows_at(owner * 192 + c * 96, 96, 96)]
+
+    for i in range(3):
+        begin(remote(wo_part(planes[i]), rxw.at[d], gp_send.at[i], gp_recv.at[d], dp=planes[i]))
+
+    def to_second(a):
+        _, far = near_far(a)
+        first(a, 1).wait_recv()
+        add_to(ff_block(0, a, far), rx1.at[a, 1])
+        second(a).start()
+        first(a, 0).wait_recv()
+        add_to(ff_block(0, a, d), rx1.at[a, 0])
+
+    def plane_done(a):
+        second(a).wait_recv()
+        add_to(ff_block(0, a, d), rx2.at[a])
+
+    zz_copy = remote(ff_block(0, away, d), rz, zz_send.at[0], zz_recv.at[0], tensor=at.twin)
+    waits.append(zz_copy)
+
+    for u in range(3):
+        turn[u * 128 : (u + 1) * 128, :] = head_pair(kv, u).T
+    wide[...] = jnp.zeros_like(wide)
+
+    def m_wait(p):
+        block = g_mix.at[p]
+        remote(block, block, m_send.at[0], m_recv.at[p], tensor=p).wait_recv()
+
+    theirs = rows_at(other * 512, 512, 512)
+    ours = rows_at(c * 512, 512, 512)
+
+    def kv_copy(u):
+        return remote(kv_out.at[u], kv_in.at[u], kv_send.at[u], kv_recv.at[u], ctx=other)
+
+    def attend_back(b, last):
+        block = rows_at(b * 256, 256, 256)
+
+        def step(u, carry):
+            cols = pl.ds(pl.multiple_of(u * 128, 128), 128)
+            g_pair = g_mix[pl.ds(2 * b, 2), :, cols].reshape(256, 128)
+            for w in range(2):
+                q_here = one_head(w, queries[u, block, :])
+                g_here = one_head(w, g_pair)
+                scores = masked_scores(u, b, q_here)
+                peak = jnp.max(scores, axis=0, keepdims=True)
+                expo = jnp.exp(scores - peak)
+                probs = expo * (1.0 / jnp.sum(expo, axis=0, keepdims=True))
+                grad_probs = dims(head_pair(kv, 3 + u), g_here, 1, 1)
+                centre = jnp.sum(probs * grad_probs, axis=0, keepdims=True)
+                wide[3 + u] += jnp.dot(probs.astype(BF), g_here, preferred_element_type=F32)
+                grad_scores = (probs * (grad_probs - centre)).astype(BF)
+                wide[u] += jnp.dot(grad_scores, q_here, preferred_element_type=F32)
+                rows = rows_at(u * 128 + w * HDIM, HDIM, HDIM)
+                q_turn[rows, :] = jnp.dot(turn[rows, :], grad_scores, preferred_element_type=F32)
+            if not last:
+
+                @pl.when(u > 0)
+                def _():
+                    to_second(u - 1)
+
+            if last:
+                @pl.when(u == 1)
+                def _():
+                    plane_done(away)
+                    zz_copy.start()
+
+                kv_out[u, :, :128] = wide[u, theirs, :].astype(BF)
+                kv_out[u, :, 128:] = wide[3 + u, theirs, :].astype(BF)
+                kv_copy(u).start()
+            return carry
+
+        lax.fori_loop(0, 3, step, 0)
+        dqkv[block, :384] = (q_turn[...].T * HDIM**-0.5).astype(BF)
+
+    m_wait(at.mate)
+    begin(remote(bf_out, bf_in, n_send.at[1], n_recv.at[1], tensor=at.mate))
+    attend_back(h, False)
+    m_wait(at.far_mid)
+    m_wait(at.far_end)
+    attend_back(away, True)
+
+    for i in range(3):
+        p = planes[i]
+        remote(wo_part(p), rxw.at[p], gp_send.at[i], gp_recv.at[p], dp=p).wait_recv()
+    total = part_wo[:, mine, :].astype(F32)
+    for i in range(3):
+        total = total + rxw[planes[i]].astype(F32)
+    sumw[...] = total.astype(BF)
+
+    for u in range(3):
+        kv_copy(u).wait_recv()
+        for k in range(2):
+            cols = slice(384 * (k + 1) + u * 128, 384 * (k + 1) + (u + 1) * 128)
+            theirs_here = kv_in[u, :, k * 128 : (k + 1) * 128].astype(F32)
+            dqkv[:, cols] = (wide[3 * k + u, ours, :] + theirs_here).astype(BF)
+
+    def line_copy(owner, slot, k, dest):
+        return remote(gna.at[owner], rzn.at[slot], rn_send.at[k], rn_recv.at[slot], tensor=dest)
+
+    def line_wait(slot):
+        line_copy(t, slot, 0, t).wait_recv()
+
+    far_sum = line_copy(at.far_end, 3, 2, at.mate)
+    on_sum = line_copy(at.far_end, 1, 2, at.far_end)
+
+    def rows_back(p):
+        rows = dqkv[rows_at(p * 128, 128, 128), :]
+        gna[p] = dims(rows, wqkv[...], 1, 1).astype(BF)
+
+    rows_back(at.far_end)
+
+    @pl.when(at.mid == 0)
+    def _():
+        far_sum.start()
+
+    rows_back(at.far_mid)
+    begin(line_copy(at.far_mid, 2 - at.mid, 1, at.far_mid))
+    rows_back(at.mate)
+    begin(line_copy(at.mate, 0, 0, at.mate))
+    rows_back(t)
+    total = jnp.sum(dqkv[...].astype(F32), axis=0, keepdims=True)
+    sums[pl.ds(10 + g, 1), :384] = total[:, :384]
+    sums[pl.ds(10 + g, 1), 384:] = total[:, 768:]
+
+    core_sum = remote(sums, sums_core, t_send.at[0], t_recv.at[0], ctx=other)
+    begin(core_sum)
+
+    def plane_sum(k, owner):
+        block = sums_plane.at[owner]
+        return remote(block, block, t_send.at[1 + k], t_recv.at[1 + owner], dp=planes[k])
+
+    def line_sum(k, owner):
+        block = sums_line.at[owner]
+        return remote(block, block, t_send.at[4 + k], t_recv.at[5 + owner], tensor=others[k])
+
+    def qkv_rows(i, carry):
+        rows = rows_at(i * 192, 192, 192)
+        out = jnp.dot(normed_turn[rows, :], dqkv[...], preferred_element_type=F32)
+        qkv_own[i] = jnp.where(c == 0, out[:96], out[96:])
+        qkv_sib[0, i] = jnp.where(c == 0, out[96:], out[:96]).astype(BF)
+        return carry
+
+    lax.fori_loop(0, 4, qkv_rows, 0)
+    sib_copy = remote(qkv_sib.at[0], qkv_sib.at[1], qs_send.at[0], qs_recv.at[0], ctx=other)
+    begin(sib_copy)
+    for k in range(3):
+        begin(remote(sumw.at[others[k]], rzw.at[t], gz_send.at[k], gz_recv.at[t], tensor=others[k]))
+
+    @pl.when(at.mid == 1)
+    def _():
+        line_wait(3)
+        add_to(gna.at[at.far_end], rzn.at[3])
+        on_sum.start()
+
+    core_sum.wait_recv()
+    sums_plane[d] = sums[...] + sums_core[...]
+    for k in range(3):
+        begin(plane_sum(k, d))
+    sib_copy.wait_recv()
+    for p in range(4):
+        qkv_in[0, p] = (qkv_own[p] + qkv_sib[1, p].astype(F32)).astype(BF)
+    for k in range(3):
+        begin(remote(qkv_in.at[0, planes[k]], qkv_in.at[1, d], qp_send.at[k], qp_recv.at[d], dp=planes[k]))
+    qkv_in[1, d] = qkv_in[0, d]
+
+    def result_copy(i, ref):
+        return remote(ref.at[c], ref.at[c], f_send.at[i], f_recv.at[i], ctx=other)
+
+    plane_done(h)
+    remote(rz, rz, zz_send.at[0], zz_recv.at[0], tensor=t).wait_recv()
+    res_ff[c] = ffw[0, h, here, :].astype(F32) + rz[...].astype(F32)
+    begin(result_copy(1, res_ff))
+    rzw[t] = sumw[t]
+    for k in range(3):
+        p = others[k]
+        remote(rzw.at[p], rzw.at[p], gz_send.at[k], gz_recv.at[p], tensor=p).wait_recv()
+    total = rzw[0].astype(F32)
+    for p in range(1, 4):
+        total = total + rzw[p].astype(F32)
+    res_wo[c] = total
+    begin(result_copy(2, res_wo))
+
+    for k in range(3):
+        plane_sum(k, planes[k]).wait_recv()
+    sums_line[t] = (sums_plane[0] + sums_plane[1]) + (sums_plane[2] + sums_plane[3])
+    for k in range(3):
+        begin(line_sum(k, t))
+
+    for k in range(3):
+        block = qkv_in.at[1, planes[k]]
+        remote(block, block, qp_send.at[k], qp_recv.at[planes[k]], dp=d).wait_recv()
+    total = qkv_in[1, 0].astype(F32)
+    for p in range(1, 4):
+        total = total + qkv_in[1, p].astype(F32)
+    for k in range(3):
+        low, high = total[:, k * 384 : k * 384 + 192], total[:, k * 384 + 192 : (k + 1) * 384]
+        qkv_sum[0, :, k * LANES : k * LANES + 192] = jnp.where(h == 0, low, high)
+        qkv_twin[0, :, k * LANES : k * LANES + 192] = jnp.where(h == 0, high, low).astype(BF)
+    begin(remote(qkv_twin.at[0], qkv_twin.at[1], qz_send.at[0], qz_recv.at[0], tensor=at.twin))
+
+    remote(bf_out, bf_in, n_send.at[1], n_recv.at[1], tensor=at.mate).wait_recv()
+    for s in range(2):
+        block_out[s] += bf_in[s * 128 : (s + 1) * 128, :].astype(F32)
+
+    for slot in range(2):
+        line_wait(slot)
+
+    @pl.when(at.mid == 1)
+    def _():
+        line_wait(2)
+
+    for s in range(2):
+        for half in range(2):
+            rows = slice(half * 64, half * 64 + 64)
+            near = gna[t, rows, :].astype(F32) + rzn[0, rows, :].astype(F32)
+            third = rzn[2, rows, :].astype(F32)
+            far = rzn[1, rows, :].astype(F32) + jnp.where(at.mid == 1, third, jnp.zeros_like(third))
+            grad_out = jnp.where(h == s, near, far)
+            grad_rows, scaled = norm_back(hidden[s, rows, :], grad_out, gain_a)
+            grad_input[s, rows, :] += grad_rows
+            late[0:1, :] += jnp.sum(grad_out * scaled, axis=0, keepdims=True)
+            late[1:2, :] += jnp.sum(grad_out, axis=0, keepdims=True)
+
+    late_line[c, t] = late[...]
+    peers = [(c, p) for p in others] + [(other, p) for p in others] + [(other, t)]
+    for k, (core, p) in enumerate(peers):
+        block = late_line.at[c, t]
+        begin(remote(block, block, ta_send.at[k], ta_recv.at[c, t], ctx=core, tensor=p))
+    block = qkv_twin.at[1]
+    remote(block, block, qz_send.at[0], qz_recv.at[0], tensor=t).wait_recv()
+    res_qkv[c] = qkv_sum[0] + qkv_twin[1].astype(F32)
+    begin(result_copy(0, res_qkv))
+    for k, (core, p) in enumerate(peers):
+        block = late_line.at[core, p]
+        remote(block, block, ta_send.at[k], ta_recv.at[core, p], ctx=core, tensor=p).wait_recv()
+    total = late_line[0, 0]
+    for k in range(1, 8):
+        total = total + late_line[k // 4, k % 4]
+    late_plane[d] = total
+    for k in range(3):
+        block = late_plane.at[d]
+        begin(remote(block, block, tb_send.at[k], tb_recv.at[d], dp=planes[k]))
+
+    for i, ref in enumerate((res_qkv, res_ff, res_wo)):
+        block = ref.at[other]
+        remote(block, block, f_send.at[i], f_recv.at[i], ctx=other).wait_recv()
+    for which in range(2):
+        rows = slice(which * 96, (which + 1) * 96)
+        for ref, start in ((g_wq, 0), (g_wk, LANES), (g_wv, 2 * LANES)):
+            ref[rows, :] = res_qkv[which, :, start : start + 192]
+    g_win[...] = res_ff[0]
+    g_wout[...] = res_ff[1]
+    g_wo[...] = res_wo[...].reshape(192, LANES).T[:192, :]
+
+    for k in range(3):
+        line_sum(k, others[k]).wait_recv()
+    total = (sums_line[0] + sums_line[1]) + (sums_line[2] + sums_line[3])
+    for i, ref in enumerate((g_gain_f, g_shift_f, g_bias_o, g_bias_out)):
+        ref[...] = total[2 + i]
+    g_bias_in[...] = jnp.concatenate([total[6 + i : 7 + i, :] for i in range(4)], axis=1).reshape(3072)
+    for ref, start in ((g_bias_q, 0), (g_bias_v, 384)):
+        pieces = []
+        for p in range(4):
+            first_lane = start + (p // 2) * 192
+            pieces.append(total[10 + p % 2 : 11 + p % 2, first_lane : first_lane + 192])
+        ref[...] = jnp.concatenate(pieces, axis=1).reshape(768)
+    for k in range(3):
+        block = late_plane.at[planes[k]]
+        remote(block, block, tb_send.at[k], tb_recv.at[planes[k]], dp=d).wait_recv()
+    total = (late_plane[0] + late_plane[1]) + (late_plane[2] + late_plane[3])
+    g_gain_a[...] = total[0]
+    g_shift_a[...] = total[1]
+
+    for copy in waits:
+        copy.wait_send()
+    for p in range(4):
+        kvf_copy(p).wait_send()
+    for u in range(3):
+        kv_copy(u).wait_send()
+    for a in range(2):
+        first(a, 0).wait_send()
+        first(a, 1).wait_send()
+        second(a).wait_send()
+        for r in range(2):
+            right_copy(a, r).wait_send()
+
+    @pl.when(at.mid == 1)
+    def _():
+        pass_end.wait_send()
+        pass_mid.wait_send()
+        on_sum.wait_send()
+
+    @pl.when(at.mid == 0)
+    def _():
+        far_sum.wait_send()
+
+
+def deliver_kernel(*refs):
+    sems = refs[-1]
+    count = (len(refs) - 1) // 2
+    copies = [pltpu.make_async_copy(refs[i], refs[count + i], sems.at[i]) for i in range(count)]
+    for copy in copies:
+        copy.start()
+    for copy in copies:
+        copy.wait()
+
+
+VM = pl.BlockSpec(memory_space=pltpu.VMEM)
+ANY = pl.BlockSpec(memory_space=pl.ANY)
+
+
+def body(*operands):
+    struct = jax.ShapeDtypeStruct
+    dma = pltpu.SemaphoreType.DMA
+    vm = pltpu.VMEM
+    operands = operands[:16] + (operands[16].T, operands[17])
+    hidden, cotangent, _, gain, _, wq, wk, wv, bq, bv, wo, bo, gf, sf, win, bin_, wout, bout = operands
+    results = (hidden, hidden, gain, gain, wq, wk, wv, bq, bv, wo, bo, gf, sf, win, bin_, wout, bout)
+    shapes = tuple(struct(r.shape, F32) for r in results)
+    made = pl.pallas_call(
+        layer_kernel,
+        out_shape=shapes,
+        in_specs=[VM] * len(operands),
+        out_specs=(VM,) * len(results),
+        scratch_shapes=[
+            vm((4, 128, 768), BF),
+            vm((128, 768), BF),
+            vm((768, 512), BF),
+            vm((3, 512, 128), BF),
+            vm((6, 2, 4, 128, 128), BF),
+            vm((2, 2, 128, 384), BF),
+            vm((2, 2, 128, 384), BF),
+            vm((2, 4, 192, 768), BF),
+            vm((768, 1152), BF),
+            vm((4, 768, LANES), BF),
+            vm((2, 768, 384), BF),
+            vm((2, 2, 768, 768), BF),
+            vm((384, 1024), BF),
+            vm((384, 256), F32),
+            vm((4, 128, 384), BF),
+            vm((4, 128, 384), BF),
+            vm((1024, 128), F32),
+            vm((2, 2, 256, 768), BF),
+            vm((2, 256, 768), BF),
+            vm((4, 768, 256), BF),
+            vm((2, 2, 2, 256, 768), BF),
+            vm((2, 2, 256, 768), BF),
+            vm((256, 768), BF),
+            vm((256, 768), BF),
+            vm((256, 768), BF),
+            vm((256, 768), BF),
+            vm((2, 256, 768), BF),
+            vm((2, 768, 256), BF),
+            vm((4, 768, LANES), BF),
+            vm((4, 4, 96, LANES), BF),
+            vm((4, 96, LANES), BF),
+            vm((4, 96, LANES), BF),
+            vm((2, 2, 192, 768), BF),
+            vm((2, 192, 768), BF),
+            vm((192, 768), BF),
+            vm((6, 1024, 128), F32),
+            vm((3, 512, 256), BF),
+            vm((3, 512, 256), BF),
+            vm((512, 1152), BF),
+            vm((4, 128, 768), BF),
+            vm((4, 128, 768), BF),
+            vm((4, 96, 1152), F32),
+            vm((2, 4, 96, 1152), BF),
+            vm((2, 4, 96, 1152), BF),
+            vm((1, 96, 768), F32),
+            vm((2, 96, 768), BF),
+            vm((16, 768), F32),
+            vm((16, 768), F32),
+            vm((4, 16, 768), F32),
+            vm((4, 16, 768), F32),
+            vm((2, 768), F32),
+            vm((2, 4, 2, 768), F32),
+            vm((4, 2, 768), F32),
+            vm((2, 192, 768), F32),
+            vm((2, 96, LANES), F32),
+            vm((2, 96, 768), F32),
+            vm((1, 1152), F32),
+            vm((4, 1, 768), F32),
+            dma((1,)), dma((2, 3)), dma((2, 4)), dma((2, 4)), dma((2, 4)),
+            dma((4,)), dma((4,)), dma((4,)), dma((4,)), dma((3,)), dma((4,)),
+            dma((2,)), dma((3, 2, 2)), dma((2, 4, 2)), dma((2, 4, 2)), dma((2, 4, 2)),
+            dma((3,)), dma((4,)), dma((3,)), dma((4,)), dma((4,)), dma((4,)),
+            dma((2,)), dma((2,)), dma((1,)), dma((1,)), dma((2, 2)), dma((2, 2)),
+            dma((2,)), dma((2,)), dma((1,)), dma((1,)), dma((1,)), dma((1,)),
+            dma((3,)), dma((4,)),
+            dma((2, 2)), dma((2, 2)), dma((2,)), dma((2,)), dma((1,)), dma((1,)),
+            dma((3,)), dma((4,)), dma((3,)), dma((4,)),
+            dma((3,)), dma((3,)), dma((3,)), dma((4,)),
+            dma((1,)), dma((1,)), dma((3,)), dma((4,)), dma((1,)), dma((1,)),
+            dma((3,)), dma((3,)), dma((7,)), dma((9,)),
+            dma((7,)), dma((2, 4)), dma((3,)), dma((4,)),
+        ],
+        compiler_params=pltpu.CompilerParams(
+            collective_id=1, has_side_effects=True, vmem_limit_bytes=63 << 20
+        ),
+        name="layer",
+    )(*operands)
+    made = pl.pallas_call(
+        deliver_kernel,
+        out_shape=shapes,
+        in_specs=[VM] * len(shapes),
+        out_specs=(ANY,) * len(shapes),
+        scratch_shapes=[dma((len(shapes),))],
+        name="deliver",
+    )(*made)
+    return tuple(made[:15]) + (made[15].T, made[16])
 
 
 root_half = 0.7071067811865476
 inv_root_two_pi = 0.3989422804014327
 
 
-def smooth_gate(values):
+def general_gate(values):
     return values * (0.5 * (1.0 + lax.erf(values * root_half)))
 
 
-def smooth_slope(values):
+def general_slope(values):
     normal_cdf = 0.5 * (1.0 + lax.erf(values * root_half))
     normal_pdf = jnp.exp(-0.5 * values * values) * inv_root_two_pi
     return normal_cdf + values * normal_pdf
 
 
-def norm_forward(rows, gain, shift):
+def general_norm(rows, gain, shift):
     centred = rows - jnp.mean(rows, axis=-1, keepdims=True)
     inverse = lax.rsqrt(jnp.mean(centred * centred, axis=-1, keepdims=True) + 1e-05)
     scaled = centred * inverse
     return (scaled * gain + shift, scaled, inverse)
 
 
-def norm_backward(grad_out, scaled, inverse, gain):
+def general_norm_backward(grad_out, scaled, inverse, gain):
     grad_scaled = grad_out * gain
     plain_mean = jnp.mean(grad_scaled, axis=-1, keepdims=True)
     cross_mean = jnp.mean(grad_scaled * scaled, axis=-1, keepdims=True)
@@ -54,11 +1066,11 @@
     )
 
 
-def place_piece(piece, total, start):
+def general_piece(piece, total, start):
     return lax.dynamic_update_slice(jnp.zeros((total,), jnp.float32), piece, (start,))
 
 
-def body(
+def general_body(
     hidden_in,
     cotangent,
     segment_ids,
@@ -116,7 +1128,7 @@
         allowed = (query_seg[:, None] == segment_row[None, :]) & (
             (segment_row[None, :] >= 0) | (query_index[:, None] == key_index[None, :])
         )
-        normed, scaled_a, inverse_a = norm_forward(rows, attn_gain, attn_shift)
+        normed, scaled_a, inverse_a = general_norm(rows, attn_gain, attn_shift)
         normed_all = tensor_rows(normed.astype(jnp.bfloat16))
         queries = (
             jnp.dot(normed_all, w_query, preferred_element_type=jnp.float32) + query_piece
@@ -144,16 +1156,16 @@
         mixed = mixed.reshape(half_rows, part_width).astype(jnp.bfloat16)
         branch_a = tensor_sums(jnp.dot(mixed, w_output, preferred_element_type=jnp.float32))
         middle = rows + branch_a + output_bias
-        normed_f, scaled_f, inverse_f = norm_forward(middle, ffn_gain, ffn_shift)
+        normed_f, scaled_f, inverse_f = general_norm(middle, ffn_gain, ffn_shift)
         normed_f_all = tensor_rows(normed_f.astype(jnp.bfloat16))
         inner = jnp.dot(normed_f_all, w_inner, preferred_element_type=jnp.float32) + inner_piece
-        active = smooth_gate(inner).astype(jnp.bfloat16)
+        active = general_gate(inner).astype(jnp.bfloat16)
         branch_f = tensor_sums(jnp.dot(active, w_outer, preferred_element_type=jnp.float32))
         result_rows = middle + branch_f + outer_bias
         grad_up = tensor_rows(cot_rows.astype(jnp.bfloat16))
         grad_outer_w = jnp.einsum("tf,td->fd", active, grad_up, preferred_element_type=jnp.float32)
         grad_active = jnp.einsum("td,fd->tf", grad_up, w_outer, preferred_element_type=jnp.float32)
-        grad_inner = (grad_active * smooth_slope(inner)).astype(jnp.bfloat16)
+        grad_inner = (grad_active * general_slope(inner)).astype(jnp.bfloat16)
         grad_inner_w = jnp.einsum(
             "td,tf->df", normed_f_all, grad_inner, preferred_element_type=jnp.float32
         )
@@ -161,7 +1173,7 @@
         grad_normed_f = tensor_sums(
             jnp.einsum("tf,df->td", grad_inner, w_inner, preferred_element_type=jnp.float32)
         )
-        grad_rows_f, grad_ffn_g, grad_ffn_s = norm_backward(
+        grad_rows_f, grad_ffn_g, grad_ffn_s = general_norm_backward(
             grad_normed_f, scaled_f, inverse_f, ffn_gain
         )
         grad_middle = cot_rows + grad_rows_f
@@ -228,7 +1240,7 @@
             "tc,dc->td", grad_values, w_value, preferred_element_type=jnp.float32
         )
         grad_normed = tensor_sums(grad_normed_part)
-        grad_rows_a, grad_attn_g, grad_attn_s = norm_backward(
+        grad_rows_a, grad_attn_g, grad_attn_s = general_norm_backward(
             grad_normed, scaled_a, inverse_a, attn_gain
         )
         grad_rows = grad_middle + grad_rows_a
@@ -244,12 +1256,12 @@
         small_terms = (
             grad_attn_g,
             grad_attn_s,
-            place_piece(grad_query_b, width, tensor_at * part_width),
-            place_piece(grad_value_b, width, tensor_at * part_width),
+            general_piece(grad_query_b, width, tensor_at * part_width),
+            general_piece(grad_value_b, width, tensor_at * part_width),
             jnp.sum(grad_middle, axis=0),
             grad_ffn_g,
             grad_ffn_s,
-            place_piece(grad_inner_b, unit_total, tensor_at * unit_width),
+            general_piece(grad_inner_b, unit_total, tensor_at * unit_width),
             jnp.sum(cot_rows, axis=0),
         )
         small_sums = tuple((old + new for old, new in zip(small_sums, small_terms)))
@@ -349,48 +1361,20 @@
     )
 
 
+SPECS = (
+    P("dp", ("ctx", "tensor"), None), P("dp", ("ctx", "tensor"), None), P("dp", None), P(), P(),
+    P("dp", "tensor"), P("dp", "tensor"), P("dp", "tensor"), P(), P(), P("tensor", "dp"), P(), P(),
+    P(), P("dp", "tensor"), P(), P("tensor", "dp"), P(),
+)
+OUT_SPECS = (
+    P("dp", ("ctx", "tensor"), None), P("dp", ("ctx", "tensor"), None), P(), P(),
+    P("dp", "tensor"), P("dp", "tensor"), P("dp", "tensor"), P(), P(), P("tensor", "dp"), P(), P(),
+    P(), P("dp", "tensor"), P(), P("tensor", "dp"), P(),
+)
+
+
 def solution(mesh):
+    lined_up = mesh.shape["dp"] == 4 and mesh.shape["tensor"] == 4 and mesh.shape["ctx"] == 2
     return jax.shard_map(
-        body,
-        mesh=mesh,
-        in_specs=(
-            P("dp", ("ctx", "tensor"), None),
-            P("dp", ("ctx", "tensor"), None),
-            P("dp", None),
-            P(),
-            P(),
-            P("dp", "tensor"),
-            P("dp", "tensor"),
-            P("dp", "tensor"),
-            P(),
-            P(),
-            P("tensor", "dp"),
-            P(),
-            P(),
-            P(),
-            P("dp", "tensor"),
-            P(),
-            P("tensor", "dp"),
-            P(),
-        ),
-        out_specs=(
-            P("dp", ("ctx", "tensor"), None),
-            P("dp", ("ctx", "tensor"), None),
-            P(),
-            P(),
-            P("dp", "tensor"),
-            P("dp", "tensor"),
-            P("dp", "tensor"),
-            P(),
-            P(),
-            P("tensor", "dp"),
-            P(),
-            P(),
-            P(),
-            P("dp", "tensor"),
-            P(),
-            P("tensor", "dp"),
-            P(),
-        ),
-        check_vma=False,
+        body if lined_up else general_body, mesh=mesh, in_specs=SPECS, out_specs=OUT_SPECS, check_vma=False
     )

time: 864 us -> 166 us (0.19)
  waiting for transfers between devices: 372 us -> 0 us
  blocking collectives: 263 us -> 0 us
  Pallas kernels: 0 us -> 165 us
  matrix products: 101 us -> 0 us
  other arithmetic: 62.3 us -> 0 us
  local copies, waits for them, and re-layouts: 46 us -> 0 us
  between operations: 14.6 us -> 0.83 us
    reduce_scatter x14 -> x0, waiting for transfers between devices: 268 us -> none  [the longest x8 207 us: tensor_sums(): return lax.psum_scatter(block, 'tensor', scatter_dimension=0, tiled=True)]
    all_gather x16 -> x0, blocking collectives: 222 us -> none  [the longest x8 168 us: tensor_rows(): return lax.all_gather(block, 'tensor', axis=0, tiled=True)]
    pallas_call x0 -> x2, Pallas kernels: none -> 165 us  [the longest x1 161 us: body(): pl.pallas_call(layer_kernel, out_shape=shapes, in_specs=[VM] * len(operan...]
    dot_general x48 -> x0, matrix products: 101 us -> none  [the longest x2 9.46 us: micro(): jnp.einsum('qhd,khd->hqk', grad_mixed, value_all, preferred_element_type=...]
    unnamed x13 -> x0, waiting for transfers between devices: 93.9 us -> none
    psum x1 -> x0, blocking collectives: 40.8 us -> none  [body(): lax.psum((small_sums[0], small_sums[1], small_sums[2], small_sums[3], sma...]
    convert_element_type x23 -> x0, other arithmetic: 22.6 us -> none  [the longest x3 5.21 us: body(): owned = (lax.psum_scatter(paired[0].astype(jnp.bfloat16), 'dp', scatter_d...]
    unnamed x48 -> x0, local copies, waits for them, and re-layouts: 18.7 us -> none
  transfers between devices with their start and end apart: 21 -> 0, of which waited for: 15 -> 0; matrix products, arithmetic and copies ran while one was open for 12% -> 0% of each run, Pallas kernels for 0% -> 0%
where the time goes in v4:
time: 166 us; the launch traced here: 165 us
  Pallas kernels  165 us (99%)
    pallas_call x1, Pallas kernels, body(): pl.pallas_call(layer_kernel, out_shape=shapes, in_specs=[VM] * len(operan...  161 us
    pallas_call x1, Pallas kernels, body(): pl.pallas_call(deliver_kernel, out_shape=shapes, in_specs=[VM] * len(shap...  3.98 us

profile of v4, /device:TPU:0, one launch (start us, length us, event | category | flops | bytes accessed | tf_op | source)
XLA Modules:
  0.0 165.4 jit_solution(1992666503039744403)
XLA Ops:
  0.7 160.6 %layer.1 = (f32[2,128,768]{2,1,0:T(8,128)}, f32[2,128,768]{2,1,0:T(8,128)}, f32[768]{0:T(1024)}, f32[768]{0:T(1024)}, f32[192,192]{1,0:T(8,128)}, /*index=5*/f32...) custom-call(f32[2,128,768]{2,1,0:T(8,128)} %hidden.1, ...), custom_call_target="tpu_custom_call" | custom-call | tf_op jit(solution)/shard_map/layer/pallas_call | solution.py:927
  161.3 4.0 %deliver.1 = (f32[2,128,768]{2,1,0:T(8,128)}, f32[2,128,768]{2,1,0:T(8,128)}, f32[768]{0:T(1024)}, f32[768]{0:T(1024)}, f32[192,192]{1,0:T(8,128)}, /*index=5*/f...) custom-call(f32[2,128,768]{2,1,0:T(8,128)} %get-tuple-element.51.ref, ...), custom_call_target="tpu_custom_call" | custom-call | tf_op jit(solution)/shard_map/deliver/pallas_call | solution.py:1010

commit v5 on v4

--- a/solution.py
+++ b/solution.py
@@ -145,9 +145,18 @@
     def q_half(a, owner, which):
         return q_land.at[a, owner, rows_at(which * 96, 96, 96)]
 
-    def q_plane(a, i, owner):
-        half = q_half(a, owner, c)
-        return remote(half, half, q_send.at[a, i], q_recv.at[a, owner], dp=planes[i])
+    def q_piece(a, owner, n):
+        if n is None:
+            return q_half(a, owner, c), 0
+        return q_land.at[a, owner, rows_at(c * 96 + n * 48, 48, 48)], n
+
+    def q_plane(a, i, owner, n=None):
+        block, n = q_piece(a, owner, n)
+        return remote(block, block, q_send.at[a, i, n], q_recv.at[a, owner, n], dp=planes[i])
+
+    def q_twin(n):
+        block, n = q_piece(h, d, n)
+        return remote(block, block, qt_send.at[n], q_recv.at[h, d, n], tensor=at.twin)
 
     def q_core(a, owner):
         half = q_half(a, owner, c)
@@ -157,11 +166,11 @@
         half = q_half(a, owner, other)
         remote(half, half, qc_send.at[a, owner], qc_recv.at[a, owner], ctx=other).wait_recv()
 
-    def q_wait(a, owner):
-        half = q_half(a, owner, c)
-        remote(half, half, qt_send.at[0], q_recv.at[a, owner], tensor=t).wait_recv()
-
-    begin(remote(q_half(h, d, c), q_half(h, d, c), qt_send.at[0], q_recv.at[h, d], tensor=at.twin))
+    def q_wait(a, owner, n=None):
+        block, n = q_piece(a, owner, n)
+        remote(block, block, qt_send.at[0], q_recv.at[a, owner, n], tensor=t).wait_recv()
+
+    begin(q_twin(0), q_twin(1))
     for i in range(3):
         begin(q_plane(h, i, d))
 
@@ -177,9 +186,6 @@
     def wo_line(k, owner):
         block = wo_land.at[owner, mine]
         return remote(block, block, wz_send.at[k], wz_recv.at[owner], tensor=others[k])
-
-    for k in range(3):
-        begin(wo_line(k, t))
 
     def normed_rows(s):
         scaled, _ = norm_parts(hidden[s])
@@ -286,9 +292,13 @@
     for i in range(3):
         q_wait(h, planes[i])
         begin(q_core(h, planes[i]))
-    q_wait(away, d)
-    for i in range(3):
-        begin(q_plane(away, i, d))
+    for k in range(3):
+        begin(wo_line(k, t))
+
+    for n in range(2):
+        q_wait(away, d, n)
+        for i in range(3):
+            begin(q_plane(away, i, d, n))
     begin(q_core(away, d))
 
     @pl.when(at.mid == 1)
@@ -299,7 +309,8 @@
         pass_mid.start()
 
     for i in range(3):
-        q_wait(away, planes[i])
+        q_wait(away, planes[i], 0)
+        q_wait(away, planes[i], 1)
         begin(q_core(away, planes[i]))
     for k in range(3):
         p = others[k]
@@ -347,6 +358,7 @@
 
     for n in range(2):
         ff_begin(ff_twin(n))
+    begin(remote(left.at[1, 0], left.at[1, 1], u_send.at[1], u_recv.at[1], tensor=at.mate))
     lax.fori_loop(0, 4, project, 0)
 
     lane_head = lax.broadcasted_iota(jnp.int32, (1, 128), 1) // HDIM
@@ -393,7 +405,6 @@
     attend(away)
     mf_copy(0, 2 * away).start()
     mf_copy(1, 2 * away + 1).start()
-    begin(remote(left.at[1, 0], left.at[1, 1], u_send.at[1], u_recv.at[1], tensor=at.mate))
     for n in range(2):
         diag(h, n)
     attend(h)
@@ -488,31 +499,17 @@
         for n in range(2):
             ff_core_wait(away, p, n)
 
-    def twin_slot(i, carry):
-        @pl.when(i == 1)
-        def _():
-            for q in range(4):
-                rows = slice(q * 64, (q + 1) * 64)
-                nf_out[rows, :] = wide_rows(768 + q * 64).astype(BF)
-            nf_copy.start()
-
-        units(away, 1 - i)
-        return carry
-
     nf_copy = remote(nf_out, nf_in, n_send.at[0], n_recv.at[0], tensor=at.mate)
     waits.append(nf_copy)
-    lax.fori_loop(0, 2, twin_slot, 0)
-    for q in range(4):
-        rows = slice(q * 64, (q + 1) * 64)
-        bf_out[rows, :] = wide_rows(512 + q * 64).astype(BF)
-
     for copy in ff_sends:
         copy.wait_send()
-    left_turn[0] = left[c, 0].T
-    left_turn[1] = left[c, 1].T
-    remote(left.at[c], left_in, l_send.at[0], l_recv.at[0], ctx=other).wait_recv()
-    left_turn[2] = left_in[0].T
-    left_turn[3] = left_in[1].T
+
+    def turn_left():
+        left_turn[0] = left[c, 0].T
+        left_turn[1] = left[c, 1].T
+        remote(left.at[c], left_in, l_send.at[0], l_recv.at[0], ctx=other).wait_recv()
+        left_turn[2] = left_in[0].T
+        left_turn[3] = left_in[1].T
 
     def first(a, j):
         near, _ = near_far(a)
@@ -522,6 +519,18 @@
     def second(a):
         _, far = near_far(a)
         return remote(ff_block(0, a, far), rx2.at[a], p2_send.at[a], p2_recv.at[a], dp=far)
+
+    def to_second(a):
+        _, far = near_far(a)
+        first(a, 1).wait_recv()
+        add_to(ff_block(0, a, far), rx1.at[a, 1])
+        second(a).start()
+        first(a, 0).start()
+
+    def plane_done(a):
+        first(a, 0).wait_recv()
+        second(a).wait_recv()
+        add_to(ff_block(0, a, d), rx1.at[a, 0], rx2.at[a])
 
     def weight_gradient(a):
         for r in range(2):
@@ -538,13 +547,25 @@
 
         lax.fori_loop(0, 4, rows_of, 0)
         first(a, 1).start()
-        first(a, 0).start()
-
-    def both_slots(a, carry):
-        weight_gradient(a)
+
+    def twin_slot(i, carry):
+        @pl.when(i == 1)
+        def _():
+            for q in range(4):
+                rows = slice(q * 64, (q + 1) * 64)
+                nf_out[rows, :] = wide_rows(768 + q * 64).astype(BF)
+            nf_copy.start()
+            turn_left()
+            weight_gradient(h)
+
+        units(away, 1 - i)
         return carry
 
-    lax.fori_loop(0, 2, both_slots, 0)
+    lax.fori_loop(0, 2, twin_slot, 0)
+    weight_gradient(away)
+    for q in range(4):
+        rows = slice(q * 64, (q + 1) * 64)
+        bf_out[rows, :] = wide_rows(512 + q * 64).astype(BF)
 
     def add_row(i, value):
         sums[i : i + 1, :] += jnp.sum(value, axis=0, keepdims=True)
@@ -556,7 +577,8 @@
         cross = jnp.mean(grad_scaled * scaled, axis=-1, keepdims=True)
         return inverse * (grad_scaled - plain - scaled * cross), scaled
 
-    remote(nf_out, nf_in, n_send.at[0], n_recv.at[0], tensor=at.mate).wait_recv()
+    nf_copy.wait_recv()
+    to_second(h)
     for s in range(2):
         for half in range(2):
             rows = slice(half * 64, half * 64 + 64)
@@ -607,20 +629,9 @@
     def wo_part(owner):
         return part_wo.at[:, rows_at(owner * 192 + c * 96, 96, 96)]
 
+    to_second(away)
     for i in range(3):
         begin(remote(wo_part(planes[i]), rxw.at[d], gp_send.at[i], gp_recv.at[d], dp=planes[i]))
-
-    def to_second(a):
-        _, far = near_far(a)
-        first(a, 1).wait_recv()
-        add_to(ff_block(0, a, far), rx1.at[a, 1])
-        second(a).start()
-        first(a, 0).wait_recv()
-        add_to(ff_block(0, a, d), rx1.at[a, 0])
-
-    def plane_done(a):
-        second(a).wait_recv()
-        add_to(ff_block(0, a, d), rx2.at[a])
 
     zz_copy = remote(ff_block(0, away, d), rz, zz_send.at[0], zz_recv.at[0], tensor=at.twin)
     waits.append(zz_copy)
@@ -638,6 +649,22 @@
 
     def kv_copy(u):
         return remote(kv_out.at[u], kv_in.at[u], kv_send.at[u], kv_recv.at[u], ctx=other)
+
+    gz_copies = [
+        remote(sumw.at[p], rzw.at[t], gz_send.at[k], gz_recv.at[t], tensor=p) for k, p in enumerate(others)
+    ]
+    waits.extend(gz_copies)
+
+    def wo_plane_done():
+        for i in range(3):
+            p = planes[i]
+            remote(wo_part(p), rxw.at[p], gp_send.at[i], gp_recv.at[p], dp=p).wait_recv()
+        total = part_wo[:, mine, :].astype(F32)
+        for i in range(3):
+            total = total + rxw[planes[i]].astype(F32)
+        sumw[...] = total.astype(BF)
+        for copy in gz_copies:
+            copy.start()
 
     def attend_back(b, last):
         block = rows_at(b * 256, 256, 256)
@@ -661,15 +688,19 @@
                 q_turn[rows, :] = jnp.dot(turn[rows, :], grad_scores, preferred_element_type=F32)
             if not last:
 
-                @pl.when(u > 0)
-                def _():
-                    to_second(u - 1)
-
-            if last:
                 @pl.when(u == 1)
                 def _():
                     plane_done(away)
                     zz_copy.start()
+
+            if last:
+                @pl.when(u == 0)
+                def _():
+                    plane_done(h)
+
+                @pl.when(u == 2)
+                def _():
+                    wo_plane_done()
 
                 kv_out[u, :, :128] = wide[u, theirs, :].astype(BF)
                 kv_out[u, :, 128:] = wide[3 + u, theirs, :].astype(BF)
@@ -686,13 +717,55 @@
     m_wait(at.far_end)
     attend_back(away, True)
 
-    for i in range(3):
-        p = planes[i]
-        remote(wo_part(p), rxw.at[p], gp_send.at[i], gp_recv.at[p], dp=p).wait_recv()
-    total = part_wo[:, mine, :].astype(F32)
-    for i in range(3):
-        total = total + rxw[planes[i]].astype(F32)
-    sumw[...] = total.astype(BF)
+    def part_cols(k):
+        return pl.ds(0, 384) if k == 0 else pl.ds(384, 768)
+
+    def sib_copy(k):
+        block, landing = qkv_sib.at[0, :, :, part_cols(k)], qkv_sib.at[1, :, :, part_cols(k)]
+        return remote(block, landing, qs_send.at[k], qs_recv.at[k], ctx=other)
+
+    def qkv_part(k):
+        def rows_of(i, carry):
+            rows = rows_at(i * 192, 192, 192)
+            out = jnp.dot(normed_turn[rows, :], dqkv[:, part_cols(k)], preferred_element_type=F32)
+            qkv_own[i, :, part_cols(k)] = jnp.where(c == 0, out[:96], out[96:])
+            qkv_sib[0, i, :, part_cols(k)] = jnp.where(c == 0, out[96:], out[:96]).astype(BF)
+            return carry
+
+        lax.fori_loop(0, 4, rows_of, 0)
+        begin(sib_copy(k))
+
+    def qkv_out(k):
+        sib_copy(k).wait_recv()
+        cols = part_cols(k)
+        for p in range(4):
+            qkv_in[0, p, :, cols] = (qkv_own[p, :, cols] + qkv_sib[1, p, :, cols].astype(F32)).astype(BF)
+        for i in range(3):
+            block, landing = qkv_in.at[0, planes[i], :, cols], qkv_in.at[1, d, :, cols]
+            begin(remote(block, landing, qp_send.at[k, i], qp_recv.at[k, d], dp=planes[i]))
+        qkv_in[1, d, :, cols] = qkv_in[0, d, :, cols]
+
+    def twin_copy(k):
+        cols = pl.ds(0, LANES) if k == 0 else pl.ds(LANES, 2 * LANES)
+        block, landing = qkv_twin.at[0, :, cols], qkv_twin.at[1, :, cols]
+        return remote(block, landing, qz_send.at[k], qz_recv.at[k], tensor=at.twin)
+
+    def qkv_to_twin(k):
+        for i in range(3):
+            block = qkv_in.at[1, planes[i], :, part_cols(k)]
+            remote(block, block, qp_send.at[k, i], qp_recv.at[k, planes[i]], dp=d).wait_recv()
+        for j in ((0,), (1, 2))[k]:
+            cols = slice(j * 384, (j + 1) * 384)
+            total = qkv_in[1, 0, :, cols].astype(F32)
+            for p in range(1, 4):
+                total = total + qkv_in[1, p, :, cols].astype(F32)
+            low, high = total[:, :192], total[:, 192:]
+            qkv_sum[0, :, j * LANES : j * LANES + 192] = jnp.where(h == 0, low, high)
+            qkv_twin[0, :, j * LANES : j * LANES + 192] = jnp.where(h == 0, high, low).astype(BF)
+        begin(twin_copy(k))
+
+    qkv_part(0)
+
 
     for u in range(3):
         kv_copy(u).wait_recv()
@@ -701,27 +774,28 @@
             theirs_here = kv_in[u, :, k * 128 : (k + 1) * 128].astype(F32)
             dqkv[:, cols] = (wide[3 * k + u, ours, :] + theirs_here).astype(BF)
 
+    qkv_out(0)
+
     def line_copy(owner, slot, k, dest):
         return remote(gna.at[owner], rzn.at[slot], rn_send.at[k], rn_recv.at[slot], tensor=dest)
 
     def line_wait(slot):
         line_copy(t, slot, 0, t).wait_recv()
 
-    far_sum = line_copy(at.far_end, 3, 2, at.mate)
-    on_sum = line_copy(at.far_end, 1, 2, at.far_end)
+    by_mate = [line_copy(at.far_end, 2, 1, at.mate), line_copy(at.far_mid, 3, 2, at.mate)]
+    on_sums = [line_copy(at.far_end, 1, 1, at.far_end), line_copy(at.far_mid, 1, 2, at.far_mid)]
 
     def rows_back(p):
         rows = dqkv[rows_at(p * 128, 128, 128), :]
         gna[p] = dims(rows, wqkv[...], 1, 1).astype(BF)
 
-    rows_back(at.far_end)
-
-    @pl.when(at.mid == 0)
-    def _():
-        far_sum.start()
-
-    rows_back(at.far_mid)
-    begin(line_copy(at.far_mid, 2 - at.mid, 1, at.far_mid))
+    for i, p in enumerate((at.far_end, at.far_mid)):
+        rows_back(p)
+
+        @pl.when(at.mid == 0)
+        def _(i=i):
+            by_mate[i].start()
+
     rows_back(at.mate)
     begin(line_copy(at.mate, 0, 0, at.mate))
     rows_back(t)
@@ -740,40 +814,24 @@
         block = sums_line.at[owner]
         return remote(block, block, t_send.at[4 + k], t_recv.at[5 + owner], tensor=others[k])
 
-    def qkv_rows(i, carry):
-        rows = rows_at(i * 192, 192, 192)
-        out = jnp.dot(normed_turn[rows, :], dqkv[...], preferred_element_type=F32)
-        qkv_own[i] = jnp.where(c == 0, out[:96], out[96:])
-        qkv_sib[0, i] = jnp.where(c == 0, out[96:], out[:96]).astype(BF)
-        return carry
-
-    lax.fori_loop(0, 4, qkv_rows, 0)
-    sib_copy = remote(qkv_sib.at[0], qkv_sib.at[1], qs_send.at[0], qs_recv.at[0], ctx=other)
-    begin(sib_copy)
-    for k in range(3):
-        begin(remote(sumw.at[others[k]], rzw.at[t], gz_send.at[k], gz_recv.at[t], tensor=others[k]))
-
+    qkv_part(1)
     @pl.when(at.mid == 1)
     def _():
-        line_wait(3)
-        add_to(gna.at[at.far_end], rzn.at[3])
-        on_sum.start()
+        for i, p in enumerate((at.far_end, at.far_mid)):
+            line_wait(2 + i)
+            add_to(gna.at[p], rzn.at[2 + i])
+            on_sums[i].start()
 
     core_sum.wait_recv()
     sums_plane[d] = sums[...] + sums_core[...]
     for k in range(3):
         begin(plane_sum(k, d))
-    sib_copy.wait_recv()
-    for p in range(4):
-        qkv_in[0, p] = (qkv_own[p] + qkv_sib[1, p].astype(F32)).astype(BF)
-    for k in range(3):
-        begin(remote(qkv_in.at[0, planes[k]], qkv_in.at[1, d], qp_send.at[k], qp_recv.at[d], dp=planes[k]))
-    qkv_in[1, d] = qkv_in[0, d]
+    qkv_out(1)
+    qkv_to_twin(0)
 
     def result_copy(i, ref):
         return remote(ref.at[c], ref.at[c], f_send.at[i], f_recv.at[i], ctx=other)
 
-    plane_done(h)
     remote(rz, rz, zz_send.at[0], zz_recv.at[0], tensor=t).wait_recv()
     res_ff[c] = ffw[0, h, here, :].astype(F32) + rz[...].astype(F32)
     begin(result_copy(1, res_ff))
@@ -793,17 +851,7 @@
     for k in range(3):
         begin(line_sum(k, t))
 
-    for k in range(3):
-        block = qkv_in.at[1, planes[k]]
-        remote(block, block, qp_send.at[k], qp_recv.at[planes[k]], dp=d).wait_recv()
-    total = qkv_in[1, 0].astype(F32)
-    for p in range(1, 4):
-        total = total + qkv_in[1, p].astype(F32)
-    for k in range(3):
-        low, high = total[:, k * 384 : k * 384 + 192], total[:, k * 384 + 192 : (k + 1) * 384]
-        qkv_sum[0, :, k * LANES : k * LANES + 192] = jnp.where(h == 0, low, high)
-        qkv_twin[0, :, k * LANES : k * LANES + 192] = jnp.where(h == 0, high, low).astype(BF)
-    begin(remote(qkv_twin.at[0], qkv_twin.at[1], qz_send.at[0], qz_recv.at[0], tensor=at.twin))
+    qkv_to_twin(1)
 
     remote(bf_out, bf_in, n_send.at[1], n_recv.at[1], tensor=at.mate).wait_recv()
     for s in range(2):
@@ -811,18 +859,12 @@
 
     for slot in range(2):
         line_wait(slot)
-
-    @pl.when(at.mid == 1)
-    def _():
-        line_wait(2)
 
     for s in range(2):
         for half in range(2):
             rows = slice(half * 64, half * 64 + 64)
             near = gna[t, rows, :].astype(F32) + rzn[0, rows, :].astype(F32)
-            third = rzn[2, rows, :].astype(F32)
-            far = rzn[1, rows, :].astype(F32) + jnp.where(at.mid == 1, third, jnp.zeros_like(third))
-            grad_out = jnp.where(h == s, near, far)
+            grad_out = jnp.where(h == s, near, rzn[1, rows, :].astype(F32))
             grad_rows, scaled = norm_back(hidden[s, rows, :], grad_out, gain_a)
             grad_input[s, rows, :] += grad_rows
             late[0:1, :] += jnp.sum(grad_out * scaled, axis=0, keepdims=True)
@@ -833,8 +875,8 @@
     for k, (core, p) in enumerate(peers):
         block = late_line.at[c, t]
         begin(remote(block, block, ta_send.at[k], ta_recv.at[c, t], ctx=core, tensor=p))
-    block = qkv_twin.at[1]
-    remote(block, block, qz_send.at[0], qz_recv.at[0], tensor=t).wait_recv()
+    for k in range(2):
+        twin_copy(k).wait_recv()
     res_qkv[c] = qkv_sum[0] + qkv_twin[1].astype(F32)
     begin(result_copy(0, res_qkv))
     for k, (core, p) in enumerate(peers):
@@ -895,21 +937,27 @@
     def _():
         pass_end.wait_send()
         pass_mid.wait_send()
-        on_sum.wait_send()
+        for copy in on_sums:
+            copy.wait_send()
 
     @pl.when(at.mid == 0)
     def _():
-        far_sum.wait_send()
+        for copy in by_mate:
+            copy.wait_send()
 
 
 def deliver_kernel(*refs):
-    sems = refs[-1]
-    count = (len(refs) - 1) // 2
-    copies = [pltpu.make_async_copy(refs[i], refs[count + i], sems.at[i]) for i in range(count)]
-    for copy in copies:
-        copy.start()
-    for copy in copies:
-        copy.wait()
+    count = (len(refs) - 2) // 3
+    made, outs, held = refs[:count], refs[count : 2 * count], refs[2 * count : 3 * count]
+    fetches = [pltpu.make_async_copy(made[i], held[i], refs[-2].at[i]) for i in range(count)]
+    puts = [pltpu.make_async_copy(held[i], outs[i], refs[-1].at[i]) for i in range(count)]
+    for fetch in fetches:
+        fetch.start()
+    for fetch, put in zip(fetches, puts):
+        fetch.wait()
+        put.start()
+    for put in puts:
+        put.wait()
 
 
 VM = pl.BlockSpec(memory_space=pltpu.VMEM)
@@ -988,7 +1036,7 @@
             vm((2, 96, 768), F32),
             vm((1, 1152), F32),
             vm((4, 1, 768), F32),
-            dma((1,)), dma((2, 3)), dma((2, 4)), dma((2, 4)), dma((2, 4)),
+            dma((2,)), dma((2, 3, 2)), dma((2, 4, 2)), dma((2, 4)), dma((2, 4)),
             dma((4,)), dma((4,)), dma((4,)), dma((4,)), dma((3,)), dma((4,)),
             dma((2,)), dma((3, 2, 2)), dma((2, 4, 2)), dma((2, 4, 2)), dma((2, 4, 2)),
             dma((3,)), dma((4,)), dma((3,)), dma((4,)), dma((4,)), dma((4,)),
@@ -998,7 +1046,7 @@
             dma((2, 2)), dma((2, 2)), dma((2,)), dma((2,)), dma((1,)), dma((1,)),
             dma((3,)), dma((4,)), dma((3,)), dma((4,)),
             dma((3,)), dma((3,)), dma((3,)), dma((4,)),
-            dma((1,)), dma((1,)), dma((3,)), dma((4,)), dma((1,)), dma((1,)),
+            dma((2,)), dma((2,)), dma((2, 3)), dma((2, 4)), dma((2,)), dma((2,)),
             dma((3,)), dma((3,)), dma((7,)), dma((9,)),
             dma((7,)), dma((2, 4)), dma((3,)), dma((4,)),
         ],
@@ -1010,9 +1058,9 @@
     made = pl.pallas_call(
         deliver_kernel,
         out_shape=shapes,
-        in_specs=[VM] * len(shapes),
+        in_specs=[ANY] * len(shapes),
         out_specs=(ANY,) * len(shapes),
-        scratch_shapes=[dma((len(shapes),))],
+        scratch_shapes=[vm(r.shape, F32) for r in shapes] + [dma((len(shapes),))] * 2,
         name="deliver",
     )(*made)
     return tuple(made[:15]) + (made[15].T, made[16])

time: 166 us -> 155 us (0.934)
  Pallas kernels: 165 us -> 154 us
    pallas_call x1, Pallas kernels: 161 us -> 151 us  [body(): pl.pallas_call(layer_kernel, out_shape=shapes, in_specs=[VM] * len(operan...]
where the time goes in v5:
time: 155 us
  Pallas kernels  154 us (99%)
    pallas_call x1, Pallas kernels, body(): pl.pallas_call(layer_kernel, out_shape=shapes, in_specs=[VM] * len(operan...  151 us
    pallas_call x1, Pallas kernels, body(): pl.pallas_call(deliver_kernel, out_shape=shapes, in_specs=[ANY] * len(sha...  3.28 us

profile of v5, /device:TPU:0, one launch (start us, length us, event | category | flops | bytes accessed | tf_op | source)
XLA Modules:
  0.0 154.8 jit_solution(16832938275520488061)
XLA Ops:
  0.7 150.7 %layer.1 = (f32[2,128,768]{2,1,0:T(8,128)}, f32[2,128,768]{2,1,0:T(8,128)}, f32[768]{0:T(1024)}, f32[768]{0:T(1024)}, f32[192,192]{1,0:T(8,128)}, /*index=5*/f32...) custom-call(f32[2,128,768]{2,1,0:T(8,128)} %hidden.1, ...), custom_call_target="tpu_custom_call" | custom-call | tf_op jit(solution)/shard_map/layer/pallas_call | solution.py:975
  151.4 3.3 %deliver.1 = (f32[2,128,768]{2,1,0:T(8,128)}, f32[2,128,768]{2,1,0:T(8,128)}, f32[768]{0:T(1024)}, f32[768]{0:T(1024)}, f32[192,192]{1,0:T(8,128)}, /*index=5*/f...) custom-call(f32[2,128,768]{2,1,0:T(8,128)} %get-tuple-element.51.ref, ...), custom_call_target="tpu_custom_call" | custom-call | tf_op jit(solution)/shard_map/deliver/pallas_call | solution.py:1058

commit v6 on v5

--- a/solution.py
+++ b/solution.py
@@ -218,6 +218,8 @@
         return ffw.at[which, a, rows_at(owner * 192, 192, 192)]
 
     def ff_half(which, a, owner, n):
+        if n is None:
+            return ff_block(which, a, owner)
         return ffw.at[which, a, rows_at(owner * 192 + n * 96, 96, 96)]
 
     def ff_twin(n):
@@ -226,19 +228,19 @@
 
     def ff_plane(axis, a, owner, n, dest):
         block = ff_half(c, a, owner, n)
-        return remote(block, block, cp_send.at[axis, a, n], c_recv.at[a, owner, n], dp=dest)
+        return remote(block, block, cp_send.at[axis, a, n or 0], c_recv.at[a, owner, n or 0], dp=dest)
 
     def ff_core(a, owner, n):
         block = ff_half(c, a, owner, n)
-        return remote(block, block, cc_send.at[a, owner, n], s_recv.at[a, owner, n], ctx=other)
+        return remote(block, block, cc_send.at[a, owner, n or 0], s_recv.at[a, owner, n or 0], ctx=other)
 
     def ff_wait(a, owner, n):
         block = ff_half(c, a, owner, n)
-        remote(block, block, ct_send.at[n], c_recv.at[a, owner, n], dp=d).wait_recv()
+        remote(block, block, ct_send.at[n or 0], c_recv.at[a, owner, n or 0], dp=d).wait_recv()
 
     def ff_core_wait(a, owner, n):
         block = ff_half(other, a, owner, n)
-        remote(block, block, cc_send.at[a, owner, n], s_recv.at[a, owner, n], ctx=other).wait_recv()
+        remote(block, block, cc_send.at[a, owner, n or 0], s_recv.at[a, owner, n or 0], ctx=other).wait_recv()
 
     ff_sends = []
 
@@ -319,8 +321,7 @@
     for i in range(3):
         begin(remote(wo_rows(d, c), wo_rows(d, c), wp_send.at[i], wp_recv.at[d], dp=planes[i]))
     begin(remote(wo_rows(d, c), wo_rows(d, c), wc_send.at[d], wc_recv.at[d], ctx=other))
-    for n in range(2):
-        spread(h, n)
+    spread(h, None)
     for i in range(3):
         q_core_wait(h, planes[i])
         q_core_wait(away, planes[i])
@@ -356,10 +357,10 @@
         kvf_copy(p).start()
         return carry
 
-    for n in range(2):
-        ff_begin(ff_twin(n))
+    ff_begin(ff_twin(0))
     begin(remote(left.at[1, 0], left.at[1, 1], u_send.at[1], u_recv.at[1], tensor=at.mate))
     lax.fori_loop(0, 4, project, 0)
+    ff_begin(ff_twin(1))
 
     lane_head = lax.broadcasted_iota(jnp.int32, (1, 128), 1) // HDIM
 
@@ -405,15 +406,13 @@
     attend(away)
     mf_copy(0, 2 * away).start()
     mf_copy(1, 2 * away + 1).start()
-    for n in range(2):
-        diag(h, n)
+    diag(h, None)
     attend(h)
     mf_copy(2, at.mate).start()
     mixed_in[g, h] = mixed[t]
     ff_wait(away, d, 0)
     spread(away, 0)
-    for n in range(2):
-        last(h, n)
+    last(h, None)
     for i in range(3):
         p = planes[i]
         remote(wo_rows(p, c), wo_rows(p, c), wp_send.at[i], wp_recv.at[p], dp=p).wait_recv()
@@ -448,8 +447,7 @@
 
     diag(away, 1)
     for p in range(4):
-        for n in range(2):
-            ff_core_wait(h, p, n)
+        ff_core_wait(h, p, None)
 
     def right_copy(a, r):
         return remote(
@@ -853,10 +851,6 @@
 
     qkv_to_twin(1)
 
-    remote(bf_out, bf_in, n_send.at[1], n_recv.at[1], tensor=at.mate).wait_recv()
-    for s in range(2):
-        block_out[s] += bf_in[s * 128 : (s + 1) * 128, :].astype(F32)
-
     for slot in range(2):
         line_wait(slot)
 
@@ -875,6 +869,10 @@
     for k, (core, p) in enumerate(peers):
         block = late_line.at[c, t]
         begin(remote(block, block, ta_send.at[k], ta_recv.at[c, t], ctx=core, tensor=p))
+    remote(bf_out, bf_in, n_send.at[1], n_recv.at[1], tensor=at.mate).wait_recv()
+    for s in range(2):
+        block_out[s] += bf_in[s * 128 : (s + 1) * 128, :].astype(F32)
+
     for k in range(2):
         twin_copy(k).wait_recv()
     res_qkv[c] = qkv_sum[0] + qkv_twin[1].astype(F32)

time: 155 us -> 155 us (level)
  no operation moved by 1% of the time
where the time goes in v6:
time: 155 us
  Pallas kernels  154 us (99%)
    pallas_call x1, Pallas kernels, body(): pl.pallas_call(layer_kernel, out_shape=shapes, in_specs=[VM] * len(operan...  151 us
    pallas_call x1, Pallas kernels, body(): pl.pallas_call(deliver_kernel, out_shape=shapes, in_specs=[ANY] * len(sha...  3.28 us

profile of v6, /device:TPU:0, one launch (start us, length us, event | category | flops | bytes accessed | tf_op | source)
XLA Modules:
  0.0 154.7 jit_solution(4481210531632827722)
XLA Ops:
  0.7 150.6 %layer.1 = (f32[2,128,768]{2,1,0:T(8,128)}, f32[2,128,768]{2,1,0:T(8,128)}, f32[768]{0:T(1024)}, f32[768]{0:T(1024)}, f32[192,192]{1,0:T(8,128)}, /*index=5*/f32...) custom-call(f32[2,128,768]{2,1,0:T(8,128)} %hidden.1, ...), custom_call_target="tpu_custom_call" | custom-call | tf_op jit(solution)/shard_map/layer/pallas_call | solution.py:973
  151.2 3.3 %deliver.1 = (f32[2,128,768]{2,1,0:T(8,128)}, f32[2,128,768]{2,1,0:T(8,128)}, f32[768]{0:T(1024)}, f32[768]{0:T(1024)}, f32[192,192]{1,0:T(8,128)}, /*index=5*/f...) custom-call(f32[2,128,768]{2,1,0:T(8,128)} %get-tuple-element.51.ref, ...), custom_call_target="tpu_custom_call" | custom-call | tf_op jit(solution)/shard_map/deliver/pallas_call | solution.py:1056
